TPU v7x, 32 devices: a whole 2x2x4 slice. The times are simulated.
32 devices in a mesh: slab: 8 (over z, y), patch: 4 (over x, core).
Axes of the slice: x: 2, y: 2, z: 4, core: 2. Of those that a mesh axis runs over, the one named last changes fastest.
Arguments:
- fields: float32 [6, 64, 8192], P(None, None, ('slab', 'patch')), may hold values from -6 to 6
- pole_state: float32 [12, 2, 16, 512], P(None, None, None, ('slab', 'patch')), may hold values from -3 to 3
- pole_decay: float32 [32, 12], P(('slab', 'patch')), may hold values from 0.1 to 0.95
- pole_gain: float32 [32, 12], P(('slab', 'patch')), may hold values from 0.05 to 0.5
- surface_resistance: float32 [32], P(('slab', 'patch')), may hold values from 0.3 to 3
- face_owner: int32 [512, 1], P(('slab', 'patch')), may hold values from 0 to 3; in each aligned block of 16 rows (0 to 15, 16 to 31, ...) at most 8 rows name the same one
Outputs:
- advanced_fields: float32 [6, 64, 8192], P(None, None, ('slab', 'patch'))
- advanced_states: float32 [12, 2, 16, 512], P(None, None, None, ('slab', 'patch'))
Inputs may be any that keep to these rules, and one draw needn't show every extreme that they name: `face_owner`: each impedance face names the owner of its patch among the 4 devices of its patch group. Among the 16 faces of one device at most 8 name the same owner, and in every draw some device has exactly 8 faces with one owner.
All inputs are finite; a program needn't handle non-finite values.
Results may differ from a plain program's by a relative error of at most 0.0003.
Values sent between devices are 32-bit elements; how exact they have to be, the bound alone decides.
No kernel may reach another device: no remote copies, remote signals or barrier semaphores. Data moves between devices by JAX's collectives and lax.ppermute only.
A program may use at most 64 MiB of HBM per device.

v0:
```python
import math

import jax
import jax.numpy as jnp
import numpy as np
from jax import lax
from jax.sharding import PartitionSpec as P

EX = 16
EY = 16


courant = 0.04
highest = lax.Precision.HIGHEST
tangent_pairs = ((1, 2), (2, 0), (0, 1))


def with_halo(block, sides, width):
    for axis, dim in sides:
        count = lax.axis_size(axis)
        forward = [(i, i + 1) for i in range(count - 1)]
        backward = [(target, source) for source, target in forward]
        low = lax.ppermute(
            lax.slice_in_dim(block, block.shape[dim] - width, None, axis=dim), axis, forward
        )
        high = lax.ppermute(lax.slice_in_dim(block, 0, width, axis=dim), axis, backward)
        block = jnp.concatenate([low, block, high], axis=dim)
    return block


def lagrange_slopes(node_points):
    count = node_points.shape[0]
    weights = np.array(
        [
            np.prod([node_points[i] - node_points[m] for m in range(count) if m != i])
            for i in range(count)
        ]
    )
    matrix = np.zeros((count, count))
    for i in range(count):
        for j in range(count):
            if i != j:
                matrix[i, j] = weights[i] / weights[j] / (node_points[i] - node_points[j])
            else:
                matrix[i, i] = sum(
                    (1.0 / (node_points[i] - node_points[m]) for m in range(count) if m != i)
                )
    return matrix


def legendre_values(node_points):
    columns = [
        0.0 * node_points + 1.0,
        node_points,
        0.5 * (3.0 * node_points**2 - 1.0),
        0.5 * (5.0 * node_points**3 - 3.0 * node_points),
    ]
    return np.stack(
        [columns[degree] * math.sqrt((2 * degree + 1) / 2.0) for degree in range(4)], axis=1
    )


def build_tables():
    node_points = np.array([-1.0, -1.0 / math.sqrt(5.0), 1.0 / math.sqrt(5.0), 1.0])
    deriv_line = lagrange_slopes(node_points)
    legendre = legendre_values(node_points)
    inverse_mass = legendre @ legendre.T
    ident_four = np.eye(4)
    ident_sixteen = np.eye(16)
    deriv_list = [
        np.kron(ident_sixteen, deriv_line),
        np.kron(np.kron(ident_four, deriv_line), ident_four),
        np.kron(deriv_line, ident_sixteen),
    ]
    lift_list = []
    for direction in range(3):
        side_blocks = []
        for end_node in (0, 3):
            column = inverse_mass[:, end_node : end_node + 1]
            if direction == 0:
                block_part = np.kron(ident_sixteen, column)
            elif direction == 1:
                block_part = np.kron(ident_four, np.kron(column, ident_four))
            else:
                block_part = np.kron(column, ident_sixteen)
            side_blocks.append(block_part)
        lift_list.append(np.concatenate(side_blocks, axis=1))
    return (
        jnp.asarray(np.stack(deriv_list), dtype=jnp.float32),
        jnp.asarray(np.stack(lift_list), dtype=jnp.float32),
    )


def face_traces(tangent, direction):
    element_count = tangent.shape[-1]
    rows_count = tangent.shape[0]
    node_cube = tangent.reshape(rows_count, 4, 4, 4, element_count)
    if direction == 0:
        lower_face, upper_face = (node_cube[:, :, :, 0], node_cube[:, :, :, 3])
    elif direction == 1:
        lower_face, upper_face = (node_cube[:, :, 0], node_cube[:, :, 3])
    else:
        lower_face, upper_face = (node_cube[:, 0], node_cube[:, 3])
    return (
        lower_face.reshape(rows_count, 16, element_count),
        upper_face.reshape(rows_count, 16, element_count),
    )


def tangent_set(fields, direction):
    first_axis, second_axis = tangent_pairs[direction]
    return jnp.stack(
        [fields[first_axis], fields[second_axis], fields[3 + first_axis], fields[3 + second_axis]]
    )


def face_flux(jump_set, side_sign):
    return jnp.stack(
        [
            jump_set[0] - side_sign * jump_set[3],
            jump_set[1] + side_sign * jump_set[2],
            jump_set[2] + side_sign * jump_set[1],
            jump_set[3] - side_sign * jump_set[0],
        ]
    )


def direction_terms(tangent, deriv_matrix, lift_matrix, jump_lower, jump_upper):
    slopes = jnp.einsum("mn,fne->fme", deriv_matrix, tangent, precision=highest)
    volume_part = jnp.stack([-slopes[3], slopes[2], slopes[1], -slopes[0]])
    fluxes = 0.5 * jnp.concatenate(
        [face_flux(jump_lower, -1.0), face_flux(jump_upper, 1.0)], axis=1
    )
    return volume_part + jnp.einsum("mq,fqe->fme", lift_matrix, fluxes, precision=highest)


def surface_current(fields, width_x, width_y):
    layer_size = width_x * width_y
    layers = fields.shape[-1] // layer_size
    magnetic = jnp.stack([fields[3], fields[5]])
    upper_face = face_traces(magnetic, 1)[1].reshape(2, 16, layers, layer_size)[
        ..., layer_size - width_x :
    ]
    top_rows = upper_face.reshape(2, 16, layers * width_x)
    return jnp.stack([-top_rows[0], top_rows[1]])


def pole_update(current, states, decay_rows, gain_rows, resistance):
    voltage = resistance * current + jnp.sum(states, axis=0)
    renewed = decay_rows * states + gain_rows * current
    return (voltage, renewed)


def section_rhs(fields, derivs, lifts, z_jumps, voltage, width_x, width_y):
    layer_size = width_x * width_y
    element_count = fields.shape[-1]
    layers = element_count // layer_size
    totals = {}
    for direction in range(3):
        tangent = tangent_set(fields, direction)
        lower_face, upper_face = face_traces(tangent, direction)
        if direction == 0:
            column_index = jnp.arange(element_count) % width_x
            edge_zero = jnp.zeros((4, 16, 1), fields.dtype)
            from_left = jnp.concatenate([edge_zero, upper_face[..., :-1]], axis=-1)
            from_right = jnp.concatenate([lower_face[..., 1:], edge_zero], axis=-1)
            from_left = jnp.where(column_index == 0, 0.0, from_left)
            from_right = jnp.where(column_index == width_x - 1, 0.0, from_right)
            jump_lower = from_left - lower_face
            jump_upper = from_right - upper_face
        elif direction == 1:
            lower_view = lower_face.reshape(4, 16, layers, layer_size)
            upper_view = upper_face.reshape(4, 16, layers, layer_size)
            row_zero = jnp.zeros((4, 16, layers, width_x), fields.dtype)
            from_below = jnp.concatenate(
                [row_zero, upper_view[..., : layer_size - width_x]], axis=-1
            )
            top_rows = upper_view[..., layer_size - width_x :]
            volt_rows = voltage.reshape(2, 16, layers, width_x)
            outside = jnp.stack(
                [
                    2.0 * volt_rows[0] - top_rows[0],
                    2.0 * volt_rows[1] - top_rows[1],
                    top_rows[2],
                    top_rows[3],
                ]
            )
            from_above = jnp.concatenate([lower_view[..., width_x:], outside], axis=-1)
            jump_lower = (from_below - lower_view).reshape(4, 16, element_count)
            jump_upper = (from_above - upper_view).reshape(4, 16, element_count)
        else:
            jump_lower, jump_upper = z_jumps(lower_face, upper_face)
        direction_sum = direction_terms(
            tangent, derivs[direction], lifts[direction], jump_lower, jump_upper
        )
        first_axis, second_axis = tangent_pairs[direction]
        for position, field_index in enumerate(
            (first_axis, second_axis, 3 + first_axis, 3 + second_axis)
        ):
            if field_index in totals:
                totals[field_index] = totals[field_index] + direction_sum[position]
            else:
                totals[field_index] = direction_sum[position]
    return jnp.stack([totals[field_index] for field_index in range(6)])


def on_device(fields, pole_state, pole_decay, pole_gain, surface_resistance, face_owner):
    derivs, lifts = build_tables()
    owner = face_owner[:, 0]
    layer_size = EX * EY
    element_count = fields.shape[-1]
    groups = lax.axis_size("patch")

    def z_jumps(lower_face, upper_face):
        outgoing = jnp.stack(
            [lower_face[..., :layer_size], upper_face[..., element_count - layer_size :]]
        )
        padded = with_halo(outgoing, ((("slab", "patch"), 0),), 1)
        from_below = jnp.concatenate(
            [padded[0], upper_face[..., : element_count - layer_size]], axis=-1
        )
        from_above = jnp.concatenate([lower_face[..., layer_size:], padded[3]], axis=-1)
        return (from_below - lower_face, from_above - upper_face)

    tables = (
        lax.all_gather(pole_decay, "patch", axis=0, tiled=True),
        lax.all_gather(pole_gain, "patch", axis=0, tiled=True),
        lax.all_gather(surface_resistance, "patch", axis=0, tiled=True),
    )
    owner_hot = (owner[None, :] == jnp.arange(groups, dtype=jnp.int32)[:, None]).astype(jnp.float32)
    decay_rows = jnp.dot(tables[0].T, owner_hot, precision=highest)[:, None, None, :]
    gain_rows = jnp.dot(tables[1].T, owner_hot, precision=highest)[:, None, None, :]
    resistance = jnp.dot(tables[2], owner_hot, precision=highest)

    def poles_step(current, states):
        return pole_update(current, states, decay_rows, gain_rows, resistance)

    def advance(state_fields, states):
        current = surface_current(state_fields, EX, EY)
        voltage, renewed = poles_step(current, states)
        return (section_rhs(state_fields, derivs, lifts, z_jumps, voltage, EX, EY), renewed)

    first_rhs, middle_states = advance(fields, pole_state)
    middle = fields + courant * first_rhs
    second_rhs, final_states = advance(middle, middle_states)
    advanced = 0.5 * fields + 0.5 * (middle + courant * second_rhs)
    return (advanced, final_states)


def solution(mesh):
    return jax.shard_map(
        on_device,
        mesh=mesh,
        in_specs=(
            P(None, None, ("slab", "patch")),
            P(None, None, None, ("slab", "patch")),
            P(("slab", "patch"), None),
            P(("slab", "patch"), None),
            P(("slab", "patch")),
            P(("slab", "patch"), None),
        ),
        out_specs=(P(None, None, ("slab", "patch")), P(None, None, None, ("slab", "patch"))),
        check_vma=False,
    )
```

profile of v0, /device:TPU:23, one launch (start us, length us, event | category | flops | bytes accessed | tf_op | source)
XLA Modules:
  0.0 56.0 jit_solution(5531254369755331483)
XLA Ops:
  0.6 1.1 %fusion.135 = (f32[2,64,256]{2,1,0:T(8,128)S(1)}, f32[2,64,256]{2,1,0:T(8,128)S(1)}, f32[2,64,256]{2,1,0:T(8,128)S(1)}, f32[2,64,256]{2,1,0:T(8,128)S(1)}) fusion(f32[6,64,256]{2,1,0:T(8,128)} %param.8), kind=kLoop, calls=%fused_computation.280 | loop fusion | bytes 1048576 | tf_op jit(solution)/shard_map/slice | solution.py:113
  2.0 3.8 %collective-permute-start = (f32[1,4,16,256]{3,2,1,0:T(8,128)S(1)}, f32[1,4,16,256]{3,2,1,0:T(8,128)S(1)}, u32[]{:S(2)}, u32[]{:S(2)}) collective-permute-start(f32[1,4,16,256]{3,2,1,0:T(8,128)S(1)} %stack_reshape_squeeze.12), channel_id=1, source_target_pairs={{0,1},{1,2},{2,3},{3,4},{4,5},{5,6},{6,7},{7,8},{8,9},{9,10},{10,1... | collective-permute-start | bytes 196616 | tf_op jit(solution)/shard_map/ppermute | solution.py:23
  5.8 1.9 %collective-permute-start.1 = (f32[1,4,16,256]{3,2,1,0:T(8,128)S(1)}, f32[1,4,16,256]{3,2,1,0:T(8,128)S(1)}, u32[]{:S(2)}, u32[]{:S(2)}) collective-permute-start(f32[1,4,16,256]{3,2,1,0:T(8,128)S(1)} %stack_reshape_squeeze.13), channel_id=1, source_target_pairs={{1,0},{2,1},{3,2},{4,3},{5,4},{6,5},{7,6},{8,7},{9,8},{10,9},{11,1... | collective-permute-start | bytes 196616 | tf_op jit(solution)/shard_map/ppermute | solution.py:26
  7.9 0.4 slice_reduce_fusion.2
  8.4 0.1 select_subtract_fusion.3
  8.6 0.7 %copy-done.4 = f32[64,64,1]{1,0,2:T(8,128)S(1)} copy-done((f32[64,64,1]{1,0,2:T(8,128)S(1)}, f32[64,64,1]{1,0,2:T(8,128)}, u32[]{:S(2)}) %copy-start.4) | copy-done | bytes 16408
  9.3 0.4 convolution_bitcast_fusion.7
  9.9 0.7 %copy-done.6 = f32[1,12]{1,0:T(1,128)S(1)} copy-done((f32[1,12]{1,0:T(1,128)S(1)}, f32[1,12]{1,0:T(1,128)}, u32[]{:S(2)}) %copy-start.6) | copy-done | bytes 72
  10.5 5.5 %all-gather = f32[4,1,12]{2,1,0:T(1,128)S(1)} all-gather(f32[1,1,12]{2,1,0:T(1,128)S(1)} %bitcast.188), channel_id=1, replica_groups=mesh['slab'=8,'patch'=4] {'patch'}, dimensions={0}, use_global_device_ids=true | all-gather | bytes 240 | tf_op jit(solution)/shard_map/all_gather | solution.py:226
  16.0 0.7 %copy-done.5 = s32[16,1]{0,1:T(1,128)S(1)} copy-done((s32[16,1]{0,1:T(1,128)S(1)}, s32[16,1]{0,1:T(1,128)}, u32[]{:S(2)}) %copy-start.5) | copy-done | bytes 88
  16.6 0.2 convolution_bitcast_fusion.13
  16.8 0.1 copy.20
  16.9 0.7 %copy-done.7 = f32[1,12]{1,0:T(1,128)S(1)} copy-done((f32[1,12]{1,0:T(1,128)S(1)}, f32[1,12]{1,0:T(1,128)}, u32[]{:S(2)}) %copy-start.7) | copy-done | bytes 72
  17.6 5.0 %all-gather.1 = f32[4,1,12]{2,1,0:T(1,128)S(1)} all-gather(f32[1,1,12]{2,1,0:T(1,128)S(1)} %bitcast.189), channel_id=1, replica_groups=mesh['slab'=8,'patch'=4] {'patch'}, dimensions={0}, use_global_device_ids=true | all-gather | bytes 240 | tf_op jit(solution)/shard_map/all_gather | solution.py:227
  22.6 0.2 convolution_bitcast_fusion.12
  23.5 0.6 %copy-done.11 = u32[32]{0:T(128)S(1)} copy-done((u32[32]{0:T(128)S(1)}, u32[32]{0:T(128)}, u32[]{:S(2)}) %copy-start.11) | copy-done | bytes 152
  24.1 0.6 %dynamic-slice = u32[1]{0:T(128)} dynamic-slice(u32[32]{0:T(128)S(1)} %copy-done.11, u32[]{:T(128)S(6)} %add.280), dynamic_slice_sizes={1} | dynamic-slice | bytes 12
  24.7 0.8 %dynamic-update-slice = f32[4]{0:T(128)S(1)} dynamic-update-slice(f32[4]{0:T(128)S(1)} %broadcast.160, f32[1]{0:T(128)S(6)} %copy.41, u32[]{:T(128)} %bitcast.7) | dynamic-update-slice | bytes 12
  25.5 0.1 copy.21
  25.5 5.2 %all-reduce.6 = f32[4]{0:T(128)S(1)} all-reduce(f32[4]{0:T(128)S(1)} %dynamic-update-slice), channel_id=1, replica_groups=mesh['slab'=8,'patch'=4] {'patch'}, use_global_device_ids=true, to_apply=%add.6 | all-reduce | flops 4 | bytes 32
  30.7 0.1 convolution_bitcast_fusion.14
  31.1 0.8 %copy-done.1 = f32[12,2,16,16]{3,2,1,0:T(8,128)S(1)} copy-done((f32[12,2,16,16]{3,2,1,0:T(8,128)S(1)}, f32[12,2,16,16]{3,2,1,0:T(8,128)}, u32[]{:S(2)}) %copy-start.1) | copy-done | bytes 24600
  32.2 0.1 maximum_subtract_fusion
  32.4 0.7 %copy-done.3 = f32[64,64,1]{1,0,2:T(8,128)S(1)} copy-done((f32[64,64,1]{1,0,2:T(8,128)S(1)}, f32[64,64,1]{1,0,2:T(8,128)}, u32[]{:S(2)}) %copy-start.3) | copy-done | bytes 16408
  33.1 0.4 convolution_bitcast_fusion.11
  33.5 0.7 %copy-done.2 = f32[64,64,1]{1,0,2:T(8,128)S(1)} copy-done((f32[64,64,1]{1,0,2:T(8,128)S(1)}, f32[64,64,1]{1,0,2:T(8,128)}, u32[]{:S(2)}) %copy-start.2) | copy-done | bytes 16408
  34.2 0.4 convolution_bitcast_fusion.9
  34.7 0.7 %copy-done.10 = f32[64,32,1]{0,1,2:T(8,128)S(1)} copy-done((f32[64,32,1]{0,1,2:T(8,128)S(1)}, f32[64,32,1]{0,1,2:T(8,128)}, u32[]{:S(2)}) %copy-start.10) | copy-done | bytes 8216
  35.4 0.4 fusion.3
  35.8 0.7 %copy-done.9 = f32[64,32,1]{0,1,2:T(8,128)S(1)} copy-done((f32[64,32,1]{0,1,2:T(8,128)S(1)}, f32[64,32,1]{0,1,2:T(8,128)}, u32[]{:S(2)}) %copy-start.9) | copy-done | bytes 8216
  36.5 0.4 fusion.5
  37.1 0.7 %copy-done.8 = f32[64,32,1]{0,1,2:T(8,128)S(1)} copy-done((f32[64,32,1]{0,1,2:T(8,128)S(1)}, f32[64,32,1]{0,1,2:T(8,128)}, u32[]{:S(2)}) %copy-start.8) | copy-done | bytes 8216
  37.8 0.4 fusion.4
  38.5 0.4 convolution_bitcast_fusion.1
  38.9 0.4 convolution_bitcast_fusion.5
  39.3 0.4 convolution_bitcast_fusion.3
  39.8 0.4 slice_reduce_fusion
  40.3 0.1 select_subtract_fusion.1
  40.8 0.1 pad_subtract_fusion
  41.1 0.1 maximum_subtract_fusion.1
  41.4 5.7 %collective-permute-start.2 = (f32[1,4,16,256]{3,2,1,0:T(8,128)S(1)}, f32[1,4,16,256]{3,2,1,0:T(8,128)S(1)}, u32[]{:S(2)}, u32[]{:S(2)}) collective-permute-start(f32[1,4,16,256]{3,2,1,0:T(8,128)S(1)} %stack_reshape_squeeze.14), channel_id=1, source_target_pairs={{0,1},{1,2},{2,3},{3,4},{4,5},{5,6},{6,7},{7,8},{8,9},{9,10},{10,1... | collective-permute-start | bytes 196616 | tf_op jit(solution)/shard_map/ppermute | solution.py:23
  47.2 1.9 %collective-permute-start.3 = (f32[1,4,16,256]{3,2,1,0:T(8,128)S(1)}, f32[1,4,16,256]{3,2,1,0:T(8,128)S(1)}, u32[]{:S(2)}, u32[]{:S(2)}) collective-permute-start(f32[1,4,16,256]{3,2,1,0:T(8,128)S(1)} %stack_reshape_squeeze.15), channel_id=1, source_target_pairs={{1,0},{2,1},{3,2},{4,3},{5,4},{6,5},{7,6},{8,7},{9,8},{10,9},{11,1... | collective-permute-start | bytes 196616 | tf_op jit(solution)/shard_map/ppermute | solution.py:26
  49.1 0.7 %multiply_add_fusion.1 = f32[12,2,16,16]{3,2,1,0:T(8,128)} fusion(f32[12,2,16,16]{3,2,1,0:T(8,128)S(1)} %copy-done.1, f32[2,16,16]{2,1,0:T(8,128)S(1)} %get-tuple-element.106, f32[2,16,16]{2,1,0:T(8,128)S(1)} %pad_maximum_fusion.8, f32[12,16]{1,0:T(8,128)S(1)} %copy.21, f32[12,16]{1,0:T(8,128)S(1)} %copy.20), kind=kLoop, calls=%fused_computation.29 | loop fusion | flops 36864 | bytes 54784 | tf_op jit(solution)/shard_map/add | solution.py:150
  49.9 0.4 fusion
  50.3 0.4 fusion.2
  50.8 3.7 %collective-permute-done.3 = f32[1,4,16,256]{3,2,1,0:T(8,128)S(1)} collective-permute-done((f32[1,4,16,256]{3,2,1,0:T(8,128)S(1)}, f32[1,4,16,256]{3,2,1,0:T(8,128)S(1)}, u32[]{:S(2)}, u32[]{:S(2)}) %collective-permute-start.3) | collective-permute-done | bytes 65568 | tf_op jit(solution)/shard_map/ppermute | solution.py:26
  54.6 0.4 fusion.1
  55.1 0.8 %add_multiply_fusion = f32[6,64,256]{2,1,0:T(8,128)} fusion(f32[6,64,256]{2,1,0:T(8,128)S(1)} %copy-done, f32[6,64,256]{2,1,0:T(8,128)S(1)} %fusion.91, f32[6,64,256]{2,1,0:T(8,128)S(1)} %fusion.97), kind=kLoop, calls=%fused_computation.21 | loop fusion | flops 589824 | bytes 1572864 | tf_op jit(solution)/shard_map/add | solution.py:246
  (113 shorter events, 2.7 us)
Async XLA Ops:
  1.9 5.9 %copy-start = (f32[6,64,256]{2,1,0:T(8,128)S(1)}, f32[6,64,256]{2,1,0:T(8,128)}, u32[]{:S(2)}) copy-start(f32[6,64,256]{2,1,0:T(8,128)} %param.8) | copy-start | bytes 1179652
  2.0 35.0 %collective-permute-start = (f32[1,4,16,256]{3,2,1,0:T(8,128)S(1)}, f32[1,4,16,256]{3,2,1,0:T(8,128)S(1)}, u32[]{:S(2)}, u32[]{:S(2)}) collective-permute-start(f32[1,4,16,256]{3,2,1,0:T(8,128)S(1)} %stack_reshape_squeeze.12), channel_id=1, source_target_pairs={{0,1},{1,2},{2,3},{3,4},{4,5},{5,6},{6,7},{7,8},{8,9},{9,10},{10,1... | collective-permute-start | bytes 196616 | tf_op jit(solution)/shard_map/ppermute | solution.py:23
  5.8 31.2 %collective-permute-start.1 = (f32[1,4,16,256]{3,2,1,0:T(8,128)S(1)}, f32[1,4,16,256]{3,2,1,0:T(8,128)S(1)}, u32[]{:S(2)}, u32[]{:S(2)}) collective-permute-start(f32[1,4,16,256]{3,2,1,0:T(8,128)S(1)} %stack_reshape_squeeze.13), channel_id=1, source_target_pairs={{1,0},{2,1},{3,2},{4,3},{5,4},{6,5},{7,6},{8,7},{9,8},{10,9},{11,1... | collective-permute-start | bytes 196616 | tf_op jit(solution)/shard_map/ppermute | solution.py:26
  8.5 0.8 %copy-start.4 = (f32[64,64,1]{1,0,2:T(8,128)S(1)}, f32[64,64,1]{1,0,2:T(8,128)}, u32[]{:S(2)}) copy-start(f32[64,64,1]{1,0,2:T(8,128)} %constant.79) | copy-start | bytes 49156
  9.9 0.7 %copy-start.6 = (f32[1,12]{1,0:T(1,128)S(1)}, f32[1,12]{1,0:T(1,128)}, u32[]{:S(2)}) copy-start(f32[1,12]{1,0:T(1,128)} %param.10) | copy-start | bytes 148
  16.0 0.7 %copy-start.5 = (s32[16,1]{0,1:T(1,128)S(1)}, s32[16,1]{0,1:T(1,128)}, u32[]{:S(2)}) copy-start(s32[16,1]{0,1:T(1,128)} %param.13) | copy-start | bytes 196
  16.9 0.7 %copy-start.7 = (f32[1,12]{1,0:T(1,128)S(1)}, f32[1,12]{1,0:T(1,128)}, u32[]{:S(2)}) copy-start(f32[1,12]{1,0:T(1,128)} %param.11) | copy-start | bytes 148
  23.5 0.7 %copy-start.11 = (u32[32]{0:T(128)S(1)}, u32[32]{0:T(128)}, u32[]{:S(2)}) copy-start(u32[32]{0:T(128)} %constant.71) | copy-start | bytes 388
  31.0 0.9 %copy-start.1 = (f32[12,2,16,16]{3,2,1,0:T(8,128)S(1)}, f32[12,2,16,16]{3,2,1,0:T(8,128)}, u32[]{:S(2)}) copy-start(f32[12,2,16,16]{3,2,1,0:T(8,128)} %param.9) | copy-start | bytes 73732
  32.4 0.8 %copy-start.3 = (f32[64,64,1]{1,0,2:T(8,128)S(1)}, f32[64,64,1]{1,0,2:T(8,128)}, u32[]{:S(2)}) copy-start(f32[64,64,1]{1,0,2:T(8,128)} %constant.75) | copy-start | bytes 49156
  33.5 0.8 %copy-start.2 = (f32[64,64,1]{1,0,2:T(8,128)S(1)}, f32[64,64,1]{1,0,2:T(8,128)}, u32[]{:S(2)}) copy-start(f32[64,64,1]{1,0,2:T(8,128)} %constant.77) | copy-start | bytes 49156
  34.6 0.7 %copy-start.10 = (f32[64,32,1]{0,1,2:T(8,128)S(1)}, f32[64,32,1]{0,1,2:T(8,128)}, u32[]{:S(2)}) copy-start(f32[64,32,1]{0,1,2:T(8,128)} %constant.80) | copy-start | bytes 24580
  35.8 0.7 %copy-start.9 = (f32[64,32,1]{0,1,2:T(8,128)S(1)}, f32[64,32,1]{0,1,2:T(8,128)}, u32[]{:S(2)}) copy-start(f32[64,32,1]{0,1,2:T(8,128)} %constant.76) | copy-start | bytes 24580
  37.1 0.7 %copy-start.8 = (f32[64,32,1]{0,1,2:T(8,128)S(1)}, f32[64,32,1]{0,1,2:T(8,128)}, u32[]{:S(2)}) copy-start(f32[64,32,1]{0,1,2:T(8,128)} %constant.78) | copy-start | bytes 24580
  41.4 9.4 %collective-permute-start.2 = (f32[1,4,16,256]{3,2,1,0:T(8,128)S(1)}, f32[1,4,16,256]{3,2,1,0:T(8,128)S(1)}, u32[]{:S(2)}, u32[]{:S(2)}) collective-permute-start(f32[1,4,16,256]{3,2,1,0:T(8,128)S(1)} %stack_reshape_squeeze.14), channel_id=1, source_target_pairs={{0,1},{1,2},{2,3},{3,4},{4,5},{5,6},{6,7},{7,8},{8,9},{9,10},{10,1... | collective-permute-start | bytes 196616 | tf_op jit(solution)/shard_map/ppermute | solution.py:23
  47.2 7.4 %collective-permute-start.3 = (f32[1,4,16,256]{3,2,1,0:T(8,128)S(1)}, f32[1,4,16,256]{3,2,1,0:T(8,128)S(1)}, u32[]{:S(2)}, u32[]{:S(2)}) collective-permute-start(f32[1,4,16,256]{3,2,1,0:T(8,128)S(1)} %stack_reshape_squeeze.15), channel_id=1, source_target_pairs={{1,0},{2,1},{3,2},{4,3},{5,4},{6,5},{7,6},{8,7},{9,8},{10,9},{11,1... | collective-permute-start | bytes 196616 | tf_op jit(solution)/shard_map/ppermute | solution.py:26
where the time goes:
time: 56.7 us; the launch traced here: 56 us
  blocking collectives  15.7 us (28%)
  starting transfers between devices  13.4 us (24%)
  local copies, waits for them, and re-layouts  12.7 us (22%)
  matrix products  5.17 us (9%)
  waiting for transfers between devices  3.75 us (7%)
  other arithmetic  3.1 us (5%)
  between operations  2.2 us (4%)
    ppermute x2, starting transfers between devices, with_halo(): lax.ppermute(lax.slice_in_dim(block, block.shape[dim] - width, None, axis...  9.55 us
    unnamed x28, local copies, waits for them, and re-layouts  9.11 us
    all_gather x1, blocking collectives, on_device(): lax.all_gather(pole_decay, 'patch', axis=0, tiled=True)  5.46 us
    unnamed x1, blocking collectives  5.2 us
    all_gather x1, blocking collectives, on_device(): lax.all_gather(pole_gain, 'patch', axis=0, tiled=True)  5.03 us
    ppermute x2, starting transfers between devices, with_halo(): lax.ppermute(lax.slice_in_dim(block, 0, width, axis=dim), axis, backward)  3.84 us
    ppermute x2, waiting for transfers between devices, with_halo(): lax.ppermute(lax.slice_in_dim(block, 0, width, axis=dim), axis, backward)  3.75 us
    dot_general x6, matrix products, direction_terms(): jnp.einsum('mq,fqe->fme', lift_matrix, fluxes, precision=highest)  2.48 us
  transfers between devices with their start and end apart: 4, of which 1 were waited for; matrix products, arithmetic and copies ran while one was open for 13% of the time, Pallas kernels for 0%

commit v1 on v0

v1 whole, which is shorter than its diff:
```python
import functools
import math

import jax
import jax.numpy as jnp
import numpy as np
from jax import lax
from jax.experimental import pallas as pl
from jax.experimental.pallas import tpu as pltpu
from jax.sharding import PartitionSpec as P

EX = 16
EY = 16
LAYER = EX * EY
POLES = 12
courant = 0.04
tangent_pairs = ((1, 2), (2, 0), (0, 1))
ROWS = 32
MESSAGE = 40
AXES = ("slab", "patch")

VM = pl.BlockSpec(memory_space=pltpu.VMEM)
HB = pl.BlockSpec(memory_space=pl.ANY)


def lagrange_slopes(node_points):
    count = node_points.shape[0]
    weights = np.array(
        [
            np.prod([node_points[i] - node_points[m] for m in range(count) if m != i])
            for i in range(count)
        ]
    )
    matrix = np.zeros((count, count))
    for i in range(count):
        for j in range(count):
            if i != j:
                matrix[i, j] = weights[i] / weights[j] / (node_points[i] - node_points[j])
            else:
                matrix[i, i] = sum(
                    (1.0 / (node_points[i] - node_points[m]) for m in range(count) if m != i)
                )
    return matrix


def legendre_values(node_points):
    columns = [
        0.0 * node_points + 1.0,
        node_points,
        0.5 * (3.0 * node_points**2 - 1.0),
        0.5 * (5.0 * node_points**3 - 3.0 * node_points),
    ]
    return np.stack(
        [columns[degree] * math.sqrt((2 * degree + 1) / 2.0) for degree in range(4)], axis=1
    )


def build_tables():
    node_points = np.array([-1.0, -1.0 / math.sqrt(5.0), 1.0 / math.sqrt(5.0), 1.0])
    slope = lagrange_slopes(node_points)
    legendre = legendre_values(node_points)
    inverse_mass = legendre @ legendre.T
    four, sixteen = np.eye(4), np.eye(16)
    derivs = [
        np.kron(sixteen, slope),
        np.kron(np.kron(four, slope), four),
        np.kron(slope, sixteen),
    ]

    def spread(direction, column):
        column = column[:, None]
        if direction == 0:
            return np.kron(sixteen, column)
        if direction == 1:
            return np.kron(four, np.kron(column, four))
        return np.kron(column, sixteen)

    whole = np.zeros((384, 512))

    def rows(field):
        return slice(64 * field, 64 * field + 64)

    for direction in range(3):
        b, c = tangent_pairs[direction]
        slopes = derivs[direction]
        whole[rows(b), rows(3 + c)] -= slopes
        whole[rows(c), rows(3 + b)] += slopes
        whole[rows(3 + b), rows(c)] += slopes
        whole[rows(3 + c), rows(b)] -= slopes
        for side in range(2):
            sign = 2.0 * side - 1.0
            lift = 0.5 * spread(direction, inverse_mass[:, 3 * side])
            trace = spread(direction, four[3 * side]).T
            parts = (((b, 1.0), (3 + c, -sign)), ((c, 1.0), (3 + b, sign)))
            goals = (((b, 1.0), (3 + c, -sign)), ((c, 1.0), (3 + b, sign)))
            for which in range(2):
                for goal, factor in goals[which]:
                    for source, weight in parts[which]:
                        whole[rows(goal), rows(source)] -= factor * weight * (lift @ trace)
                    if direction < 2:
                        start = 384 + 64 * direction + 32 * side + 16 * which
                        whole[rows(goal), start : start + 16] += factor * lift
    return courant * whole, 0.5 * courant * inverse_mass[:, 0], 0.5 * courant * inverse_mass[:, 3]


WHOLE, LOW_WEIGHT, HIGH_WEIGHT = build_tables()
LOW_WEIGHT = [float(w) for w in LOW_WEIGHT]
HIGH_WEIGHT = [float(w) for w in HIGH_WEIGHT]
WHOLE_HIGH = WHOLE.astype(jnp.bfloat16)
WHOLE_REST = (WHOLE - WHOLE_HIGH.astype(np.float64)).astype(jnp.bfloat16)


def group_rounds(groups):
    rounds = groups.bit_length() - 1
    held = [0]
    plan = []
    for r in range(1, rounds + 1):
        flip = (1 << r) - 1
        plan.append((flip, list(held)))
        held = held + [offset ^ flip for offset in held]
    return plan, held


def crossing_pairs(slabs, groups):
    pairs = []
    for g in range(slabs):
        first, last = g * groups, g * groups + groups - 1
        if g + 1 < slabs:
            pairs += [(last, last + 1), (last + 1, last)]
        idle = [
            d
            for d in range(first, last + 1)
            if not ((d == first and g > 0) or (d == last and g + 1 < slabs))
        ]
        pairs += [(d, idle[(k + 1) % len(idle)]) for k, d in enumerate(idle)]
    return pairs


def to_message(out1_ref, out2_ref, up, down):
    even = lax.rem(lax.axis_index("patch"), 2) == 0
    for which in range(2):
        here = slice(16 * which, 16 * which + 16)
        out1_ref[here, :] = jnp.where(even, up[which], down[which])
        out2_ref[here, :] = jnp.where(even, down[which], up[which])


def first_kernel(fields, decay, gain, resist, out1, out2, own, faces, decays, gains, resists, sems):
    copies = [
        pltpu.make_async_copy(fields.at[0:2, 48:64], faces.at[0, 0:2], sems.at[0]),
        pltpu.make_async_copy(fields.at[3:5, 48:64], faces.at[0, 2:4], sems.at[1]),
        pltpu.make_async_copy(fields.at[0:2, 0:16], faces.at[1, 0:2], sems.at[2]),
        pltpu.make_async_copy(fields.at[3:5, 0:16], faces.at[1, 2:4], sems.at[3]),
        pltpu.make_async_copy(decay, decays, sems.at[4]),
        pltpu.make_async_copy(gain, gains, sems.at[5]),
        pltpu.make_async_copy(resist, resists, sems.at[6]),
    ]
    for copy in copies:
        copy.start()
    for copy in copies:
        copy.wait()
    ex, ey, hx, hy = (faces[0, f] for f in range(4))
    up = (ex + hy, ey - hx)
    ex, ey, hx, hy = (faces[1, f] for f in range(4))
    down = (ex - hy, ey + hx)
    to_message(out1, out2, up, down)
    own[...] = jnp.zeros_like(own)
    for which, ref in enumerate((decays, gains, resists)):
        own[which : which + 1, 0 : ref.shape[1]] = ref[...]
    out1[32:40, 0:128] = own[...]


def y_rows(block, j):
    return jnp.concatenate([block[16 * k + 4 * j : 16 * k + 4 * j + 4] for k in range(4)], axis=0)


def exteriors(ref, halves, voltage):
    lane = lax.broadcasted_iota(jnp.int32, (16, LAYER), 1)
    column = lane % EX
    left, right = column == 0, column == EX - 1
    bottom, top = lane < EX, lane >= LAYER - EX

    for slot, field in enumerate((1, 2, 4, 5)):
        for half in range(2):
            halves[2 * slot + half] = ref[field, :, 128 * half : 128 * half + 128]

    def at_x(slot, i):
        return jnp.concatenate(
            [halves[2 * slot + half, pl.ds(i, 16, stride=4), :] for half in range(2)], axis=1
        )

    def at_y(field, j):
        return y_rows(ref[field], j)

    ey, ez, hy, hz = (at_x(slot, 3) for slot in range(4))
    low = (ey + hz, ez - hy)
    ey, ez, hy, hz = (at_x(slot, 0) for slot in range(4))
    high = (ey - hz, ez + hy)
    parts = [jnp.where(left, 0.0, pltpu.roll(v, 1, 1)) for v in low]
    parts += [jnp.where(right, 0.0, pltpu.roll(v, LAYER - 1, 1)) for v in high]
    ez, ex, hz, hx = (at_y(f, 3) for f in (2, 0, 5, 3))
    low = (ez + hx, ex - hz)
    ez, ex, hz, hx = (at_y(f, 0) for f in (2, 0, 5, 3))
    high = (ez - hx, ex + hz)
    parts += [jnp.where(bottom, 0.0, pltpu.roll(v, EX, 1)) for v in low]
    empty = jnp.zeros((16, LAYER - 128), jnp.float32)
    for which in range(2):
        mirror = 2.0 * jnp.concatenate([empty, voltage[which]], axis=1) - low[which]
        parts.append(jnp.where(top, mirror, pltpu.roll(high[which], LAYER - EX, 1)))
    return jnp.concatenate(parts, axis=0)


def update(ref, halves, voltage, high_ref, rest_ref):
    stacked = jnp.concatenate([ref[f] for f in range(6)] + [exteriors(ref, halves, voltage)], axis=0)
    high = stacked.astype(jnp.bfloat16)
    rest = (stacked - high.astype(jnp.float32)).astype(jnp.bfloat16)
    dot = functools.partial(jnp.dot, preferred_element_type=jnp.float32)
    return dot(high_ref[...], high) + (dot(high_ref[...], rest) + dot(rest_ref[...], high))


def currents(ref):
    found = []
    for field, sign in ((3, -1.0), (5, 1.0)):
        rows = y_rows(ref[field, :, LAYER - 128 : LAYER], 3)
        found.append(sign * pltpu.roll(rows, EX, 1))
    return found


def second_kernel(fields, states, high_ref, rest_ref, out, current, sums, halves):
    sums[...] = jnp.zeros_like(sums)
    for part in range(2):
        total = states[0, part]
        for pole in range(1, POLES):
            total = total + states[pole, part]
        sums[part, :, 0:EX] = total
    voltage = [pltpu.roll(sums[part], 128 - EX, 1) for part in range(2)]
    result = update(fields, halves, voltage, high_ref, rest_ref)
    for f in range(6):
        out[f] = fields[f] + result[64 * f : 64 * f + 64]
    for part, value in enumerate(currents(fields)):
        current[part] = value


def z_exteriors(slabs, groups, got1, others, crossing):
    position = lax.axis_index("patch")
    device = lax.axis_index("slab") * groups + position
    even = lax.rem(position, 2) == 0
    edge = position + lax.rem(position, 2)
    end = (device == 0) | (device == slabs * groups - 1)
    low, high = [], []
    for which in range(2):
        here = slice(16 * which, 16 * which + 16)
        far = crossing[here, :]
        for r, ref in enumerate(others):
            half = 2 << r
            inside = (lax.rem(edge, 2 * half) == half) & (edge < groups)
            far = jnp.where(inside, ref[here, :], far)
        far = jnp.where(end, 0.0, far)
        near = got1[here, :]
        low.append(jnp.where(even, far, near))
        high.append(jnp.where(even, near, far))
    return low, high


def face_parameter(owner, sets, row, column):
    total = None
    for source, ref, start in sets:
        value = jnp.where(owner == source, ref[start + row : start + row + 1, column : column + 1], 0.0)
        total = value if total is None else total + value
    return total


def parameter_sets(held, refs):
    position = lax.axis_index("patch")
    return [(position ^ offset, refs[ref], start) for offset, ref, start in held]


def at_faces(value):
    return pltpu.roll(value, 128 - EX, 1)


def third_kernel(slabs, groups, held, *refs):
    rounds = groups.bit_length() - 1
    before, current, owner, own = refs[:4]
    got = refs[4 : 4 + rounds]
    crossing = refs[4 + rounds]
    out1, out2, outz, drive = refs[5 + rounds : 9 + rounds]
    low, high = z_exteriors(slabs, groups, got[0], got[1:], crossing)
    sets = parameter_sets(held, (own,) + tuple(got))
    resist = face_parameter(owner[...], sets, 2, 0)
    pushes = []
    for part in range(2):
        drive[part] = jnp.zeros((16, 128), jnp.float32)
        drive[part, :, 0:EX] = resist * current[part, :, 0:EX]
        rolled = at_faces(drive[part])
        drive[part] = rolled
        pushes.append(jnp.concatenate([jnp.zeros((16, LAYER - 128), jnp.float32), rolled], axis=1))
    for which in range(2):
        here = slice(16 * which, 16 * which + 16)
        outz[here, :] = low[which]
        outz[32 + 16 * which : 48 + 16 * which, :] = high[which]

    def pushed(part, k):
        rows = pushes[part][4 * k : 4 * k + 4]
        return jnp.concatenate([2.0 * HIGH_WEIGHT[j] * rows for j in range(4)], axis=0)

    ex, ey, hx, hy = (before[f, 48:64, :] for f in (0, 1, 3, 4))
    weight = 2.0 * LOW_WEIGHT[3]
    up = (
        ex + hy + weight * low[0] + pushed(1, 3),
        ey - hx + weight * low[1] + pushed(0, 3),
    )
    ex, ey, hx, hy = (before[f, 0:16, :] for f in (0, 1, 3, 4))
    weight = 2.0 * HIGH_WEIGHT[0]
    down = (
        ex - hy + weight * high[0] + pushed(1, 0),
        ey + hx + weight * high[1] - pushed(0, 0),
    )
    to_message(out1, out2, up, down)


def z_update(field, k, low, high):
    a, b = LOW_WEIGHT[k], HIGH_WEIGHT[k]
    if field == 0:
        return a * low[0] + b * high[0]
    if field == 1:
        return a * low[1] + b * high[1]
    if field == 3:
        return b * high[1] - a * low[1]
    return a * low[0] - b * high[0]


def fourth_kernel(held, rounds, *refs):
    fields, before, current, states, beyond, drive, owner, own = refs[:8]
    got = refs[8 : 8 + rounds]
    high_ref, rest_ref, out, new_states, middle, sums, table, halves = refs[8 + rounds :]
    low = [beyond[0:16, :], beyond[16:32, :]]
    high = [beyond[32:48, :], beyond[48:64, :]]
    for f in (0, 1, 3, 4):
        for k in range(4):
            here = slice(16 * k, 16 * k + 16)
            middle[f, here, :] = before[f, here, :] + z_update(f, k, low, high)
    for f in (2, 5):
        middle[f] = before[f]
    for f, part, sign in ((2, 0, 2.0), (3, 0, -2.0), (0, 1, 2.0), (5, 1, 2.0)):
        for k in range(4):
            rows = drive[part, 4 * k : 4 * k + 4, :]
            added = jnp.concatenate([sign * HIGH_WEIGHT[j] * rows for j in range(4)], axis=0)
            here = slice(16 * k, 16 * k + 16)
            middle[f, here, LAYER - 128 : LAYER] = middle[f, here, LAYER - 128 : LAYER] + added
    sets = parameter_sets(held, (own,) + tuple(got))
    names = owner[...]
    for row in range(2):
        for pole in range(POLES):
            table[POLES * row + pole : POLES * row + pole + 1, 0:EX] = face_parameter(
                names, sets, row, pole
            )
    resist = face_parameter(names, sets, 2, 0)
    later = currents(middle)
    sums[...] = jnp.zeros_like(sums)
    for part in range(2):
        total = resist * later[part][:, 0:EX]
        first_current = current[part, :, 0:EX]
        for pole in range(POLES):
            decay = table[pole : pole + 1, 0:EX]
            gain = table[POLES + pole : POLES + pole + 1, 0:EX]
            renewed = decay * states[pole, part] + gain * first_current
            total = total + renewed
            new_states[pole, part] = decay * renewed + gain * later[part][:, 0:EX]
        sums[part, :, 0:EX] = total
    voltage = [at_faces(sums[part]) for part in range(2)]
    result = update(middle, halves, voltage, high_ref, rest_ref)
    for f in range(6):
        out[f] = 0.5 * fields[f] + 0.5 * (middle[f] + result[64 * f : 64 * f + 64])


def fifth_kernel(slabs, groups, *refs):
    rounds = groups.bit_length() - 1
    before = refs[0]
    got = refs[1 : 1 + rounds]
    crossing, out, held, sems = refs[1 + rounds :]
    copies = []
    for f in (2, 5):
        copies.append(pltpu.make_async_copy(before.at[f], out.at[f], sems.at[f]))
        copies[-1].start()
    low, high = z_exteriors(slabs, groups, got[0], got[1:], crossing)
    low = [0.5 * v for v in low]
    high = [0.5 * v for v in high]
    for slot, f in enumerate((0, 1, 3, 4)):
        for k in range(4):
            here = slice(16 * k, 16 * k + 16)
            held[slot, here, :] = before[f, here, :] + z_update(f, k, low, high)
        copies.append(pltpu.make_async_copy(held.at[slot], out.at[f], sems.at[f]))
        copies[-1].start()
    for copy in copies:
        copy.wait()


def in_vmem(*arrays):
    return tuple(pltpu.with_memory_space_constraint(a, pltpu.VMEM) for a in arrays)


def on_device(slabs, groups, fields, pole_state, pole_decay, pole_gain, surface_resistance, face_owner):
    f32 = jnp.float32
    plan, held_offsets = group_rounds(groups)
    rounds = len(plan)
    held = [(0, 0, 0)]
    for r, (flip, carried) in enumerate(plan):
        held += [(offset ^ flip, r + 1, 32 + 3 * k) for k, offset in enumerate(carried)]
    cross = crossing_pairs(slabs, groups)

    def within(message, flip):
        pairs = [
            (g * groups + p, g * groups + (p ^ flip)) for g in range(slabs) for p in range(groups)
        ]
        return lax.ppermute(message, AXES, pairs)

    owner = face_owner.reshape(1, -1)
    width = fields.shape[-1]
    message = pltpu.VMEM((MESSAGE, width), f32)
    faces_only = pltpu.VMEM((ROWS, width), f32)
    block = pltpu.VMEM(fields.shape, f32)
    first1, first2, own = pl.pallas_call(
        first_kernel,
        out_shape=(message, faces_only, pltpu.VMEM((8, 128), f32)),
        in_specs=[HB] * 4,
        out_specs=[VM] * 3,
        scratch_shapes=[
            pltpu.VMEM((2, 4, 16, width), f32),
            pltpu.VMEM((1, POLES), f32),
            pltpu.VMEM((1, POLES), f32),
            pltpu.VMEM((1, 1), f32),
            pltpu.SemaphoreType.DMA((7,)),
        ],
        name="send_first",
    )(fields, pole_decay, pole_gain, surface_resistance.reshape(1, 1))

    got = [within(first1, plan[0][0])]
    got_cross = lax.ppermute(first2, AXES, cross)
    known = [own[0:3]]
    for r, (flip, carried) in enumerate(plan):
        if r == 0:
            continue
        known = known + [got[r - 1][32 + 3 * k : 35 + 3 * k, 0:128] for k in range(len(known))]
        extra = jnp.concatenate(known, axis=0)
        extra = jnp.pad(extra, ((0, -extra.shape[0] % 8), (0, width - 128)))
        got.append(within(jnp.concatenate([first2, extra], axis=0), flip))

    high, rest = jnp.asarray(WHOLE_HIGH), jnp.asarray(WHOLE_REST)
    fields_v, states_v, high_v, rest_v, owner_v = in_vmem(fields, pole_state, high, rest, owner)
    before, current = pl.pallas_call(
        second_kernel,
        out_shape=(block, pltpu.VMEM((2, 16, 128), f32)),
        in_specs=[VM] * 4,
        out_specs=[VM] * 2,
        scratch_shapes=[pltpu.VMEM((2, 16, 128), f32), pltpu.VMEM((8, 64, 128), f32)],
        name="local_first",
    )(fields_v, states_v, high_v, rest_v)

    got_v = in_vmem(*got, got_cross)
    second1, second2, beyond, drive = pl.pallas_call(
        functools.partial(third_kernel, slabs, groups, held),
        out_shape=(faces_only, faces_only, pltpu.VMEM((64, width), f32), pltpu.VMEM((2, 16, 128), f32)),
        in_specs=[VM] * (5 + rounds),
        out_specs=[VM] * 4,
        name="send_second",
    )(before, current, owner_v, own, *got_v)

    later_cross = lax.ppermute(second2, AXES, cross)
    later = [within(second1 if r == 0 else second2, flip) for r, (flip, _) in enumerate(plan)]

    almost, advanced_states = pl.pallas_call(
        functools.partial(fourth_kernel, held, rounds),
        out_shape=(block, jax.ShapeDtypeStruct(pole_state.shape, f32)),
        in_specs=[VM] * (10 + rounds),
        out_specs=[VM] * 2,
        scratch_shapes=[
            pltpu.VMEM(fields.shape, f32),
            pltpu.VMEM((2, 16, 128), f32),
            pltpu.VMEM((2 * POLES, 128), f32),
            pltpu.VMEM((8, 64, 128), f32),
        ],
        name="local_second",
    )(fields_v, before, current, states_v, beyond, drive, owner_v, own, *got_v[:rounds], high_v, rest_v)

    advanced = pl.pallas_call(
        functools.partial(fifth_kernel, slabs, groups),
        out_shape=jax.ShapeDtypeStruct(fields.shape, f32),
        in_specs=[VM] * (2 + rounds),
        out_specs=HB,
        scratch_shapes=[pltpu.VMEM((4, 64, width), f32), pltpu.SemaphoreType.DMA((6,))],
        name="finish",
    )(almost, *in_vmem(*later, later_cross))
    return advanced, advanced_states


def solution(mesh):
    return jax.shard_map(
        functools.partial(on_device, mesh.shape["slab"], mesh.shape["patch"]),
        mesh=mesh,
        in_specs=(
            P(None, None, ("slab", "patch")),
            P(None, None, None, ("slab", "patch")),
            P(("slab", "patch"), None),
            P(("slab", "patch"), None),
            P(("slab", "patch")),
            P(("slab", "patch"), None),
        ),
        out_specs=(P(None, None, ("slab", "patch")), P(None, None, None, ("slab", "patch"))),
        check_vma=False,
    )
```

time: 56.7 us -> 22.5 us (0.40)
  the two profiles are of different devices: /device:TPU:23 before, /device:TPU:1 now
where the time goes in v1:
time: 22.5 us; the launch traced here: 22.1 us
  local copies, waits for them, and re-layouts  6.88 us (31%)
  Pallas kernels  6.43 us (29%)
  starting transfers between devices  5.69 us (25%)
  waiting for transfers between devices  1.71 us (8%)
  between operations  1.41 us (6%)
    unnamed x22, local copies, waits for them, and re-layouts  6.87 us
    ppermute x4, starting transfers between devices, within(): return lax.ppermute(message, AXES, pairs)  3.27 us
    ppermute x1, starting transfers between devices, on_device(): later_cross = lax.ppermute(second2, AXES, cross)  2.35 us
    pallas_call x1, Pallas kernels, on_device(): pl.pallas_call(functools.partial(fourth_kernel, held, rounds), out_shape=...  2 us
    pallas_call x1, Pallas kernels, on_device(): pl.pallas_call(functools.partial(fifth_kernel, slabs, groups), out_shape=...  1.78 us
    ppermute x4, waiting for transfers between devices, within(): return lax.ppermute(message, AXES, pairs)  1.71 us
    pallas_call x1, Pallas kernels, on_device(): pl.pallas_call(functools.partial(third_kernel, slabs, groups, held), out_...  1.18 us
    pallas_call x1, Pallas kernels, on_device(): pl.pallas_call(first_kernel, out_shape=(message, faces_only, pltpu.VMEM((...  0.89 us
  transfers between devices with their start and end apart: 6, of which 2 were waited for; matrix products, arithmetic and copies ran while one was open for 0% of the time, Pallas kernels for 12%

profile of v1, /device:TPU:1, one launch (start us, length us, event | category | flops | bytes accessed | tf_op | source)
XLA Modules:
  0.0 22.1 jit_solution(1392598856625932399)
XLA Ops:
  0.6 0.0 copy-start
  1.3 0.9 %send_first.1 = (f32[40,256]{1,0:T(8,128)S(1)}, f32[32,256]{1,0:T(8,128)S(1)}, f32[8,128]{1,0:T(8,128)S(1)}) custom-call(f32[6,64,256]{2,1,0:T(8,128)} %refs_0_.1, f32[1,12]{1,0:T(1,128)} %decay.1, f32[1,12]{1,0:T(1,128)} %gain.1, f32[1,1]{1,0:T(1,128)} %bitcast.2.resist), custom_call_target="tpu_custom_call" | custom-call | tf_op jit(solution)/shard_map/send_first/pallas_call | solution.py:422
  2.2 0.0 copy-start.8
  2.2 0.1 collective-permute-start
  2.4 1.2 %collective-permute-done.refs_4_.refs_8_ = f32[40,256]{1,0:T(8,128)S(1)} collective-permute-done((f32[40,256]{1,0:T(8,128)S(1)}, f32[40,256]{1,0:T(8,128)S(1)}, u32[]{:S(2)}, u32[]{:S(2)}) %collective-permute-start) | collective-permute-done | bytes 40992 | tf_op jit(solution)/shard_map/ppermute | solution.py:415
  3.5 0.0 copy-done.8
  3.6 2.7 %collective-permute-start.1 = (f32[40,256]{1,0:T(8,128)S(1)}, f32[40,256]{1,0:T(8,128)S(1)}, u32[]{:S(2)}, u32[]{:S(2)}) collective-permute-start(f32[40,256]{1,0:T(8,128)S(1)} %pad_maximum_fusion), channel_id=1, source_target_pairs={{0,3},{1,2},{2,1},{3,0},{4,7},{5,6},{6,5},{7,4},{8,11},{9,10},{10,... | collective-permute-start | bytes 122888 | tf_op jit(solution)/shard_map/ppermute | solution.py:415
  6.2 0.1 collective-permute-start.2
  6.3 0.0 copy-done
  6.3 0.0 copy-start.2
  6.3 1.0 %copy-done.2 = bf16[384,512]{1,0:T(8,128)(2,1)S(1)} copy-done((bf16[384,512]{1,0:T(8,128)(2,1)S(1)}, bf16[384,512]{1,0:T(8,128)(2,1)}, u32[]{:S(2)}) %copy-start.2) | copy-done | bytes 393240
  7.3 0.0 copy-start.3
  7.3 1.0 %copy-done.3 = bf16[384,512]{1,0:T(8,128)(2,1)S(1)} copy-done((bf16[384,512]{1,0:T(8,128)(2,1)S(1)}, bf16[384,512]{1,0:T(8,128)(2,1)}, u32[]{:S(2)}) %copy-start.3) | copy-done | bytes 393240
  8.3 0.0 copy-start.4
  8.3 0.9 %copy-done.4 = f32[12,2,16,16]{3,2,1,0:T(8,128)S(1)} copy-done((f32[12,2,16,16]{3,2,1,0:T(8,128)S(1)}, f32[12,2,16,16]{3,2,1,0:T(8,128)}, u32[]{:S(2)}) %copy-start.4) | copy-done | bytes 24600
  9.2 0.6 %local_first.1 = (f32[6,64,256]{2,1,0:T(8,128)S(1)}, f32[2,16,128]{2,1,0:T(8,128)S(1)}) custom-call(f32[6,64,256]{2,1,0:T(8,128)S(1)} %copy-done, f32[12,2,16,16]{3,2,1,0:T(8,128)S(1)} %copy-done.4, bf16[384,512]{1,0:T(8,128)(2,1)S(1)} %copy-done.3, bf16[384,512]{1,0:T(8,128)(2,1)S(1)} %copy-done.2), custom_call_target="tpu_custom_call" | custom-call | tf_op jit(solution)/shard_map/local_first/pallas_call | solution.py:450
  9.8 0.0 copy-start.1
  9.8 0.7 %copy-done.1 = f32[6,64,256]{2,1,0:T(8,128)} copy-done((f32[6,64,256]{2,1,0:T(8,128)}, f32[6,64,256]{2,1,0:T(8,128)S(1)}, u32[]{:S(2)}) %copy-start.1) | copy-done | bytes 393240
  10.5 0.0 copy-start.6
  10.5 0.6 %copy-done.6 = f32[2,16,128]{2,1,0:T(8,128)} copy-done((f32[2,16,128]{2,1,0:T(8,128)}, f32[2,16,128]{2,1,0:T(8,128)S(1)}, u32[]{:S(2)}) %copy-start.6) | copy-done | bytes 16408
  11.1 0.0 collective-permute-done.2.refs_6_
  11.1 0.0 collective-permute-done.1.refs_5_.refs_9_
  11.1 0.0 copy-start.10
  11.2 0.7 %copy-done.10 = s32[16,1]{0,1:T(1,128)S(1)} copy-done((s32[16,1]{0,1:T(1,128)S(1)}, s32[16,1]{0,1:T(1,128)}, u32[]{:S(2)}) %copy-start.10) | copy-done | bytes 88
  11.8 1.2 %send_second.1 = (f32[32,256]{1,0:T(8,128)S(1)}, f32[32,256]{1,0:T(8,128)S(1)}, f32[64,256]{1,0:T(8,128)S(1)}, f32[2,16,128]{2,1,0:T(8,128)S(1)}) custom-call(f32[6,64,256]{2,1,0:T(8,128)} %copy-done.1, f32[2,16,128]{2,1,0:T(8,128)} %copy-done.6, s32[1,16]{1,0:T(1,128)S(1)} %bitcast.3, f32[8,128]{1,0:T(8,128)} %copy-done.8, ...), custom_call_target="tpu_custom_call" | custom-call | tf_op jit(solution)/shard_map/send_second/pallas_call | solution.py:460
  13.0 0.0 copy-start.7
  13.0 0.6 %copy-done.7 = f32[64,256]{1,0:T(8,128)} copy-done((f32[64,256]{1,0:T(8,128)}, f32[64,256]{1,0:T(8,128)S(1)}, u32[]{:S(2)}) %copy-start.7) | copy-done | bytes 65560
  13.6 0.0 copy-start.9
  13.6 0.6 %copy-done.9 = f32[2,16,128]{2,1,0:T(8,128)} copy-done((f32[2,16,128]{2,1,0:T(8,128)}, f32[2,16,128]{2,1,0:T(8,128)S(1)}, u32[]{:S(2)}) %copy-start.9) | copy-done | bytes 16408
  14.2 0.4 %collective-permute-start.3 = (f32[32,256]{1,0:T(8,128)S(1)}, f32[32,256]{1,0:T(8,128)S(1)}, u32[]{:S(2)}, u32[]{:S(2)}) collective-permute-start(f32[32,256]{1,0:T(8,128)S(1)} %get-tuple-element.21), channel_id=1, source_target_pairs={{0,1},{1,0},{2,3},{3,2},{4,5},{5,4},{6,7},{7,6},{8,9},{9,8},{10,11... | collective-permute-start | bytes 98312 | tf_op jit(solution)/shard_map/ppermute | solution.py:415
  14.6 2.4 %collective-permute-start.5 = (f32[32,256]{1,0:T(8,128)S(1)}, f32[32,256]{1,0:T(8,128)S(1)}, u32[]{:S(2)}, u32[]{:S(2)}) collective-permute-start(f32[32,256]{1,0:T(8,128)S(1)} %get-tuple-element.22), channel_id=1, source_target_pairs={{3,4},{4,3},{0,1},{1,2},{2,0},{7,8},{8,7},{5,6},{6,5},{11,12},{12,... | collective-permute-start | bytes 98312 | tf_op jit(solution)/shard_map/ppermute | solution.py:468
  17.0 0.0 collective-permute-start.4
  17.0 2.0 %local_second.1 = (f32[6,64,256]{2,1,0:T(8,128)S(1)}, f32[12,2,16,16]{3,2,1,0:T(8,128)}) custom-call(f32[6,64,256]{2,1,0:T(8,128)S(1)} %copy-done, f32[6,64,256]{2,1,0:T(8,128)} %copy-done.1, f32[2,16,128]{2,1,0:T(8,128)} %copy-done.6, f32[12,2,16,16]{3,2,1,0:T(8,128)S(1)} %copy-done.4, f32[64,256]{1,0:T(8,128)} %copy-done.7, f32[2,16,128]{2,1,0:T(8,128)} %copy-done.9, ...), custom_call_target="tpu_custom_call" | custom-call | tf_op jit(solution)/shard_map/local_second/pallas_call | solution.py:471
  19.0 0.0 copy-start.5
  19.0 0.8 %copy-done.5 = f32[6,64,256]{2,1,0:T(8,128)} copy-done((f32[6,64,256]{2,1,0:T(8,128)}, f32[6,64,256]{2,1,0:T(8,128)S(1)}, u32[]{:S(2)}) %copy-start.5) | copy-done | bytes 393240
  19.8 0.0 collective-permute-done.3.refs_1_
  19.8 0.0 collective-permute-done.5.refs_3_
  19.8 0.5 %collective-permute-done.4.refs_2_ = f32[32,256]{1,0:T(8,128)S(1)} collective-permute-done((f32[32,256]{1,0:T(8,128)S(1)}, f32[32,256]{1,0:T(8,128)S(1)}, u32[]{:S(2)}, u32[]{:S(2)}) %collective-permute-start.4) | collective-permute-done | bytes 32800 | tf_op jit(solution)/shard_map/ppermute | solution.py:415
  20.3 1.8 %finish.1 = f32[6,64,256]{2,1,0:T(8,128)} custom-call(f32[6,64,256]{2,1,0:T(8,128)} %copy-done.5, f32[32,256]{1,0:T(8,128)S(1)} %collective-permute-done.3.refs_1_, f32[32,256]{1,0:T(8,128)S(1)} %collective-permute-done.4.refs_2_, f32[32,256]{1,0:T(8,128)S(1)} %collective-permute-done.5.refs_3_), custom_call_target="tpu_custom_call" | custom-call | tf_op jit(solution)/shard_map/finish/pallas_call | solution.py:485
  (4 shorter events, 0.0 us)
Async XLA Ops:
  0.6 5.7 %copy-start = (f32[6,64,256]{2,1,0:T(8,128)S(1)}, f32[6,64,256]{2,1,0:T(8,128)}, u32[]{:S(2)}) copy-start(f32[6,64,256]{2,1,0:T(8,128)} %refs_0_.1) | copy-start | bytes 1179652
  2.2 1.3 %copy-start.8 = (f32[8,128]{1,0:T(8,128)}, f32[8,128]{1,0:T(8,128)S(1)}, u32[]{:S(2)}) copy-start(f32[8,128]{1,0:T(8,128)S(1)} %get-tuple-element.15.refs_3_.refs_7_) | copy-start | bytes 12292
  2.2 1.3 %collective-permute-start = (f32[40,256]{1,0:T(8,128)S(1)}, f32[40,256]{1,0:T(8,128)S(1)}, u32[]{:S(2)}, u32[]{:S(2)}) collective-permute-start(f32[40,256]{1,0:T(8,128)S(1)} %get-tuple-element.16), channel_id=1, source_target_pairs={{0,1},{1,0},{2,3},{3,2},{4,5},{5,4},{6,7},{7,6},{8,9},{9,8},{10,11... | collective-permute-start | bytes 122888 | tf_op jit(solution)/shard_map/ppermute | solution.py:415
  3.6 7.6 %collective-permute-start.1 = (f32[40,256]{1,0:T(8,128)S(1)}, f32[40,256]{1,0:T(8,128)S(1)}, u32[]{:S(2)}, u32[]{:S(2)}) collective-permute-start(f32[40,256]{1,0:T(8,128)S(1)} %pad_maximum_fusion), channel_id=1, source_target_pairs={{0,3},{1,2},{2,1},{3,0},{4,7},{5,6},{6,5},{7,4},{8,11},{9,10},{10,... | collective-permute-start | bytes 122888 | tf_op jit(solution)/shard_map/ppermute | solution.py:415
  6.2 4.9 %collective-permute-start.2 = (f32[32,256]{1,0:T(8,128)S(1)}, f32[32,256]{1,0:T(8,128)S(1)}, u32[]{:S(2)}, u32[]{:S(2)}) collective-permute-start(f32[32,256]{1,0:T(8,128)S(1)} %get-tuple-element.17), channel_id=1, source_target_pairs={{3,4},{4,3},{0,1},{1,2},{2,0},{7,8},{8,7},{5,6},{6,5},{11,12},{12,... | collective-permute-start | bytes 98312 | tf_op jit(solution)/shard_map/ppermute | solution.py:438
  6.3 1.0 %copy-start.2 = (bf16[384,512]{1,0:T(8,128)(2,1)S(1)}, bf16[384,512]{1,0:T(8,128)(2,1)}, u32[]{:S(2)}) copy-start(bf16[384,512]{1,0:T(8,128)(2,1)} %constant.8.clone.rest_ref.refs_11_) | copy-start | bytes 1179652
  7.3 1.0 %copy-start.3 = (bf16[384,512]{1,0:T(8,128)(2,1)S(1)}, bf16[384,512]{1,0:T(8,128)(2,1)}, u32[]{:S(2)}) copy-start(bf16[384,512]{1,0:T(8,128)(2,1)} %constant.7.clone.high_ref.refs_10_) | copy-start | bytes 1179652
  8.3 0.9 %copy-start.4 = (f32[12,2,16,16]{3,2,1,0:T(8,128)S(1)}, f32[12,2,16,16]{3,2,1,0:T(8,128)}, u32[]{:S(2)}) copy-start(f32[12,2,16,16]{3,2,1,0:T(8,128)} %refs_3_.1) | copy-start | bytes 73732
  9.8 0.7 %copy-start.1 = (f32[6,64,256]{2,1,0:T(8,128)}, f32[6,64,256]{2,1,0:T(8,128)S(1)}, u32[]{:S(2)}) copy-start(f32[6,64,256]{2,1,0:T(8,128)S(1)} %get-tuple-element.13.refs_0_.refs_1_) | copy-start | bytes 1179652
  10.5 0.6 %copy-start.6 = (f32[2,16,128]{2,1,0:T(8,128)}, f32[2,16,128]{2,1,0:T(8,128)S(1)}, u32[]{:S(2)}) copy-start(f32[2,16,128]{2,1,0:T(8,128)S(1)} %get-tuple-element.14.refs_1_.refs_2_) | copy-start | bytes 49156
  11.1 0.7 %copy-start.10 = (s32[16,1]{0,1:T(1,128)S(1)}, s32[16,1]{0,1:T(1,128)}, u32[]{:S(2)}) copy-start(s32[16,1]{0,1:T(1,128)} %param.13) | copy-start | bytes 196
  13.0 0.6 %copy-start.7 = (f32[64,256]{1,0:T(8,128)}, f32[64,256]{1,0:T(8,128)S(1)}, u32[]{:S(2)}) copy-start(f32[64,256]{1,0:T(8,128)S(1)} %get-tuple-element.18.refs_4_) | copy-start | bytes 196612
  13.6 0.6 %copy-start.9 = (f32[2,16,128]{2,1,0:T(8,128)}, f32[2,16,128]{2,1,0:T(8,128)S(1)}, u32[]{:S(2)}) copy-start(f32[2,16,128]{2,1,0:T(8,128)S(1)} %get-tuple-element.19.refs_5_) | copy-start | bytes 49156
  14.2 5.6 %collective-permute-start.3 = (f32[32,256]{1,0:T(8,128)S(1)}, f32[32,256]{1,0:T(8,128)S(1)}, u32[]{:S(2)}, u32[]{:S(2)}) collective-permute-start(f32[32,256]{1,0:T(8,128)S(1)} %get-tuple-element.21), channel_id=1, source_target_pairs={{0,1},{1,0},{2,3},{3,2},{4,5},{5,4},{6,7},{7,6},{8,9},{9,8},{10,11... | collective-permute-start | bytes 98312 | tf_op jit(solution)/shard_map/ppermute | solution.py:415
  14.6 5.2 %collective-permute-start.5 = (f32[32,256]{1,0:T(8,128)S(1)}, f32[32,256]{1,0:T(8,128)S(1)}, u32[]{:S(2)}, u32[]{:S(2)}) collective-permute-start(f32[32,256]{1,0:T(8,128)S(1)} %get-tuple-element.22), channel_id=1, source_target_pairs={{3,4},{4,3},{0,1},{1,2},{2,0},{7,8},{8,7},{5,6},{6,5},{11,12},{12,... | collective-permute-start | bytes 98312 | tf_op jit(solution)/shard_map/ppermute | solution.py:468
  17.0 3.3 %collective-permute-start.4 = (f32[32,256]{1,0:T(8,128)S(1)}, f32[32,256]{1,0:T(8,128)S(1)}, u32[]{:S(2)}, u32[]{:S(2)}) collective-permute-start(f32[32,256]{1,0:T(8,128)S(1)} %get-tuple-element.22), channel_id=1, source_target_pairs={{0,3},{1,2},{2,1},{3,0},{4,7},{5,6},{6,5},{7,4},{8,11},{9,10},{10,... | collective-permute-start | bytes 98312 | tf_op jit(solution)/shard_map/ppermute | solution.py:415
  19.0 0.8 %copy-start.5 = (f32[6,64,256]{2,1,0:T(8,128)}, f32[6,64,256]{2,1,0:T(8,128)S(1)}, u32[]{:S(2)}) copy-start(f32[6,64,256]{2,1,0:T(8,128)S(1)} %get-tuple-element.20.refs_0_) | copy-start | bytes 1179652

commit v2 on v1

--- a/solution.py
+++ b/solution.py
@@ -144,7 +144,9 @@
         out2_ref[here, :] = jnp.where(even, down[which], up[which])
 
 
-def first_kernel(fields, decay, gain, resist, out1, out2, own, faces, decays, gains, resists, sems):
+def first_kernel(
+    fields, decay, gain, resist, owner, out1, out2, own, names, faces, decays, gains, resists, sems
+):
     copies = [
         pltpu.make_async_copy(fields.at[0:2, 48:64], faces.at[0, 0:2], sems.at[0]),
         pltpu.make_async_copy(fields.at[3:5, 48:64], faces.at[0, 2:4], sems.at[1]),
@@ -153,6 +155,7 @@
         pltpu.make_async_copy(decay, decays, sems.at[4]),
         pltpu.make_async_copy(gain, gains, sems.at[5]),
         pltpu.make_async_copy(resist, resists, sems.at[6]),
+        pltpu.make_async_copy(owner, names, sems.at[7]),
     ]
     for copy in copies:
         copy.start()
@@ -164,8 +167,9 @@
     down = (ex - hy, ey + hx)
     to_message(out1, out2, up, down)
     own[...] = jnp.zeros_like(own)
-    for which, ref in enumerate((decays, gains, resists)):
-        own[which : which + 1, 0 : ref.shape[1]] = ref[...]
+    own[0:1, 0:POLES] = decays[...]
+    own[1:2, 0:POLES] = gains[...]
+    own[2:3, :] = jnp.full((1, 128), resists[0], jnp.float32)
     out1[32:40, 0:128] = own[...]
 
 
@@ -209,10 +213,12 @@
     return jnp.concatenate(parts, axis=0)
 
 
-def update(ref, halves, voltage, high_ref, rest_ref):
+def update(ref, halves, voltage, high_ref, rest_ref, copies=()):
     stacked = jnp.concatenate([ref[f] for f in range(6)] + [exteriors(ref, halves, voltage)], axis=0)
     high = stacked.astype(jnp.bfloat16)
     rest = (stacked - high.astype(jnp.float32)).astype(jnp.bfloat16)
+    for copy in copies:
+        copy.wait()
     dot = functools.partial(jnp.dot, preferred_element_type=jnp.float32)
     return dot(high_ref[...], high) + (dot(high_ref[...], rest) + dot(rest_ref[...], high))
 
@@ -225,7 +231,16 @@
     return found
 
 
-def second_kernel(fields, states, high_ref, rest_ref, out, current, sums, halves):
+def second_kernel(
+    fields, states_h, high_h, rest_h, out, current, states, high_ref, rest_ref, sums, halves, sems
+):
+    copies = [
+        pltpu.make_async_copy(source, goal, sems.at[k])
+        for k, (source, goal) in enumerate(((states_h, states), (high_h, high_ref), (rest_h, rest_ref)))
+    ]
+    for copy in copies:
+        copy.start()
+    copies[0].wait()
     sums[...] = jnp.zeros_like(sums)
     for part in range(2):
         total = states[0, part]
@@ -233,7 +248,7 @@
             total = total + states[pole, part]
         sums[part, :, 0:EX] = total
     voltage = [pltpu.roll(sums[part], 128 - EX, 1) for part in range(2)]
-    result = update(fields, halves, voltage, high_ref, rest_ref)
+    result = update(fields, halves, voltage, high_ref, rest_ref, copies[1:])
     for f in range(6):
         out[f] = fields[f] + result[64 * f : 64 * f + 64]
     for part, value in enumerate(currents(fields)):
@@ -419,20 +434,20 @@
     message = pltpu.VMEM((MESSAGE, width), f32)
     faces_only = pltpu.VMEM((ROWS, width), f32)
     block = pltpu.VMEM(fields.shape, f32)
-    first1, first2, own = pl.pallas_call(
+    first1, first2, own, names = pl.pallas_call(
         first_kernel,
-        out_shape=(message, faces_only, pltpu.VMEM((8, 128), f32)),
-        in_specs=[HB] * 4,
-        out_specs=[VM] * 3,
+        out_shape=(message, faces_only, pltpu.VMEM((8, 128), f32), pltpu.VMEM(owner.shape, owner.dtype)),
+        in_specs=[HB] * 5,
+        out_specs=[VM] * 4,
         scratch_shapes=[
             pltpu.VMEM((2, 4, 16, width), f32),
             pltpu.VMEM((1, POLES), f32),
             pltpu.VMEM((1, POLES), f32),
-            pltpu.VMEM((1, 1), f32),
-            pltpu.SemaphoreType.DMA((7,)),
+            pltpu.SMEM((1,), f32),
+            pltpu.SemaphoreType.DMA((8,)),
         ],
         name="send_first",
-    )(fields, pole_decay, pole_gain, surface_resistance.reshape(1, 1))
+    )(fields, pole_decay, pole_gain, surface_resistance, owner)
 
     got = [within(first1, plan[0][0])]
     got_cross = lax.ppermute(first2, AXES, cross)
@@ -445,16 +460,22 @@
         extra = jnp.pad(extra, ((0, -extra.shape[0] % 8), (0, width - 128)))
         got.append(within(jnp.concatenate([first2, extra], axis=0), flip))
 
-    high, rest = jnp.asarray(WHOLE_HIGH), jnp.asarray(WHOLE_REST)
-    fields_v, states_v, high_v, rest_v, owner_v = in_vmem(fields, pole_state, high, rest, owner)
-    before, current = pl.pallas_call(
+    fields_v = pltpu.with_memory_space_constraint(fields, pltpu.VMEM)
+    table = pltpu.VMEM(WHOLE.shape, jnp.bfloat16)
+    local = pl.pallas_call(
         second_kernel,
-        out_shape=(block, pltpu.VMEM((2, 16, 128), f32)),
-        in_specs=[VM] * 4,
-        out_specs=[VM] * 2,
-        scratch_shapes=[pltpu.VMEM((2, 16, 128), f32), pltpu.VMEM((8, 64, 128), f32)],
+        out_shape=(block, pltpu.VMEM((2, 16, 128), f32), pltpu.VMEM(pole_state.shape, f32), table, table),
+        in_specs=[VM] + [HB] * 3,
+        out_specs=[VM] * 5,
+        scratch_shapes=[
+            pltpu.VMEM((2, 16, 128), f32),
+            pltpu.VMEM((8, 64, 128), f32),
+            pltpu.SemaphoreType.DMA((3,)),
+        ],
         name="local_first",
-    )(fields_v, states_v, high_v, rest_v)
+    )(fields_v, pole_state, jnp.asarray(WHOLE_HIGH), jnp.asarray(WHOLE_REST))
+    before, current, states_v, high_v, rest_v = in_vmem(*local)
+    own_v, owner_v = in_vmem(own, names)
 
     got_v = in_vmem(*got, got_cross)
     second1, second2, beyond, drive = pl.pallas_call(
@@ -463,7 +484,7 @@
         in_specs=[VM] * (5 + rounds),
         out_specs=[VM] * 4,
         name="send_second",
-    )(before, current, owner_v, own, *got_v)
+    )(before, current, owner_v, own_v, *got_v)
 
     later_cross = lax.ppermute(second2, AXES, cross)
     later = [within(second1 if r == 0 else second2, flip) for r, (flip, _) in enumerate(plan)]
@@ -480,7 +501,9 @@
             pltpu.VMEM((8, 64, 128), f32),
         ],
         name="local_second",
-    )(fields_v, before, current, states_v, beyond, drive, owner_v, own, *got_v[:rounds], high_v, rest_v)
+    )(
+        fields_v, before, current, states_v, *in_vmem(beyond, drive), owner_v, own_v, *got_v[:rounds], high_v, rest_v
+    )
 
     advanced = pl.pallas_call(
         functools.partial(fifth_kernel, slabs, groups),
@@ -489,7 +512,7 @@
         out_specs=HB,
         scratch_shapes=[pltpu.VMEM((4, 64, width), f32), pltpu.SemaphoreType.DMA((6,))],
         name="finish",
-    )(almost, *in_vmem(*later, later_cross))
+    )(*in_vmem(almost, *later, later_cross))
     return advanced, advanced_states
 
 

time: 22.5 us -> 16.6 us (0.74)
  the two profiles are of different devices: /device:TPU:1 before, /device:TPU:0 now
where the time goes in v2:
time: 16.6 us; the launch traced here: 16.4 us
  starting transfers between devices  6.68 us (40%)
  Pallas kernels  4.53 us (27%)
  waiting for transfers between devices  3.83 us (23%)
  between operations  1.37 us (8%)
    ppermute x4, starting transfers between devices, within(): return lax.ppermute(message, AXES, pairs)  5.83 us
    ppermute x4, waiting for transfers between devices, within(): return lax.ppermute(message, AXES, pairs)  1.99 us
    ppermute x1, waiting for transfers between devices, on_device(): got_cross = lax.ppermute(first2, AXES, cross)  1.84 us
    pallas_call x1, Pallas kernels, on_device(): pl.pallas_call(second_kernel, out_shape=(block, pltpu.VMEM((2, 16, 128),...  1.72 us
    pallas_call x1, Pallas kernels, on_device(): pl.pallas_call(functools.partial(fourth_kernel, held, rounds), out_shape=...  0.96 us
    pallas_call x1, Pallas kernels, on_device(): pl.pallas_call(first_kernel, out_shape=(message, faces_only, pltpu.VMEM((...  0.91 us
    pallas_call x1, Pallas kernels, on_device(): pl.pallas_call(functools.partial(fifth_kernel, slabs, groups), out_shape=...  0.79 us
    ppermute x1, starting transfers between devices, on_device(): later_cross = lax.ppermute(second2, AXES, cross)  0.5 us
  transfers between devices with their start and end apart: 6, of which 3 were waited for; matrix products, arithmetic and copies ran while one was open for 0% of the time, Pallas kernels for 16%

profile of v2, /device:TPU:0, one launch (start us, length us, event | category | flops | bytes accessed | tf_op | source)
XLA Modules:
  0.0 16.4 jit_solution(10831984381218387311)
XLA Ops:
  0.6 0.0 copy-start
  1.3 0.9 %send_first.1 = (f32[40,256]{1,0:T(8,128)S(1)}, f32[32,256]{1,0:T(8,128)S(1)}, f32[8,128]{1,0:T(8,128)S(1)}, s32[1,16]{1,0:T(1,128)S(1)}) custom-call(f32[6,64,256]{2,1,0:T(8,128)} %refs_0_.1, f32[1,12]{1,0:T(1,128)} %decay.1, f32[1,12]{1,0:T(1,128)} %gain.1, f32[1]{0:T(128)S(6)} %copy.10.resist, s32[1,16]{1,0:T(1,128)} %bitcast.1), custom_call_target="tpu_custom_call" | custom-call | tf_op jit(solution)/shard_map/send_first/pallas_call | solution.py:437
  2.3 0.5 %collective-permute-start = (f32[40,256]{1,0:T(8,128)S(1)}, f32[40,256]{1,0:T(8,128)S(1)}, u32[]{:S(2)}, u32[]{:S(2)}) collective-permute-start(f32[40,256]{1,0:T(8,128)S(1)} %get-tuple-element.22), channel_id=1, source_target_pairs={{0,1},{1,0},{2,3},{3,2},{4,5},{5,4},{6,7},{7,6},{8,9},{9,8},{10,11... | collective-permute-start | bytes 122888 | tf_op jit(solution)/shard_map/ppermute | solution.py:430
  2.8 0.9 %collective-permute-done.refs_4_.refs_8_ = f32[40,256]{1,0:T(8,128)S(1)} collective-permute-done((f32[40,256]{1,0:T(8,128)S(1)}, f32[40,256]{1,0:T(8,128)S(1)}, u32[]{:S(2)}, u32[]{:S(2)}) %collective-permute-start) | collective-permute-done | bytes 40992 | tf_op jit(solution)/shard_map/ppermute | solution.py:430
  3.7 2.7 %collective-permute-start.1 = (f32[40,256]{1,0:T(8,128)S(1)}, f32[40,256]{1,0:T(8,128)S(1)}, u32[]{:S(2)}, u32[]{:S(2)}) collective-permute-start(f32[40,256]{1,0:T(8,128)S(1)} %pad_maximum_fusion), channel_id=1, source_target_pairs={{0,3},{1,2},{2,1},{3,0},{4,7},{5,6},{6,5},{7,4},{8,11},{9,10},{10,... | collective-permute-start | bytes 122888 | tf_op jit(solution)/shard_map/ppermute | solution.py:430
  6.3 0.3 %collective-permute-start.2 = (f32[32,256]{1,0:T(8,128)S(1)}, f32[32,256]{1,0:T(8,128)S(1)}, u32[]{:S(2)}, u32[]{:S(2)}) collective-permute-start(f32[32,256]{1,0:T(8,128)S(1)} %get-tuple-element.23), channel_id=1, source_target_pairs={{3,4},{4,3},{0,1},{1,2},{2,0},{7,8},{8,7},{5,6},{6,5},{11,12},{12,... | collective-permute-start | bytes 98312 | tf_op jit(solution)/shard_map/ppermute | solution.py:453
  6.7 0.0 copy-done
  6.7 1.7 %local_first.1 = (f32[6,64,256]{2,1,0:T(8,128)S(1)}, f32[2,16,128]{2,1,0:T(8,128)S(1)}, f32[12,2,16,16]{3,2,1,0:T(8,128)S(1)}, bf16[384,512]{1,0:T(8,128)(2,1)S(1)}, bf16[384,512]{1,0:T(8,128)(2,1)S(1)}) custom-call(f32[6,64,256]{2,1,0:T(8,128)S(1)} %copy-done, f32[12,2,16,16]{3,2,1,0:T(8,128)} %states_h.1, bf16[384,512]{1,0:T(8,128)(2,1)} %constant.7.clone.high_h, ...), custom_call_target="tpu_custom_call" | custom-call | tf_op jit(solution)/shard_map/local_first/pallas_call | solution.py:465
  8.4 1.8 %collective-permute-done.2.refs_6_ = f32[32,256]{1,0:T(8,128)S(1)} collective-permute-done((f32[32,256]{1,0:T(8,128)S(1)}, f32[32,256]{1,0:T(8,128)S(1)}, u32[]{:S(2)}, u32[]{:S(2)}) %collective-permute-start.2) | collective-permute-done | bytes 32800 | tf_op jit(solution)/shard_map/ppermute | solution.py:453
  10.2 0.0 collective-permute-done.1.refs_5_.refs_9_
  10.3 0.2 send_second.1
  10.4 0.1 collective-permute-start.3
  10.5 0.5 %collective-permute-start.5 = (f32[32,256]{1,0:T(8,128)S(1)}, f32[32,256]{1,0:T(8,128)S(1)}, u32[]{:S(2)}, u32[]{:S(2)}) collective-permute-start(f32[32,256]{1,0:T(8,128)S(1)} %get-tuple-element.30), channel_id=1, source_target_pairs={{3,4},{4,3},{0,1},{1,2},{2,0},{7,8},{8,7},{5,6},{6,5},{11,12},{12,... | collective-permute-start | bytes 98312 | tf_op jit(solution)/shard_map/ppermute | solution.py:489
  11.0 2.6 %collective-permute-start.4 = (f32[32,256]{1,0:T(8,128)S(1)}, f32[32,256]{1,0:T(8,128)S(1)}, u32[]{:S(2)}, u32[]{:S(2)}) collective-permute-start(f32[32,256]{1,0:T(8,128)S(1)} %get-tuple-element.30), channel_id=1, source_target_pairs={{0,3},{1,2},{2,1},{3,0},{4,7},{5,6},{6,5},{7,4},{8,11},{9,10},{10,... | collective-permute-start | bytes 98312 | tf_op jit(solution)/shard_map/ppermute | solution.py:430
  13.6 1.0 %local_second.1 = (f32[6,64,256]{2,1,0:T(8,128)S(1)}, f32[12,2,16,16]{3,2,1,0:T(8,128)}) custom-call(f32[6,64,256]{2,1,0:T(8,128)S(1)} %copy-done, f32[6,64,256]{2,1,0:T(8,128)S(1)} %get-tuple-element.17.refs_0_.refs_1_, f32[2,16,128]{2,1,0:T(8,128)S(1)} %get-tuple-element.18.refs_1_.refs_2_, f32[12,2,16,16]{3,2,1,0:T(8,128)S(1)} %get-tuple-element.19.refs_3_, ...), custom_call_target="tpu_custom_call" | custom-call | tf_op jit(solution)/shard_map/local_second/pallas_call | solution.py:492
  14.5 0.0 collective-permute-done.3.refs_1_
  14.5 0.0 collective-permute-done.5.refs_3_
  14.5 1.1 %collective-permute-done.4.refs_2_ = f32[32,256]{1,0:T(8,128)S(1)} collective-permute-done((f32[32,256]{1,0:T(8,128)S(1)}, f32[32,256]{1,0:T(8,128)S(1)}, u32[]{:S(2)}, u32[]{:S(2)}) %collective-permute-start.4) | collective-permute-done | bytes 32800 | tf_op jit(solution)/shard_map/ppermute | solution.py:430
  15.6 0.8 %finish.1 = f32[6,64,256]{2,1,0:T(8,128)} custom-call(f32[6,64,256]{2,1,0:T(8,128)S(1)} %get-tuple-element.28.refs_0_, f32[32,256]{1,0:T(8,128)S(1)} %collective-permute-done.3.refs_1_, f32[32,256]{1,0:T(8,128)S(1)} %collective-permute-done.4.refs_2_, f32[32,256]{1,0:T(8,128)S(1)} %collective-permute-done.5.refs_3_), custom_call_target="tpu_custom_call" | custom-call | tf_op jit(solution)/shard_map/finish/pallas_call | solution.py:508
  (4 shorter events, 0.0 us)
Async XLA Ops:
  0.6 6.1 %copy-start = (f32[6,64,256]{2,1,0:T(8,128)S(1)}, f32[6,64,256]{2,1,0:T(8,128)}, u32[]{:S(2)}) copy-start(f32[6,64,256]{2,1,0:T(8,128)} %refs_0_.1) | copy-start | bytes 1179652
  2.3 1.4 %collective-permute-start = (f32[40,256]{1,0:T(8,128)S(1)}, f32[40,256]{1,0:T(8,128)S(1)}, u32[]{:S(2)}, u32[]{:S(2)}) collective-permute-start(f32[40,256]{1,0:T(8,128)S(1)} %get-tuple-element.22), channel_id=1, source_target_pairs={{0,1},{1,0},{2,3},{3,2},{4,5},{5,4},{6,7},{7,6},{8,9},{9,8},{10,11... | collective-permute-start | bytes 122888 | tf_op jit(solution)/shard_map/ppermute | solution.py:430
  3.7 6.6 %collective-permute-start.1 = (f32[40,256]{1,0:T(8,128)S(1)}, f32[40,256]{1,0:T(8,128)S(1)}, u32[]{:S(2)}, u32[]{:S(2)}) collective-permute-start(f32[40,256]{1,0:T(8,128)S(1)} %pad_maximum_fusion), channel_id=1, source_target_pairs={{0,3},{1,2},{2,1},{3,0},{4,7},{5,6},{6,5},{7,4},{8,11},{9,10},{10,... | collective-permute-start | bytes 122888 | tf_op jit(solution)/shard_map/ppermute | solution.py:430
  6.3 3.9 %collective-permute-start.2 = (f32[32,256]{1,0:T(8,128)S(1)}, f32[32,256]{1,0:T(8,128)S(1)}, u32[]{:S(2)}, u32[]{:S(2)}) collective-permute-start(f32[32,256]{1,0:T(8,128)S(1)} %get-tuple-element.23), channel_id=1, source_target_pairs={{3,4},{4,3},{0,1},{1,2},{2,0},{7,8},{8,7},{5,6},{6,5},{11,12},{12,... | collective-permute-start | bytes 98312 | tf_op jit(solution)/shard_map/ppermute | solution.py:453
  10.4 4.1 %collective-permute-start.3 = (f32[32,256]{1,0:T(8,128)S(1)}, f32[32,256]{1,0:T(8,128)S(1)}, u32[]{:S(2)}, u32[]{:S(2)}) collective-permute-start(f32[32,256]{1,0:T(8,128)S(1)} %get-tuple-element.29), channel_id=1, source_target_pairs={{0,1},{1,0},{2,3},{3,2},{4,5},{5,4},{6,7},{7,6},{8,9},{9,8},{10,11... | collective-permute-start | bytes 98312 | tf_op jit(solution)/shard_map/ppermute | solution.py:430
  10.5 4.0 %collective-permute-start.5 = (f32[32,256]{1,0:T(8,128)S(1)}, f32[32,256]{1,0:T(8,128)S(1)}, u32[]{:S(2)}, u32[]{:S(2)}) collective-permute-start(f32[32,256]{1,0:T(8,128)S(1)} %get-tuple-element.30), channel_id=1, source_target_pairs={{3,4},{4,3},{0,1},{1,2},{2,0},{7,8},{8,7},{5,6},{6,5},{11,12},{12,... | collective-permute-start | bytes 98312 | tf_op jit(solution)/shard_map/ppermute | solution.py:489
  11.0 4.7 %collective-permute-start.4 = (f32[32,256]{1,0:T(8,128)S(1)}, f32[32,256]{1,0:T(8,128)S(1)}, u32[]{:S(2)}, u32[]{:S(2)}) collective-permute-start(f32[32,256]{1,0:T(8,128)S(1)} %get-tuple-element.30), channel_id=1, source_target_pairs={{0,3},{1,2},{2,1},{3,0},{4,7},{5,6},{6,5},{7,4},{8,11},{9,10},{10,... | collective-permute-start | bytes 98312 | tf_op jit(solution)/shard_map/ppermute | solution.py:430

commit v3 on v1

--- a/solution.py
+++ b/solution.py
@@ -110,41 +110,36 @@
 WHOLE_REST = (WHOLE - WHOLE_HIGH.astype(np.float64)).astype(jnp.bfloat16)
 
 
-def group_rounds(groups):
-    rounds = groups.bit_length() - 1
-    held = [0]
-    plan = []
-    for r in range(1, rounds + 1):
-        flip = (1 << r) - 1
-        plan.append((flip, list(held)))
-        held = held + [offset ^ flip for offset in held]
-    return plan, held
-
-
 def crossing_pairs(slabs, groups):
-    pairs = []
-    for g in range(slabs):
-        first, last = g * groups, g * groups + groups - 1
-        if g + 1 < slabs:
-            pairs += [(last, last + 1), (last + 1, last)]
-        idle = [
-            d
-            for d in range(first, last + 1)
-            if not ((d == first and g > 0) or (d == last and g + 1 < slabs))
-        ]
-        pairs += [(d, idle[(k + 1) % len(idle)]) for k, d in enumerate(idle)]
+    count = slabs * groups
+    pairs = [(d, d + 1) for d in range(3, count - 3, 2)]
+    pairs += [(d + 1, d) for d, _ in pairs]
+    for cycle in ((0, 1, 2), (count - 3, count - 2, count - 1)):
+        pairs += [(d, cycle[(k + 1) % 3]) for k, d in enumerate(cycle)]
     return pairs
 
 
-def to_message(out1_ref, out2_ref, up, down):
+def end_pairs(slabs, groups):
+    count = slabs * groups
+    pairs = [(d, d ^ 1) for d in range(4, count - 4)]
+    for base in (0, count - 4):
+        pairs += [(base + p, base + q) for p, q in ((2, 1), (1, 0), (0, 3), (3, 2))]
+    return pairs
+
+
+def to_message(out1_ref, out2_ref, out3_ref, up, down):
     even = lax.rem(lax.axis_index("patch"), 2) == 0
     for which in range(2):
         here = slice(16 * which, 16 * which + 16)
         out1_ref[here, :] = jnp.where(even, up[which], down[which])
-        out2_ref[here, :] = jnp.where(even, down[which], up[which])
-
-
-def first_kernel(fields, decay, gain, resist, out1, out2, own, faces, decays, gains, resists, sems):
+        far = jnp.where(even, down[which], up[which])
+        out2_ref[here, :] = far
+        out3_ref[here, :] = far
+
+
+def first_kernel(
+    fields, decay, gain, resist, owner, out2, own, out1, out3, names, faces, decays, gains, resists, sems
+):
     copies = [
         pltpu.make_async_copy(fields.at[0:2, 48:64], faces.at[0, 0:2], sems.at[0]),
         pltpu.make_async_copy(fields.at[3:5, 48:64], faces.at[0, 2:4], sems.at[1]),
@@ -153,6 +148,7 @@
         pltpu.make_async_copy(decay, decays, sems.at[4]),
         pltpu.make_async_copy(gain, gains, sems.at[5]),
         pltpu.make_async_copy(resist, resists, sems.at[6]),
+        pltpu.make_async_copy(owner, names, sems.at[7]),
     ]
     for copy in copies:
         copy.start()
@@ -162,10 +158,11 @@
     up = (ex + hy, ey - hx)
     ex, ey, hx, hy = (faces[1, f] for f in range(4))
     down = (ex - hy, ey + hx)
-    to_message(out1, out2, up, down)
+    to_message(out1, out2, out3, up, down)
     own[...] = jnp.zeros_like(own)
-    for which, ref in enumerate((decays, gains, resists)):
-        own[which : which + 1, 0 : ref.shape[1]] = ref[...]
+    own[0:1, 0:POLES] = decays[...]
+    own[1:2, 0:POLES] = gains[...]
+    own[2:3, :] = jnp.full((1, 128), resists[0], jnp.float32)
     out1[32:40, 0:128] = own[...]
 
 
@@ -209,12 +206,14 @@
     return jnp.concatenate(parts, axis=0)
 
 
-def update(ref, halves, voltage, high_ref, rest_ref):
+def update(ref, halves, voltage, tables, loads=()):
     stacked = jnp.concatenate([ref[f] for f in range(6)] + [exteriors(ref, halves, voltage)], axis=0)
     high = stacked.astype(jnp.bfloat16)
     rest = (stacked - high.astype(jnp.float32)).astype(jnp.bfloat16)
     dot = functools.partial(jnp.dot, preferred_element_type=jnp.float32)
-    return dot(high_ref[...], high) + (dot(high_ref[...], rest) + dot(rest_ref[...], high))
+    for load in loads:
+        load.wait()
+    return dot(tables[0], high) + (dot(tables[0], rest) + dot(tables[1], high))
 
 
 def currents(ref):
@@ -225,72 +224,72 @@
     return found
 
 
-def second_kernel(fields, states, high_ref, rest_ref, out, current, sums, halves):
-    sums[...] = jnp.zeros_like(sums)
+def second_kernel(fields, states_h, tables_h, out, current, summed, states, tables, halves, sems):
+    loads = [pltpu.make_async_copy(tables_h.at[k], tables.at[k], sems.at[k]) for k in range(2)]
+    copy = pltpu.make_async_copy(states_h, states, sems.at[2])
+    for load in loads:
+        load.start()
+    copy.start()
+    nothing = [jnp.zeros((16, 128), jnp.float32)] * 2
+    result = update(fields, halves, nothing, tables, loads)
+    for f in range(6):
+        out[f] = fields[f] + result[64 * f : 64 * f + 64]
+    for part, value in enumerate(currents(fields)):
+        current[part] = value
+    copy.wait()
     for part in range(2):
         total = states[0, part]
         for pole in range(1, POLES):
             total = total + states[pole, part]
-        sums[part, :, 0:EX] = total
-    voltage = [pltpu.roll(sums[part], 128 - EX, 1) for part in range(2)]
-    result = update(fields, halves, voltage, high_ref, rest_ref)
-    for f in range(6):
-        out[f] = fields[f] + result[64 * f : 64 * f + 64]
-    for part, value in enumerate(currents(fields)):
-        current[part] = value
-
-
-def z_exteriors(slabs, groups, got1, others, crossing):
+        summed[part] = jnp.zeros((16, 128), jnp.float32)
+        summed[part, :, 0:EX] = total
+
+
+def z_exteriors(slabs, groups, near_ref, far_ref, ends_ref):
     position = lax.axis_index("patch")
     device = lax.axis_index("slab") * groups + position
+    count = slabs * groups
     even = lax.rem(position, 2) == 0
-    edge = position + lax.rem(position, 2)
-    end = (device == 0) | (device == slabs * groups - 1)
+    outside = (device == 0) | (device == count - 1)
+    at_end = (device == 1) | (device == count - 3)
     low, high = [], []
     for which in range(2):
         here = slice(16 * which, 16 * which + 16)
-        far = crossing[here, :]
-        for r, ref in enumerate(others):
-            half = 2 << r
-            inside = (lax.rem(edge, 2 * half) == half) & (edge < groups)
-            far = jnp.where(inside, ref[here, :], far)
-        far = jnp.where(end, 0.0, far)
-        near = got1[here, :]
+        far = jnp.where(at_end, ends_ref[here, :], far_ref[here, :])
+        far = jnp.where(outside, 0.0, far)
+        near = near_ref[here, :]
         low.append(jnp.where(even, far, near))
         high.append(jnp.where(even, near, far))
     return low, high
 
 
 def face_parameter(owner, sets, row, column):
-    total = None
-    for source, ref, start in sets:
-        value = jnp.where(owner == source, ref[start + row : start + row + 1, column : column + 1], 0.0)
-        total = value if total is None else total + value
+    position = lax.axis_index("patch")
+    total = 0.0
+    for offset, ref, start in sets:
+        value = ref[start + row : start + row + 1, column : column + 1]
+        total = total + jnp.where(owner == (position ^ offset), value, 0.0)
     return total
-
-
-def parameter_sets(held, refs):
-    position = lax.axis_index("patch")
-    return [(position ^ offset, refs[ref], start) for offset, ref, start in held]
 
 
 def at_faces(value):
     return pltpu.roll(value, 128 - EX, 1)
 
 
-def third_kernel(slabs, groups, held, *refs):
-    rounds = groups.bit_length() - 1
-    before, current, owner, own = refs[:4]
-    got = refs[4 : 4 + rounds]
-    crossing = refs[4 + rounds]
-    out1, out2, outz, drive = refs[5 + rounds : 9 + rounds]
-    low, high = z_exteriors(slabs, groups, got[0], got[1:], crossing)
-    sets = parameter_sets(held, (own,) + tuple(got))
-    resist = face_parameter(owner[...], sets, 2, 0)
+def parameters(held, own, near, others):
+    refs = (own, near) + tuple(others)
+    return [(offset, refs[ref], start) for offset, ref, start in held]
+
+
+def third_kernel(slabs, groups, held, before, current, summed, owner, own, far, near, ends, *refs):
+    others = refs[:-5]
+    out2, out1, out3, outz, drive = refs[-5:]
+    low, high = z_exteriors(slabs, groups, near, far, ends)
+    resist = face_parameter(owner[...], parameters(held, own, near, others), 2, 0)
     pushes = []
     for part in range(2):
         drive[part] = jnp.zeros((16, 128), jnp.float32)
-        drive[part, :, 0:EX] = resist * current[part, :, 0:EX]
+        drive[part, :, 0:EX] = resist * current[part, :, 0:EX] + summed[part, :, 0:EX]
         rolled = at_faces(drive[part])
         drive[part] = rolled
         pushes.append(jnp.concatenate([jnp.zeros((16, LAYER - 128), jnp.float32), rolled], axis=1))
@@ -315,7 +314,7 @@
         ex - hy + weight * high[0] + pushed(1, 0),
         ey + hx + weight * high[1] - pushed(0, 0),
     )
-    to_message(out1, out2, up, down)
+    to_message(out1, out2, out3, up, down)
 
 
 def z_update(field, k, low, high):
@@ -329,10 +328,11 @@
     return a * low[0] - b * high[0]
 
 
-def fourth_kernel(held, rounds, *refs):
-    fields, before, current, states, beyond, drive, owner, own = refs[:8]
-    got = refs[8 : 8 + rounds]
-    high_ref, rest_ref, out, new_states, middle, sums, table, halves = refs[8 + rounds :]
+def fourth_kernel(
+    held, fields, before, current, states, beyond, drive, owner, own, near, tables, *refs
+):
+    others = refs[:-6]
+    out, new_states, middle, sums, table, halves = refs[-6:]
     low = [beyond[0:16, :], beyond[16:32, :]]
     high = [beyond[32:48, :], beyond[48:64, :]]
     for f in (0, 1, 3, 4):
@@ -347,7 +347,7 @@
             added = jnp.concatenate([sign * HIGH_WEIGHT[j] * rows for j in range(4)], axis=0)
             here = slice(16 * k, 16 * k + 16)
             middle[f, here, LAYER - 128 : LAYER] = middle[f, here, LAYER - 128 : LAYER] + added
-    sets = parameter_sets(held, (own,) + tuple(got))
+    sets = parameters(held, own, near, others)
     names = owner[...]
     for row in range(2):
         for pole in range(POLES):
@@ -368,21 +368,17 @@
             new_states[pole, part] = decay * renewed + gain * later[part][:, 0:EX]
         sums[part, :, 0:EX] = total
     voltage = [at_faces(sums[part]) for part in range(2)]
-    result = update(middle, halves, voltage, high_ref, rest_ref)
+    result = update(middle, halves, voltage, tables)
     for f in range(6):
         out[f] = 0.5 * fields[f] + 0.5 * (middle[f] + result[64 * f : 64 * f + 64])
 
 
-def fifth_kernel(slabs, groups, *refs):
-    rounds = groups.bit_length() - 1
-    before = refs[0]
-    got = refs[1 : 1 + rounds]
-    crossing, out, held, sems = refs[1 + rounds :]
+def fifth_kernel(slabs, groups, before, far, near, ends, out, held, sems):
     copies = []
     for f in (2, 5):
         copies.append(pltpu.make_async_copy(before.at[f], out.at[f], sems.at[f]))
         copies[-1].start()
-    low, high = z_exteriors(slabs, groups, got[0], got[1:], crossing)
+    low, high = z_exteriors(slabs, groups, near, far, ends)
     low = [0.5 * v for v in low]
     high = [0.5 * v for v in high]
     for slot, f in enumerate((0, 1, 3, 4)):
@@ -401,12 +397,8 @@
 
 def on_device(slabs, groups, fields, pole_state, pole_decay, pole_gain, surface_resistance, face_owner):
     f32 = jnp.float32
-    plan, held_offsets = group_rounds(groups)
-    rounds = len(plan)
-    held = [(0, 0, 0)]
-    for r, (flip, carried) in enumerate(plan):
-        held += [(offset ^ flip, r + 1, 32 + 3 * k) for k, offset in enumerate(carried)]
-    cross = crossing_pairs(slabs, groups)
+    crossing = crossing_pairs(slabs, groups)
+    ending = end_pairs(slabs, groups)
 
     def within(message, flip):
         pairs = [
@@ -416,80 +408,108 @@
 
     owner = face_owner.reshape(1, -1)
     width = fields.shape[-1]
-    message = pltpu.VMEM((MESSAGE, width), f32)
     faces_only = pltpu.VMEM((ROWS, width), f32)
     block = pltpu.VMEM(fields.shape, f32)
-    first1, first2, own = pl.pallas_call(
+    per_face = pltpu.VMEM((2, 16, 128), f32)
+    work = pl.CostEstimate(
+        flops=2 * 10**9, bytes_accessed=4 * fields.size, transcendentals=0
+    )
+    first2, own, first1, first3, names = pl.pallas_call(
         first_kernel,
-        out_shape=(message, faces_only, pltpu.VMEM((8, 128), f32)),
-        in_specs=[HB] * 4,
-        out_specs=[VM] * 3,
+        out_shape=(
+            faces_only,
+            pltpu.VMEM((8, 128), f32),
+            pltpu.VMEM((MESSAGE, width), f32),
+            faces_only,
+            pltpu.VMEM(owner.shape, owner.dtype),
+        ),
+        in_specs=[HB] * 5,
+        out_specs=[VM] * 5,
         scratch_shapes=[
             pltpu.VMEM((2, 4, 16, width), f32),
             pltpu.VMEM((1, POLES), f32),
             pltpu.VMEM((1, POLES), f32),
-            pltpu.VMEM((1, 1), f32),
-            pltpu.SemaphoreType.DMA((7,)),
+            pltpu.SMEM((1,), f32),
+            pltpu.SemaphoreType.DMA((8,)),
         ],
         name="send_first",
-    )(fields, pole_decay, pole_gain, surface_resistance.reshape(1, 1))
-
-    got = [within(first1, plan[0][0])]
-    got_cross = lax.ppermute(first2, AXES, cross)
-    known = [own[0:3]]
-    for r, (flip, carried) in enumerate(plan):
-        if r == 0:
+    )(fields, pole_decay, pole_gain, surface_resistance, owner)
+    far = lax.ppermute(first2, AXES, crossing)
+    near = within(first1, 1)
+    known, held, others = [own[0:3]], [(0, 0, 0)], []
+    for r in range(1, groups.bit_length()):
+        flip = (1 << r) - 1
+        if r == 1:
+            held.append((1, 1, ROWS))
+            known.append(near[ROWS : ROWS + 3, 0:128])
             continue
-        known = known + [got[r - 1][32 + 3 * k : 35 + 3 * k, 0:128] for k in range(len(known))]
-        extra = jnp.concatenate(known, axis=0)
-        extra = jnp.pad(extra, ((0, -extra.shape[0] % 8), (0, width - 128)))
-        got.append(within(jnp.concatenate([first2, extra], axis=0), flip))
-
-    high, rest = jnp.asarray(WHOLE_HIGH), jnp.asarray(WHOLE_REST)
-    fields_v, states_v, high_v, rest_v, owner_v = in_vmem(fields, pole_state, high, rest, owner)
-    before, current = pl.pallas_call(
-        second_kernel,
-        out_shape=(block, pltpu.VMEM((2, 16, 128), f32)),
-        in_specs=[VM] * 4,
-        out_specs=[VM] * 2,
-        scratch_shapes=[pltpu.VMEM((2, 16, 128), f32), pltpu.VMEM((8, 64, 128), f32)],
-        name="local_first",
-    )(fields_v, states_v, high_v, rest_v)
-
-    got_v = in_vmem(*got, got_cross)
-    second1, second2, beyond, drive = pl.pallas_call(
-        functools.partial(third_kernel, slabs, groups, held),
-        out_shape=(faces_only, faces_only, pltpu.VMEM((64, width), f32), pltpu.VMEM((2, 16, 128), f32)),
-        in_specs=[VM] * (5 + rounds),
-        out_specs=[VM] * 4,
-        name="send_second",
-    )(before, current, owner_v, own, *got_v)
-
-    later_cross = lax.ppermute(second2, AXES, cross)
-    later = [within(second1 if r == 0 else second2, flip) for r, (flip, _) in enumerate(plan)]
+        sent = jnp.concatenate(known, axis=0)
+        sent = jnp.pad(sent, ((0, -sent.shape[0] % 8), (0, 0)))
+        sent, first3 = lax.optimization_barrier((sent, first3))
+        others.append(within(sent, flip))
+        for k in range(len(known)):
+            held.append((held[k][0] ^ flip, r, 3 * k))
+            known.append(others[-1][3 * k : 3 * k + 3])
+    ends = lax.ppermute(first3, AXES, ending)
+
+    (fields_v,) = in_vmem(fields)
+    both = np.stack([WHOLE_HIGH, WHOLE_REST])
+    before, current, summed, states_v, tables = in_vmem(
+        *pl.pallas_call(
+            second_kernel,
+            out_shape=(
+                block,
+                per_face,
+                per_face,
+                pltpu.VMEM(pole_state.shape, f32),
+                pltpu.VMEM(both.shape, both.dtype),
+            ),
+            in_specs=[VM, HB, HB],
+            out_specs=[VM] * 5,
+            scratch_shapes=[pltpu.VMEM((8, 64, 128), f32), pltpu.SemaphoreType.DMA((3,))],
+            cost_estimate=work,
+            name="local_first",
+        )(fields_v, pole_state, jnp.asarray(both))
+    )
+
+    own, names, near, far, ends, *others = in_vmem(own, names, near, far, ends, *others)
+    second2, second1, second3, beyond, drive = in_vmem(
+        *pl.pallas_call(
+            functools.partial(third_kernel, slabs, groups, held),
+            out_shape=(faces_only, faces_only, faces_only, pltpu.VMEM((64, width), f32), per_face),
+            in_specs=[VM] * (8 + len(others)),
+            out_specs=[VM] * 5,
+            name="send_second",
+        )(before, current, summed, names, own, far, near, ends, *others)
+    )
+
+    later_far = lax.ppermute(second2, AXES, crossing)
+    later_near = within(second1, 1)
+    later_ends = lax.ppermute(second3, AXES, ending)
 
     almost, advanced_states = pl.pallas_call(
-        functools.partial(fourth_kernel, held, rounds),
+        functools.partial(fourth_kernel, held),
         out_shape=(block, jax.ShapeDtypeStruct(pole_state.shape, f32)),
-        in_specs=[VM] * (10 + rounds),
+        in_specs=[VM] * (10 + len(others)),
         out_specs=[VM] * 2,
         scratch_shapes=[
             pltpu.VMEM(fields.shape, f32),
-            pltpu.VMEM((2, 16, 128), f32),
+            per_face,
             pltpu.VMEM((2 * POLES, 128), f32),
             pltpu.VMEM((8, 64, 128), f32),
         ],
+        cost_estimate=work,
         name="local_second",
-    )(fields_v, before, current, states_v, beyond, drive, owner_v, own, *got_v[:rounds], high_v, rest_v)
+    )(fields_v, before, current, states_v, beyond, drive, names, own, near, tables, *others)
 
     advanced = pl.pallas_call(
         functools.partial(fifth_kernel, slabs, groups),
         out_shape=jax.ShapeDtypeStruct(fields.shape, f32),
-        in_specs=[VM] * (2 + rounds),
+        in_specs=[VM] * 4,
         out_specs=HB,
         scratch_shapes=[pltpu.VMEM((4, 64, width), f32), pltpu.SemaphoreType.DMA((6,))],
         name="finish",
-    )(almost, *in_vmem(*later, later_cross))
+    )(*in_vmem(almost, later_far, later_near, later_ends))
     return advanced, advanced_states
 
 

time: 22.5 us -> 14.6 us (0.65)
  local copies, waits for them, and re-layouts: 6.88 us -> 0.01 us
  Pallas kernels: 6.43 us -> 4.49 us
  waiting for transfers between devices: 1.71 us -> 3.46 us
  starting transfers between devices: 5.69 us -> 5.06 us
    unnamed x22 -> x2, local copies, waits for them, and re-layouts: 6.87 us -> 0.01 us
    ppermute x2 -> x4, waiting for transfers between devices: 0.01 us -> 3.46 us  [the longest x1 2.25 us: on_device(): later_ends = lax.ppermute(second3, AXES, ending)]
    ppermute x4 -> x3, waiting for transfers between devices: 1.71 us -> 0.01 us  [within(): return lax.ppermute(message, AXES, pairs)]
    ppermute x4 -> x3, starting transfers between devices: 3.27 us -> 1.74 us  [within(): return lax.ppermute(message, AXES, pairs)]
    pallas_call x1, Pallas kernels: 1.18 us -> 0.16 us  [on_device(): pl.pallas_call(functools.partial(third_kernel, slabs, groups, held), out_...]
    pallas_call x1, Pallas kernels: 1.78 us -> 0.79 us  [on_device(): pl.pallas_call(functools.partial(fifth_kernel, slabs, groups), out_shape=...]
    ppermute x2 -> x4, starting transfers between devices: 2.42 us -> 3.32 us  [the longest x1 2.61 us: on_device(): far = lax.ppermute(first2, AXES, crossing)]
  transfers between devices with their start and end apart: 6 -> 7, of which waited for: 2 -> 2; matrix products, arithmetic and copies ran while one was open for 0% -> 0% of each run, Pallas kernels for 12% -> 18%
where the time goes in v3:
time: 14.6 us; the launch traced here: 14.4 us
  starting transfers between devices  5.06 us (35%)
  Pallas kernels  4.49 us (31%)
  waiting for transfers between devices  3.46 us (24%)
  between operations  1.38 us (9%)
    ppermute x1, starting transfers between devices, on_device(): far = lax.ppermute(first2, AXES, crossing)  2.61 us
    ppermute x1, waiting for transfers between devices, on_device(): later_ends = lax.ppermute(second3, AXES, ending)  2.25 us
    ppermute x3, starting transfers between devices, within(): return lax.ppermute(message, AXES, pairs)  1.74 us
    pallas_call x1, Pallas kernels, on_device(): pl.pallas_call(second_kernel, out_shape=(block, per_face, per_face, pltpu...  1.66 us
    ppermute x1, waiting for transfers between devices, on_device(): ends = lax.ppermute(first3, AXES, ending)  1.2 us
    pallas_call x1, Pallas kernels, on_device(): pl.pallas_call(functools.partial(fourth_kernel, held), out_shape=(block,...  0.97 us
    pallas_call x1, Pallas kernels, on_device(): pl.pallas_call(first_kernel, out_shape=(faces_only, pltpu.VMEM((8, 128),...  0.91 us
    pallas_call x1, Pallas kernels, on_device(): pl.pallas_call(functools.partial(fifth_kernel, slabs, groups), out_shape=...  0.79 us
  transfers between devices with their start and end apart: 7, of which 2 were waited for; matrix products, arithmetic and copies ran while one was open for 0% of the time, Pallas kernels for 18%

profile of v3, /device:TPU:1, one launch (start us, length us, event | category | flops | bytes accessed | tf_op | source)
XLA Modules:
  0.0 14.4 jit_solution(8849704262882439559)
XLA Ops:
  0.6 0.0 copy-start
  1.3 0.9 %send_first.1 = (f32[32,256]{1,0:T(8,128)S(1)}, f32[8,128]{1,0:T(8,128)S(1)}, f32[40,256]{1,0:T(8,128)S(1)}, f32[32,256]{1,0:T(8,128)S(1)}, s32[1,16]{1,0:T(1,128)S(1)}) custom-call(f32[6,64,256]{2,1,0:T(8,128)} %fields.5, f32[1,12]{1,0:T(1,128)} %decay.1, f32[1,12]{1,0:T(1,128)} %gain.1, f32[1]{0:T(128)S(6)} %copy.9.resist, s32[1,16]{1,0:T(1,128)} %bitcast.1), custom_call_target="tpu_custom_call" | custom-call | tf_op jit(solution)/shard_map/send_first/pallas_call | solution.py:417
  2.3 0.1 collective-permute-start.1
  2.4 2.6 %collective-permute-start = (f32[32,256]{1,0:T(8,128)S(1)}, f32[32,256]{1,0:T(8,128)S(1)}, u32[]{:S(2)}, u32[]{:S(2)}) collective-permute-start(f32[32,256]{1,0:T(8,128)S(1)} %get-tuple-element.27), channel_id=1, source_target_pairs={{3,4},{5,6},{7,8},{9,10},{11,12},{13,14},{15,16},{17,18},{19,20},{... | collective-permute-start | bytes 98312 | tf_op jit(solution)/shard_map/ppermute | solution.py:437
  5.0 0.0 collective-permute-done.1.near
  5.0 1.2 %collective-permute-start.3 = (f32[8,128]{1,0:T(8,128)S(1)}, f32[8,128]{1,0:T(8,128)S(1)}, u32[]{:S(2)}, u32[]{:S(2)}) collective-permute-start(f32[8,128]{1,0:T(8,128)S(1)} %select_maximum_fusion), channel_id=1, source_target_pairs={{0,3},{1,2},{2,1},{3,0},{4,7},{5,6},{6,5},{7,4},{8,11},{9,10},{10,... | collective-permute-start | bytes 12296 | tf_op jit(solution)/shard_map/ppermute | solution.py:407
  6.2 0.5 %collective-permute-start.2 = (f32[32,256]{1,0:T(8,128)S(1)}, f32[32,256]{1,0:T(8,128)S(1)}, u32[]{:S(2)}, u32[]{:S(2)}) collective-permute-start(f32[32,256]{1,0:T(8,128)S(1)} %get-tuple-element.30), channel_id=1, source_target_pairs={{4,5},{5,4},{6,7},{7,6},{8,9},{9,8},{10,11},{11,10},{12,13},{13,12... | collective-permute-start | bytes 98312 | tf_op jit(solution)/shard_map/ppermute | solution.py:453
  6.7 0.0 copy-done
  6.7 1.7 %local_first.1 = (f32[6,64,256]{2,1,0:T(8,128)S(1)}, f32[2,16,128]{2,1,0:T(8,128)S(1)}, f32[2,16,128]{2,1,0:T(8,128)S(1)}, f32[12,2,16,16]{3,2,1,0:T(8,128)S(1)}, bf16[2,384,512]{2,1,0:T(8,128)(2,1)S(1)}) custom-call(f32[6,64,256]{2,1,0:T(8,128)S(1)} %copy-done, f32[12,2,16,16]{3,2,1,0:T(8,128)} %states_h.1, bf16[2,384,512]{2,1,0:T(8,128)(2,1)} %constant.5.clone.tables_h), custom_call_target="tpu_custom_call" | custom-call | flops 2000000000 | bytes 393216 | tf_op jit(solution)/shard_map/local_first/pallas_call | solution.py:458
  8.3 0.0 collective-permute-done.far
  8.4 0.0 collective-permute-done.3.refs_0_
  8.4 1.2 %collective-permute-done.2.ends = f32[32,256]{1,0:T(8,128)S(1)} collective-permute-done((f32[32,256]{1,0:T(8,128)S(1)}, f32[32,256]{1,0:T(8,128)S(1)}, u32[]{:S(2)}, u32[]{:S(2)}) %collective-permute-start.2) | collective-permute-done | bytes 32800 | tf_op jit(solution)/shard_map/ppermute | solution.py:453
  9.6 0.2 %send_second.1 = (f32[32,256]{1,0:T(8,128)S(1)}, f32[32,256]{1,0:T(8,128)S(1)}, f32[32,256]{1,0:T(8,128)S(1)}, f32[64,256]{1,0:T(8,128)S(1)}, f32[2,16,128]{2,1,0:T(8,128)S(1)}) custom-call(f32[6,64,256]{2,1,0:T(8,128)S(1)} %get-tuple-element.21.before, f32[2,16,128]{2,1,0:T(8,128)S(1)} %get-tuple-element.22.current, ...), custom_call_target="tpu_custom_call" | custom-call | tf_op jit(solution)/shard_map/send_second/pallas_call | solution.py:477
  9.7 0.2 %collective-permute-start.4 = (f32[32,256]{1,0:T(8,128)S(1)}, f32[32,256]{1,0:T(8,128)S(1)}, u32[]{:S(2)}, u32[]{:S(2)}) collective-permute-start(f32[32,256]{1,0:T(8,128)S(1)} %get-tuple-element.36), channel_id=1, source_target_pairs={{3,4},{5,6},{7,8},{9,10},{11,12},{13,14},{15,16},{17,18},{19,20},{... | collective-permute-start | bytes 98312 | tf_op jit(solution)/shard_map/ppermute | solution.py:486
  9.9 0.4 %collective-permute-start.5 = (f32[32,256]{1,0:T(8,128)S(1)}, f32[32,256]{1,0:T(8,128)S(1)}, u32[]{:S(2)}, u32[]{:S(2)}) collective-permute-start(f32[32,256]{1,0:T(8,128)S(1)} %get-tuple-element.37), channel_id=1, source_target_pairs={{0,1},{1,0},{2,3},{3,2},{4,5},{5,4},{6,7},{7,6},{8,9},{9,8},{10,11... | collective-permute-start | bytes 98312 | tf_op jit(solution)/shard_map/ppermute | solution.py:407
  10.3 0.1 collective-permute-start.6
  10.4 1.0 %local_second.1 = (f32[6,64,256]{2,1,0:T(8,128)S(1)}, f32[12,2,16,16]{3,2,1,0:T(8,128)}) custom-call(f32[6,64,256]{2,1,0:T(8,128)S(1)} %copy-done, f32[6,64,256]{2,1,0:T(8,128)S(1)} %get-tuple-element.21.before, f32[2,16,128]{2,1,0:T(8,128)S(1)} %get-tuple-element.22.current, f32[12,2,16,16]{3,2,1,0:T(8,128)S(1)} %get-tuple-element.23.states, ...), custom_call_target="tpu_custom_call" | custom-call | flops 2000000000 | bytes 393216 | tf_op jit(solution)/shard_map/local_second/pallas_call | solution.py:490
  11.4 0.0 collective-permute-done.4.far
  11.4 0.0 collective-permute-done.5.near
  11.4 2.3 %collective-permute-done.6.ends = f32[32,256]{1,0:T(8,128)S(1)} collective-permute-done((f32[32,256]{1,0:T(8,128)S(1)}, f32[32,256]{1,0:T(8,128)S(1)}, u32[]{:S(2)}, u32[]{:S(2)}) %collective-permute-start.6) | collective-permute-done | bytes 32800 | tf_op jit(solution)/shard_map/ppermute | solution.py:488
  13.6 0.8 %finish.1 = f32[6,64,256]{2,1,0:T(8,128)} custom-call(f32[6,64,256]{2,1,0:T(8,128)S(1)} %get-tuple-element.35.before, f32[32,256]{1,0:T(8,128)S(1)} %collective-permute-done.4.far, f32[32,256]{1,0:T(8,128)S(1)} %collective-permute-done.5.near, f32[32,256]{1,0:T(8,128)S(1)} %collective-permute-done.6.ends), custom_call_target="tpu_custom_call" | custom-call | tf_op jit(solution)/shard_map/finish/pallas_call | solution.py:505
  (3 shorter events, 0.0 us)
Async XLA Ops:
  0.6 6.0 %copy-start = (f32[6,64,256]{2,1,0:T(8,128)S(1)}, f32[6,64,256]{2,1,0:T(8,128)}, u32[]{:S(2)}) copy-start(f32[6,64,256]{2,1,0:T(8,128)} %fields.5) | copy-start | bytes 1179652
  2.3 2.7 %collective-permute-start.1 = (f32[40,256]{1,0:T(8,128)S(1)}, f32[40,256]{1,0:T(8,128)S(1)}, u32[]{:S(2)}, u32[]{:S(2)}) collective-permute-start(f32[40,256]{1,0:T(8,128)S(1)} %get-tuple-element.28), channel_id=1, source_target_pairs={{0,1},{1,0},{2,3},{3,2},{4,5},{5,4},{6,7},{7,6},{8,9},{9,8},{10,11... | collective-permute-start | bytes 122888 | tf_op jit(solution)/shard_map/ppermute | solution.py:407
  2.4 6.0 %collective-permute-start = (f32[32,256]{1,0:T(8,128)S(1)}, f32[32,256]{1,0:T(8,128)S(1)}, u32[]{:S(2)}, u32[]{:S(2)}) collective-permute-start(f32[32,256]{1,0:T(8,128)S(1)} %get-tuple-element.27), channel_id=1, source_target_pairs={{3,4},{5,6},{7,8},{9,10},{11,12},{13,14},{15,16},{17,18},{19,20},{... | collective-permute-start | bytes 98312 | tf_op jit(solution)/shard_map/ppermute | solution.py:437
  5.0 3.4 %collective-permute-start.3 = (f32[8,128]{1,0:T(8,128)S(1)}, f32[8,128]{1,0:T(8,128)S(1)}, u32[]{:S(2)}, u32[]{:S(2)}) collective-permute-start(f32[8,128]{1,0:T(8,128)S(1)} %select_maximum_fusion), channel_id=1, source_target_pairs={{0,3},{1,2},{2,1},{3,0},{4,7},{5,6},{6,5},{7,4},{8,11},{9,10},{10,... | collective-permute-start | bytes 12296 | tf_op jit(solution)/shard_map/ppermute | solution.py:407
  6.2 3.3 %collective-permute-start.2 = (f32[32,256]{1,0:T(8,128)S(1)}, f32[32,256]{1,0:T(8,128)S(1)}, u32[]{:S(2)}, u32[]{:S(2)}) collective-permute-start(f32[32,256]{1,0:T(8,128)S(1)} %get-tuple-element.30), channel_id=1, source_target_pairs={{4,5},{5,4},{6,7},{7,6},{8,9},{9,8},{10,11},{11,10},{12,13},{13,12... | collective-permute-start | bytes 98312 | tf_op jit(solution)/shard_map/ppermute | solution.py:453
  9.7 1.6 %collective-permute-start.4 = (f32[32,256]{1,0:T(8,128)S(1)}, f32[32,256]{1,0:T(8,128)S(1)}, u32[]{:S(2)}, u32[]{:S(2)}) collective-permute-start(f32[32,256]{1,0:T(8,128)S(1)} %get-tuple-element.36), channel_id=1, source_target_pairs={{3,4},{5,6},{7,8},{9,10},{11,12},{13,14},{15,16},{17,18},{19,20},{... | collective-permute-start | bytes 98312 | tf_op jit(solution)/shard_map/ppermute | solution.py:486
  9.9 1.5 %collective-permute-start.5 = (f32[32,256]{1,0:T(8,128)S(1)}, f32[32,256]{1,0:T(8,128)S(1)}, u32[]{:S(2)}, u32[]{:S(2)}) collective-permute-start(f32[32,256]{1,0:T(8,128)S(1)} %get-tuple-element.37), channel_id=1, source_target_pairs={{0,1},{1,0},{2,3},{3,2},{4,5},{5,4},{6,7},{7,6},{8,9},{9,8},{10,11... | collective-permute-start | bytes 98312 | tf_op jit(solution)/shard_map/ppermute | solution.py:407
  10.3 3.3 %collective-permute-start.6 = (f32[32,256]{1,0:T(8,128)S(1)}, f32[32,256]{1,0:T(8,128)S(1)}, u32[]{:S(2)}, u32[]{:S(2)}) collective-permute-start(f32[32,256]{1,0:T(8,128)S(1)} %get-tuple-element.38), channel_id=1, source_target_pairs={{4,5},{5,4},{6,7},{7,6},{8,9},{9,8},{10,11},{11,10},{12,13},{13,12... | collective-permute-start | bytes 98312 | tf_op jit(solution)/shard_map/ppermute | solution.py:488

commit v4 on v3

v4 whole, which is shorter than its diff:
```python
import functools
import math

import jax
import jax.numpy as jnp
import numpy as np
from jax import lax
from jax.experimental import pallas as pl
from jax.experimental.pallas import tpu as pltpu
from jax.sharding import PartitionSpec as P

EX = 16
EY = 16
LAYER = EX * EY
POLES = 12
courant = 0.04
tangent_pairs = ((1, 2), (2, 0), (0, 1))
ROWS = 32
MESSAGE = 40
AXES = ("slab", "patch")

COVER = pl.CostEstimate(flops=2 * 10**9, bytes_accessed=0, transcendentals=0)
VM = pl.BlockSpec(memory_space=pltpu.VMEM)
HB = pl.BlockSpec(memory_space=pl.ANY)


def lagrange_slopes(node_points):
    count = node_points.shape[0]
    weights = np.array(
        [
            np.prod([node_points[i] - node_points[m] for m in range(count) if m != i])
            for i in range(count)
        ]
    )
    matrix = np.zeros((count, count))
    for i in range(count):
        for j in range(count):
            if i != j:
                matrix[i, j] = weights[i] / weights[j] / (node_points[i] - node_points[j])
            else:
                matrix[i, i] = sum(
                    (1.0 / (node_points[i] - node_points[m]) for m in range(count) if m != i)
                )
    return matrix


def legendre_values(node_points):
    columns = [
        0.0 * node_points + 1.0,
        node_points,
        0.5 * (3.0 * node_points**2 - 1.0),
        0.5 * (5.0 * node_points**3 - 3.0 * node_points),
    ]
    return np.stack(
        [columns[degree] * math.sqrt((2 * degree + 1) / 2.0) for degree in range(4)], axis=1
    )


def build_tables():
    node_points = np.array([-1.0, -1.0 / math.sqrt(5.0), 1.0 / math.sqrt(5.0), 1.0])
    slope = lagrange_slopes(node_points)
    legendre = legendre_values(node_points)
    inverse_mass = legendre @ legendre.T
    low, high = 0.5 * courant * inverse_mass[:, 0], 0.5 * courant * inverse_mass[:, 3]
    rise, fall = -0.5 * courant * slope, 0.5 * courant * slope
    rise[:, 0] -= low
    fall[:, 3] -= high
    return rise.tolist(), fall.tolist(), low.tolist(), high.tolist()


RISE, FALL, LOW_WEIGHT, HIGH_WEIGHT = build_tables()


def crossing_pairs(slabs, groups):
    count = slabs * groups
    pairs = [(d, d + 1) for d in range(3, count - 3, 2)]
    pairs += [(d + 1, d) for d, _ in pairs]
    cycle = ((0, 1), (1, 2), (2, 0))
    return pairs + list(cycle) + [(count - 1 - d, count - 1 - e) for d, e in cycle]


def end_pairs(slabs, groups):
    count = slabs * groups
    pairs = [(d, d ^ 1) for d in range(4, count - 4)]
    cycle = ((2, 1), (1, 0), (0, 3), (3, 2))
    return pairs + list(cycle) + [(count - 1 - d, count - 1 - e) for d, e in cycle]


def is_even():
    return lax.rem(lax.axis_index("patch"), 2) == 0


def first_kernel(
    fields, decay, gain, resist, owner, out2, own, out1, names, faces, decays, gains, resists, sems
):
    copies = [
        pltpu.make_async_copy(fields.at[0:2, 48:64], faces.at[0, 0:2], sems.at[0]),
        pltpu.make_async_copy(fields.at[3:5, 48:64], faces.at[0, 2:4], sems.at[1]),
        pltpu.make_async_copy(fields.at[0:2, 0:16], faces.at[1, 0:2], sems.at[2]),
        pltpu.make_async_copy(fields.at[3:5, 0:16], faces.at[1, 2:4], sems.at[3]),
        pltpu.make_async_copy(decay, decays, sems.at[4]),
        pltpu.make_async_copy(gain, gains, sems.at[5]),
        pltpu.make_async_copy(resist, resists, sems.at[6]),
        pltpu.make_async_copy(owner, names, sems.at[7]),
    ]
    for copy in copies:
        copy.start()
    for copy in copies:
        copy.wait()
    ex, ey, hx, hy = (faces[0, f] for f in range(4))
    up = (ex + hy, ey - hx)
    ex, ey, hx, hy = (faces[1, f] for f in range(4))
    down = (ex - hy, ey + hx)
    for which in range(2):
        here = slice(16 * which, 16 * which + 16)
        out1[here, :] = jnp.where(is_even(), up[which], down[which])
        out2[here, :] = jnp.where(is_even(), down[which], up[which])
    own[...] = jnp.zeros_like(own)
    own[0:1, 0:POLES] = decays[...]
    own[1:2, 0:POLES] = gains[...]
    own[2:3, :] = jnp.full((1, 128), resists[0], jnp.float32)
    out1[32:40, 0:128] = own[...]


def y_rows(block, j):
    return jnp.concatenate([block[16 * k + 4 * j : 16 * k + 4 * j + 4] for k in range(4)], axis=0)


def by_row(values):
    row = lax.broadcasted_iota(jnp.int32, (8, LAYER), 0)
    found = jnp.full((8, LAYER), values[7], jnp.float32)
    for r in range(7):
        if values[r] != values[7]:
            found = jnp.where(row == r, values[r], found)
    return found


def along_x(matrix, weights, rises):
    shifts = {
        s: by_row([matrix[r % 4][r % 4 - s] if 0 <= r % 4 - s < 4 else 0.0 for r in range(8)])
        for s in range(-3, 4)
    }
    weight = by_row([weights[r % 4] for r in range(8)])
    place = lax.rem(lax.broadcasted_iota(jnp.int32, (8, 8, LAYER), 1), 4)
    column = lax.rem(lax.broadcasted_iota(jnp.int32, (8, 8, LAYER), 2), EX)

    def apply(value):
        rolled = {s: value if s == 0 else pltpu.roll(value, s % 8, 1) for s in range(-3, 4)}
        total = shifts[0] * value
        for s in range(-3, 4):
            if s != 0:
                total = total + shifts[s] * rolled[s]
        trace = value
        for step in range(1, 4):
            s, i = (-step, 3 - step) if rises else (step, step)
            trace = jnp.where(place == i, rolled[s], trace)
        moved = pltpu.roll(trace, 1 if rises else LAYER - 1, 2)
        moved = jnp.where(column == (0 if rises else EX - 1), 0.0, moved)
        return total + weight * moved

    return apply


def along_y(matrix, weights):
    parts = []
    for half in range(2):
        rows = [2 * half + r // 4 for r in range(8)]
        parts.append(
            (
                by_row([matrix[j][r // 4] for r, j in enumerate(rows)]),
                by_row([matrix[j][1 - r // 4] for r, j in enumerate(rows)]),
                by_row([matrix[j][2 + r // 4] for r, j in enumerate(rows)]),
                by_row([matrix[j][3 - r // 4] for r, j in enumerate(rows)]),
                by_row([weights[j] for j in rows]),
            )
        )

    def apply(low, high, low_turned, high_turned, beyond):
        return [
            a * low + b * low_turned + c * high + d * high_turned + w * beyond
            for a, b, c, d, w in parts
        ]

    return apply


def update(ref, base, goal, voltage, axes):
    begun = set()

    def add(field, value):
        held = goal if field in begun else base
        goal[field] = held[field] + value
        begun.add(field)

    def split(e, h, sign):
        e, h = ref[e], sign * ref[h]
        return e + h, e - h

    def join(e, h, sign, rising, falling):
        add(e, rising + falling)
        add(h, sign * (rising - falling))

    rise, fall = along_x(RISE, LOW_WEIGHT, True), along_x(FALL, HIGH_WEIGHT, False)
    for e, h, sign in ((1, 5, 1.0), (2, 4, -1.0)) if "x" in axes else ():
        p, q = split(e, h, sign)
        rising = rise(p.reshape(8, 8, LAYER)).reshape(64, LAYER)
        falling = fall(q.reshape(8, 8, LAYER)).reshape(64, LAYER)
        join(e, h, sign, rising, falling)

    rise, fall = along_y(RISE, LOW_WEIGHT), along_y(FALL, HIGH_WEIGHT)
    first = lax.broadcasted_iota(jnp.int32, (4, 8, LAYER), 1) < 4
    lane = lax.broadcasted_iota(jnp.int32, (4, 8, LAYER), 2)
    bottom, top = lane < EX, lane >= LAYER - EX
    for e, h, sign, part in ((2, 3, 1.0, 0), (0, 5, -1.0, 1)) if "y" in axes else ():
        p, q = split(e, h, sign)
        p, q = p.reshape(4, 2, 8, LAYER), q.reshape(4, 2, 8, LAYER)
        p0, p1, q0, q1 = p[:, 0], p[:, 1], q[:, 0], q[:, 1]
        p0_turned, p1_turned = pltpu.roll(p0, 4, 1), pltpu.roll(p1, 4, 1)
        q0_turned, q1_turned = pltpu.roll(q0, 4, 1), pltpu.roll(q1, 4, 1)
        upper = jnp.where(first, p1_turned, p1)
        below = jnp.where(bottom, 0.0, pltpu.roll(upper, EX, 2))
        lower = jnp.where(first, q0, q0_turned)
        if voltage is None:
            mirror = -upper
        else:
            doubled = []
            for k in range(4):
                rows = 2.0 * voltage[part][4 * k : 4 * k + 4]
                doubled.append(jnp.concatenate([rows, rows], axis=0)[None])
            doubled = jnp.concatenate(doubled, axis=0)
            empty = jnp.zeros((4, 8, LAYER - 128), jnp.float32)
            mirror = jnp.concatenate([empty, doubled], axis=2) - upper
        above = jnp.where(top, mirror, pltpu.roll(lower, LAYER - EX, 2))
        rising = rise(p0, p1, p0_turned, p1_turned, below)
        falling = fall(q0, q1, q0_turned, q1_turned, above)
        rising, falling = (
            jnp.concatenate([v[:, None] for v in pair], axis=1).reshape(64, LAYER)
            for pair in (rising, falling)
        )
        join(e, h, sign, rising, falling)

    for e, h, sign in ((0, 4, 1.0), (1, 3, -1.0)) if "z" in axes else ():
        p, q = split(e, h, sign)
        p = [p[16 * k : 16 * k + 16] for k in range(4)]
        q = [q[16 * k : 16 * k + 16] for k in range(4)]
        rising, falling = (
            jnp.concatenate([sum(m * v for m, v in zip(row, planes)) for row in matrix], axis=0)
            for matrix, planes in ((RISE, p), (FALL, q))
        )
        join(e, h, sign, rising, falling)


def currents(ref):
    found = []
    for field, sign in ((3, -1.0), (5, 1.0)):
        rows = y_rows(ref[field, :, LAYER - 128 : LAYER], 3)
        found.append(sign * pltpu.roll(rows, EX, 1))
    return found


def second_kernel(fields, states_h, out, current, summed, states, sem):
    copy = pltpu.make_async_copy(states_h, states, sem)
    copy.start()
    update(fields, fields, out, None, "xy")
    for part, value in enumerate(currents(fields)):
        current[part] = value
    copy.wait()
    for part in range(2):
        total = states[0, part]
        for pole in range(1, POLES):
            total = total + states[pole, part]
        summed[part] = jnp.zeros((16, 128), jnp.float32)
        summed[part, :, 0:EX] = total


def upright_kernel(fields, partial, out):
    update(fields, partial, out, None, "z")
    for field in (2, 5):
        out[field] = partial[field]


def far_exterior(slabs, groups, far_ref, ends_ref, start):
    device = lax.axis_index("slab") * groups + lax.axis_index("patch")
    count = slabs * groups
    left_out = (device == 1) | (device == count - 2)
    outside = (device == 0) | (device == count - 1)
    found = []
    for which in range(2):
        far = jnp.where(outside, 0.0, far_ref[16 * which : 16 * which + 16, :])
        ends = 0.0
        if ends_ref is not None:
            ends = ends_ref[start + 16 * which : start + 16 * which + 16, :]
        found.append(jnp.where(left_out, ends, far))
    return found


def low_and_high(near, far):
    low = [jnp.where(is_even(), far[which], near[which]) for which in range(2)]
    high = [jnp.where(is_even(), near[which], far[which]) for which in range(2)]
    return low, high


def face_parameter(owner, sets, row, column):
    position = lax.axis_index("patch")
    total = 0.0
    for offset, ref, start in sets:
        value = ref[start + row : start + row + 1, column : column + 1]
        total = total + jnp.where(owner == (position ^ offset), value, 0.0)
    return total


def at_faces(value):
    return pltpu.roll(value, 128 - EX, 1)


def parameters(held, own, near, others):
    refs = (own, near) + tuple(others)
    return [(offset, refs[ref], start) for offset, ref, start in held]


def driven(drive, part, k):
    rows = drive[part, 4 * k : 4 * k + 4, :]
    rows = jnp.concatenate([2.0 * HIGH_WEIGHT[j] * rows for j in range(4)], axis=0)
    return jnp.concatenate([jnp.zeros((16, LAYER - 128), jnp.float32), rows], axis=1)


def upper_message(before, drive, low):
    ex, ey, hx, hy = (before[f, 48:64, :] for f in (0, 1, 3, 4))
    weight = 2.0 * LOW_WEIGHT[3]
    return (
        ex + hy + weight * low[0] + driven(drive, 1, 3),
        ey - hx + weight * low[1] + driven(drive, 0, 3),
    )


def lower_message(before, drive, high):
    ex, ey, hx, hy = (before[f, 0:16, :] for f in (0, 1, 3, 4))
    weight = 2.0 * HIGH_WEIGHT[0]
    return (
        ex - hy + weight * high[0] + driven(drive, 1, 0),
        ey + hx + weight * high[1] - driven(drive, 0, 0),
    )


def third_kernel(held, before, current, summed, owner, own, near, *refs):
    others = refs[:-3]
    out2, out3, drive = refs[-3:]
    resist = face_parameter(owner[...], parameters(held, own, near, others), 2, 0)
    for part in range(2):
        drive[part] = jnp.zeros((16, 128), jnp.float32)
        drive[part, :, 0:EX] = resist * current[part, :, 0:EX] + summed[part, :, 0:EX]
        drive[part] = at_faces(drive[part])
    exterior = [near[16 * which : 16 * which + 16, :] for which in range(2)]
    up = upper_message(before, drive, exterior)
    down = lower_message(before, drive, exterior)
    for which in range(2):
        here = slice(16 * which, 16 * which + 16)
        far = jnp.where(is_even(), down[which], up[which])
        out2[here, :] = far
        out3[here, :] = far


def near_kernel(slabs, groups, before, drive, far, out1):
    exterior = far_exterior(slabs, groups, far, None, 0)
    up = upper_message(before, drive, exterior)
    down = lower_message(before, drive, exterior)
    for which in range(2):
        here = slice(16 * which, 16 * which + 16)
        out1[here, :] = jnp.where(is_even(), up[which], down[which])
    out1[ROWS : 2 * ROWS, :] = far[...]


def z_update(field, k, low, high):
    a, b = LOW_WEIGHT[k], HIGH_WEIGHT[k]
    if field == 0:
        return a * low[0] + b * high[0]
    if field == 1:
        return a * low[1] + b * high[1]
    if field == 3:
        return b * high[1] - a * low[1]
    return a * low[0] - b * high[0]


def poles_kernel(held, states, current, owner, own, near, *refs):
    others = refs[:-3]
    renewed, total, table = refs[-3:]
    sets = parameters(held, own, near, others)
    names = owner[...]
    for row in range(2):
        for pole in range(POLES):
            here = slice(POLES * row + pole, POLES * row + pole + 1)
            table[here, 0:EX] = face_parameter(names, sets, row, pole)
    table[2 * POLES : 2 * POLES + 1, 0:EX] = face_parameter(names, sets, 2, 0)
    for part in range(2):
        added = 0.0
        for pole in range(POLES):
            decay = table[pole : pole + 1, 0:EX]
            gain = table[POLES + pole : POLES + pole + 1, 0:EX]
            state = decay * states[pole, part] + gain * current[part, :, 0:EX]
            renewed[pole, part] = state
            added = added + state
        total[part] = jnp.zeros((16, 128), jnp.float32)
        total[part, :, 0:EX] = added


def fourth_kernel(
    slabs, groups, fields, before, far, passed, near, drive, renewed, total, table,
    out, new_states, middle, after, sums
):
    low, high = low_and_high(
        [near[0:16, :], near[16:32, :]], far_exterior(slabs, groups, far, passed, ROWS)
    )
    for f in (0, 1, 3, 4):
        for k in range(4):
            here = slice(16 * k, 16 * k + 16)
            middle[f, here, :] = before[f, here, :] + z_update(f, k, low, high)
    for f in (2, 5):
        middle[f] = before[f]
    for f, part, sign in ((2, 0, 2.0), (3, 0, -2.0), (0, 1, 2.0), (5, 1, 2.0)):
        for k in range(4):
            rows = drive[part, 4 * k : 4 * k + 4, :]
            added = jnp.concatenate([sign * HIGH_WEIGHT[j] * rows for j in range(4)], axis=0)
            here = slice(16 * k, 16 * k + 16)
            middle[f, here, LAYER - 128 : LAYER] = middle[f, here, LAYER - 128 : LAYER] + added
    later = currents(middle)
    resist = table[2 * POLES : 2 * POLES + 1, 0:EX]
    sums[...] = jnp.zeros_like(sums)
    for part in range(2):
        now = later[part][:, 0:EX]
        for pole in range(POLES):
            decay = table[pole : pole + 1, 0:EX]
            gain = table[POLES + pole : POLES + pole + 1, 0:EX]
            new_states[pole, part] = decay * renewed[pole, part] + gain * now
        sums[part, :, 0:EX] = resist * now + total[part, :, 0:EX]
    voltage = [at_faces(sums[part]) for part in range(2)]
    update(middle, middle, after, voltage, "xyz")
    for f in range(6):
        out[f] = 0.5 * fields[f] + 0.5 * after[f]


def fifth_kernel(slabs, groups, before, near, far, ends, first_far, out, held, sems):
    copies = []
    for f in (2, 5):
        copies.append(pltpu.make_async_copy(before.at[f], out.at[f], sems.at[f]))
        copies[-1].start()
    device = lax.axis_index("slab") * groups + lax.axis_index("patch")
    outside = (device == 0) | (device == slabs * groups - 1)
    share = jnp.where(outside, 2.0 * HIGH_WEIGHT[0], 0.0)
    beside = []
    for which in range(2):
        here = slice(16 * which, 16 * which + 16)
        beside.append(near[here, :] + share * first_far[here, :])
    low, high = low_and_high(beside, far_exterior(slabs, groups, far, ends, 0))
    low = [0.5 * v for v in low]
    high = [0.5 * v for v in high]
    for slot, f in enumerate((0, 1, 3, 4)):
        for k in range(4):
            here = slice(16 * k, 16 * k + 16)
            held[slot, here, :] = before[f, here, :] + z_update(f, k, low, high)
        copies.append(pltpu.make_async_copy(held.at[slot], out.at[f], sems.at[f]))
        copies[-1].start()
    for copy in copies:
        copy.wait()


def in_vmem(*arrays):
    return tuple(pltpu.with_memory_space_constraint(a, pltpu.VMEM) for a in arrays)


def on_device(slabs, groups, fields, pole_state, pole_decay, pole_gain, surface_resistance, face_owner):
    f32 = jnp.float32
    crossing = crossing_pairs(slabs, groups)
    ending = end_pairs(slabs, groups)

    def within(message, flip):
        pairs = [
            (g * groups + p, g * groups + (p ^ flip)) for g in range(slabs) for p in range(groups)
        ]
        return lax.ppermute(message, AXES, pairs)

    owner = face_owner.reshape(1, -1)
    width = fields.shape[-1]
    faces_only = pltpu.VMEM((ROWS, width), f32)
    block = pltpu.VMEM(fields.shape, f32)
    per_face = pltpu.VMEM((2, 16, 128), f32)
    (fields_v,) = in_vmem(fields)
    first2, own, first1, names = pl.pallas_call(
        first_kernel,
        out_shape=(
            faces_only,
            pltpu.VMEM((8, 128), f32),
            pltpu.VMEM((MESSAGE, width), f32),
            pltpu.VMEM(owner.shape, owner.dtype),
        ),
        in_specs=[HB] * 5,
        out_specs=[VM] * 4,
        scratch_shapes=[
            pltpu.VMEM((2, 4, 16, width), f32),
            pltpu.VMEM((1, POLES), f32),
            pltpu.VMEM((1, POLES), f32),
            pltpu.SMEM((1,), f32),
            pltpu.SemaphoreType.DMA((8,)),
        ],
        name="send_first",
    )(fields, pole_decay, pole_gain, surface_resistance, owner)
    near = within(first1, 1)
    partial, current, summed, states_v = pl.pallas_call(
            second_kernel,
            out_shape=(
                block,
                per_face,
                per_face,
                pltpu.VMEM(pole_state.shape, f32),
            ),
            in_specs=[VM, HB],
            out_specs=[VM] * 4,
            scratch_shapes=[pltpu.SemaphoreType.DMA],
            name="local_first",
        )(fields_v, pole_state)

    known, held, others = [own[0:3]], [(0, 0, 0)], []
    for r in range(1, groups.bit_length()):
        flip = (1 << r) - 1
        if r == 1:
            held.append((1, 1, ROWS))
            known.append(near[ROWS : ROWS + 3, 0:128])
            continue
        sent = jnp.concatenate(known, axis=0)
        sent = jnp.pad(sent, ((0, -sent.shape[0] % 8), (0, 0)))
        sent, first2, summed = lax.optimization_barrier((sent, first2, summed))
        others.append(within(sent, flip))
        for k in range(len(known)):
            held.append((held[k][0] ^ flip, r, 3 * k))
            known.append(others[-1][3 * k : 3 * k + 3])
    far = lax.ppermute(first2, AXES, crossing)

    (partial,) = in_vmem(partial)
    before = pl.pallas_call(
        upright_kernel,
        out_shape=block,
        in_specs=[VM] * 2,
        out_specs=VM,
        cost_estimate=COVER,
        name="local_z",
    )(fields_v, partial)
    own, names, near, *others = in_vmem(own, names, near, *others)
    before, current, summed, states_v = in_vmem(before, current, summed, states_v)
    second2, second3, drive = pl.pallas_call(
        functools.partial(third_kernel, held),
        out_shape=(faces_only, faces_only, per_face),
        in_specs=[VM] * (6 + len(others)),
        out_specs=[VM] * 3,
        name="send_far",
    )(before, current, summed, names, own, near, *others)
    later_far = lax.ppermute(second2, AXES, crossing)

    far, drive = in_vmem(far, drive)
    second1 = pl.pallas_call(
        functools.partial(near_kernel, slabs, groups),
        out_shape=pltpu.VMEM((2 * ROWS, width), f32),
        in_specs=[VM] * 3,
        out_specs=VM,
        name="send_near",
    )(before, drive, far)
    second1, second3 = lax.optimization_barrier((second1, second3))
    later_near = within(second1, 1)
    ends = lax.ppermute(second3, AXES, ending)
    later_near, later_far, ends = in_vmem(later_near, later_far, ends)

    renewed, total, table = pl.pallas_call(
        functools.partial(poles_kernel, held),
        out_shape=(pltpu.VMEM(pole_state.shape, f32), per_face, pltpu.VMEM((32, 128), f32)),
        in_specs=[VM] * (5 + len(others)),
        out_specs=[VM] * 3,
        cost_estimate=COVER,
        name="poles",
    )(states_v, current, names, own, near, *others)
    almost, advanced_states = pl.pallas_call(
        functools.partial(fourth_kernel, slabs, groups),
        out_shape=(block, jax.ShapeDtypeStruct(pole_state.shape, f32)),
        in_specs=[VM] * 9,
        out_specs=[VM] * 2,
        scratch_shapes=[
            pltpu.VMEM(fields.shape, f32),
            pltpu.VMEM(fields.shape, f32),
            per_face,
        ],
        cost_estimate=COVER,
        name="local_second",
    )(fields_v, before, far, later_near, near, drive, *in_vmem(renewed, total, table))

    advanced = pl.pallas_call(
        functools.partial(fifth_kernel, slabs, groups),
        out_shape=jax.ShapeDtypeStruct(fields.shape, f32),
        in_specs=[VM] * 5,
        out_specs=HB,
        scratch_shapes=[pltpu.VMEM((4, 64, width), f32), pltpu.SemaphoreType.DMA((6,))],
        name="finish",
    )(*in_vmem(almost), later_near, later_far, ends, far)
    return advanced, advanced_states


def solution(mesh):
    return jax.shard_map(
        functools.partial(on_device, mesh.shape["slab"], mesh.shape["patch"]),
        mesh=mesh,
        in_specs=(
            P(None, None, ("slab", "patch")),
            P(None, None, None, ("slab", "patch")),
            P(("slab", "patch"), None),
            P(("slab", "patch"), None),
            P(("slab", "patch")),
            P(("slab", "patch"), None),
        ),
        out_specs=(P(None, None, ("slab", "patch")), P(None, None, None, ("slab", "patch"))),
        check_vma=False,
    )
```

time: 14.6 us -> 15.1 us (1.034)
  starting transfers between devices: 5.06 us -> 5.71 us
  Pallas kernels: 4.49 us -> 4.25 us
    ppermute x1, starting transfers between devices: 2.61 us -> 0.06 us  [on_device(): far = lax.ppermute(first2, AXES, crossing)]
    ppermute x3, starting transfers between devices: 1.74 us -> 3.79 us  [within(): return lax.ppermute(message, AXES, pairs)]
    ppermute x3, waiting for transfers between devices: 0.01 us -> 1.92 us  [within(): return lax.ppermute(message, AXES, pairs)]
    ppermute x2 -> x1, waiting for transfers between devices: 3.45 us -> 1.64 us  [on_device(): ends = lax.ppermute(second3, AXES, ending)]
    ppermute x1, starting transfers between devices: 0.15 us -> 1.79 us  [on_device(): later_far = lax.ppermute(second2, AXES, crossing)]
    pallas_call x1, Pallas kernels: 1.66 us -> 0.95 us  [on_device(): pl.pallas_call(second_kernel, out_shape=(block, per_face, per_face, pltpu...]
    ppermute x2 -> x1, starting transfers between devices: 0.56 us -> 0.06 us  [on_device(): ends = lax.ppermute(second3, AXES, ending)]
    pallas_call x2 -> x5, Pallas kernels: 1.14 us -> 1.6 us  [the longest x1 1.07 us: on_device(): pl.pallas_call(functools.partial(fourth_kernel, slabs, groups), out_shape...]
  transfers between devices with their start and end apart: 7 -> 6, of which waited for: 2 -> 4; matrix products, arithmetic and copies ran while one was open for 0% -> 0% of each run, Pallas kernels for 18% -> 17%
where the time goes in v4:
time: 15.1 us; the launch traced here: 14.9 us
  starting transfers between devices  5.71 us (38%)
  Pallas kernels  4.25 us (28%)
  waiting for transfers between devices  3.57 us (24%)
  between operations  1.38 us (9%)
    ppermute x3, starting transfers between devices, within(): return lax.ppermute(message, AXES, pairs)  3.79 us
    ppermute x3, waiting for transfers between devices, within(): return lax.ppermute(message, AXES, pairs)  1.92 us
    ppermute x1, starting transfers between devices, on_device(): later_far = lax.ppermute(second2, AXES, crossing)  1.79 us
    ppermute x1, waiting for transfers between devices, on_device(): ends = lax.ppermute(second3, AXES, ending)  1.64 us
    pallas_call x1, Pallas kernels, on_device(): pl.pallas_call(functools.partial(fourth_kernel, slabs, groups), out_shape...  1.07 us
    pallas_call x1, Pallas kernels, on_device(): pl.pallas_call(second_kernel, out_shape=(block, per_face, per_face, pltpu...  0.95 us
    pallas_call x1, Pallas kernels, on_device(): pl.pallas_call(first_kernel, out_shape=(faces_only, pltpu.VMEM((8, 128),...  0.91 us
    pallas_call x1, Pallas kernels, on_device(): pl.pallas_call(functools.partial(fifth_kernel, slabs, groups), out_shape=...  0.79 us
  transfers between devices with their start and end apart: 6, of which 4 were waited for; matrix products, arithmetic and copies ran while one was open for 0% of the time, Pallas kernels for 17%

profile of v4, /device:TPU:1, one launch (start us, length us, event | category | flops | bytes accessed | tf_op | source)
XLA Modules:
  0.0 14.9 jit_solution(10353299225877809515)
XLA Ops:
  0.6 0.0 copy-start
  1.3 0.9 %send_first.1 = (f32[32,256]{1,0:T(8,128)S(1)}, f32[8,128]{1,0:T(8,128)S(1)}, f32[40,256]{1,0:T(8,128)S(1)}, s32[1,16]{1,0:T(1,128)S(1)}) custom-call(f32[6,64,256]{2,1,0:T(8,128)} %fields.7, f32[1,12]{1,0:T(1,128)} %decay.1, f32[1,12]{1,0:T(1,128)} %gain.1, f32[1]{0:T(128)S(6)} %copy.8.resist, s32[1,16]{1,0:T(1,128)} %bitcast.1), custom_call_target="tpu_custom_call" | custom-call | tf_op jit(solution)/shard_map/send_first/pallas_call | solution.py:487
  2.3 0.1 collective-permute-start
  2.4 0.0 copy-done
  2.4 1.0 %local_first.1 = (f32[6,64,256]{2,1,0:T(8,128)S(1)}, f32[2,16,128]{2,1,0:T(8,128)S(1)}, f32[2,16,128]{2,1,0:T(8,128)S(1)}, f32[12,2,16,16]{3,2,1,0:T(8,128)S(1)}) custom-call(f32[6,64,256]{2,1,0:T(8,128)S(1)} %copy-done, f32[12,2,16,16]{3,2,1,0:T(8,128)} %states_h.1), custom_call_target="tpu_custom_call" | custom-call | tf_op jit(solution)/shard_map/local_first/pallas_call | solution.py:507
  3.3 0.2 %collective-permute-done.near = f32[40,256]{1,0:T(8,128)S(1)} collective-permute-done((f32[40,256]{1,0:T(8,128)S(1)}, f32[40,256]{1,0:T(8,128)S(1)}, u32[]{:S(2)}, u32[]{:S(2)}) %collective-permute-start) | collective-permute-done | bytes 40992 | tf_op jit(solution)/shard_map/ppermute | solution.py:479
  3.6 2.7 %collective-permute-start.2 = (f32[8,128]{1,0:T(8,128)S(1)}, f32[8,128]{1,0:T(8,128)S(1)}, u32[]{:S(2)}, u32[]{:S(2)}) collective-permute-start(f32[8,128]{1,0:T(8,128)S(1)} %select_maximum_fusion), channel_id=1, source_target_pairs={{0,3},{1,2},{2,1},{3,0},{4,7},{5,6},{6,5},{7,4},{8,11},{9,10},{10,... | collective-permute-start | bytes 12296 | tf_op jit(solution)/shard_map/ppermute | solution.py:479
  6.2 0.1 collective-permute-start.1
  6.3 0.1 local_z.1.before
  6.4 1.1 %collective-permute-done.2.refs_0_ = f32[8,128]{1,0:T(8,128)S(1)} collective-permute-done((f32[8,128]{1,0:T(8,128)S(1)}, f32[8,128]{1,0:T(8,128)S(1)}, u32[]{:S(2)}, u32[]{:S(2)}) %collective-permute-start.2) | collective-permute-done | bytes 4128 | tf_op jit(solution)/shard_map/ppermute | solution.py:479
  7.5 0.2 %send_far.1 = (f32[32,256]{1,0:T(8,128)S(1)}, f32[32,256]{1,0:T(8,128)S(1)}, f32[2,16,128]{2,1,0:T(8,128)S(1)}) custom-call(f32[6,64,256]{2,1,0:T(8,128)S(1)} %local_z.1.before, f32[2,16,128]{2,1,0:T(8,128)S(1)} %get-tuple-element.29.current, f32[2,16,128]{2,1,0:T(8,128)S(1)} %get-tuple-element.30.summed, s32[1,16]{1,0:T(1,128)S(1)} %get-tuple-element.31.owner, ...), custom_call_target="tpu_custom_call" | custom-call | tf_op jit(solution)/shard_map/send_far/pallas_call | solution.py:548
  7.7 1.8 %collective-permute-start.4 = (f32[32,256]{1,0:T(8,128)S(1)}, f32[32,256]{1,0:T(8,128)S(1)}, u32[]{:S(2)}, u32[]{:S(2)}) collective-permute-start(f32[32,256]{1,0:T(8,128)S(1)} %get-tuple-element.41), channel_id=1, source_target_pairs={{3,4},{5,6},{7,8},{9,10},{11,12},{13,14},{15,16},{17,18},{19,20},{... | collective-permute-start | bytes 98312 | tf_op jit(solution)/shard_map/ppermute | solution.py:555
  9.5 0.0 collective-permute-done.1.far.first_far
  9.5 1.0 %collective-permute-start.3 = (f32[64,256]{1,0:T(8,128)S(1)}, f32[64,256]{1,0:T(8,128)S(1)}, u32[]{:S(2)}, u32[]{:S(2)}) collective-permute-start(f32[64,256]{1,0:T(8,128)S(1)} %send_near.1), channel_id=1, source_target_pairs={{0,1},{1,0},{2,3},{3,2},{4,5},{5,4},{6,7},{7,6},{8,9},{9,8},{10,11... | collective-permute-start | bytes 196616 | tf_op jit(solution)/shard_map/ppermute | solution.py:479
  10.5 0.2 %poles.1 = (f32[12,2,16,16]{3,2,1,0:T(8,128)S(1)}, f32[2,16,128]{2,1,0:T(8,128)S(1)}, f32[32,128]{1,0:T(8,128)S(1)}) custom-call(f32[12,2,16,16]{3,2,1,0:T(8,128)S(1)} %get-tuple-element.36.states, f32[2,16,128]{2,1,0:T(8,128)S(1)} %get-tuple-element.29.current, s32[1,16]{1,0:T(1,128)S(1)} %get-tuple-element.31.owner, f32[8,128]{1,0:T(8,128)S(1)} %get-tuple-element.24.own, ...), custom_call_target="tpu_custom_call" | custom-call | flops 2000000000 | tf_op jit(solution)/shard_map/poles/pallas_call | solution.py:570
  10.7 0.1 collective-permute-start.5
  10.8 0.6 %collective-permute-done.3.passed.near = f32[64,256]{1,0:T(8,128)S(1)} collective-permute-done((f32[64,256]{1,0:T(8,128)S(1)}, f32[64,256]{1,0:T(8,128)S(1)}, u32[]{:S(2)}, u32[]{:S(2)}) %collective-permute-start.3) | collective-permute-done | bytes 65568 | tf_op jit(solution)/shard_map/ppermute | solution.py:479
  11.4 1.1 %local_second.1 = (f32[6,64,256]{2,1,0:T(8,128)S(1)}, f32[12,2,16,16]{3,2,1,0:T(8,128)}) custom-call(f32[6,64,256]{2,1,0:T(8,128)S(1)} %copy-done, f32[6,64,256]{2,1,0:T(8,128)S(1)} %local_z.1.before, f32[32,256]{1,0:T(8,128)S(1)} %collective-permute-done.1.far.first_far, f32[64,256]{1,0:T(8,128)S(1)} %collective-permute-done.3.passed.near, ...), custom_call_target="tpu_custom_call" | custom-call | flops 2000000000 | tf_op jit(solution)/shard_map/local_second/pallas_call | solution.py:578
  12.5 0.0 collective-permute-done.4.far
  12.5 1.6 %collective-permute-done.5.ends = f32[32,256]{1,0:T(8,128)S(1)} collective-permute-done((f32[32,256]{1,0:T(8,128)S(1)}, f32[32,256]{1,0:T(8,128)S(1)}, u32[]{:S(2)}, u32[]{:S(2)}) %collective-permute-start.5) | collective-permute-done | bytes 32800 | tf_op jit(solution)/shard_map/ppermute | solution.py:567
  14.1 0.8 %finish.1 = f32[6,64,256]{2,1,0:T(8,128)} custom-call(f32[6,64,256]{2,1,0:T(8,128)S(1)} %get-tuple-element.40.before, f32[64,256]{1,0:T(8,128)S(1)} %collective-permute-done.3.passed.near, f32[32,256]{1,0:T(8,128)S(1)} %collective-permute-done.4.far, f32[32,256]{1,0:T(8,128)S(1)} %collective-permute-done.5.ends, ...), custom_call_target="tpu_custom_call" | custom-call | tf_op jit(solution)/shard_map/finish/pallas_call | solution.py:592
  (4 shorter events, 0.0 us)
Async XLA Ops:
  0.6 1.7 %copy-start = (f32[6,64,256]{2,1,0:T(8,128)S(1)}, f32[6,64,256]{2,1,0:T(8,128)}, u32[]{:S(2)}) copy-start(f32[6,64,256]{2,1,0:T(8,128)} %fields.7) | copy-start | bytes 1179652
  2.3 1.3 %collective-permute-start = (f32[40,256]{1,0:T(8,128)S(1)}, f32[40,256]{1,0:T(8,128)S(1)}, u32[]{:S(2)}, u32[]{:S(2)}) collective-permute-start(f32[40,256]{1,0:T(8,128)S(1)} %get-tuple-element.25), channel_id=1, source_target_pairs={{0,1},{1,0},{2,3},{3,2},{4,5},{5,4},{6,7},{7,6},{8,9},{9,8},{10,11... | collective-permute-start | bytes 122888 | tf_op jit(solution)/shard_map/ppermute | solution.py:479
  3.6 4.0 %collective-permute-start.2 = (f32[8,128]{1,0:T(8,128)S(1)}, f32[8,128]{1,0:T(8,128)S(1)}, u32[]{:S(2)}, u32[]{:S(2)}) collective-permute-start(f32[8,128]{1,0:T(8,128)S(1)} %select_maximum_fusion), channel_id=1, source_target_pairs={{0,3},{1,2},{2,1},{3,0},{4,7},{5,6},{6,5},{7,4},{8,11},{9,10},{10,... | collective-permute-start | bytes 12296 | tf_op jit(solution)/shard_map/ppermute | solution.py:479
  6.2 3.3 %collective-permute-start.1 = (f32[32,256]{1,0:T(8,128)S(1)}, f32[32,256]{1,0:T(8,128)S(1)}, u32[]{:S(2)}, u32[]{:S(2)}) collective-permute-start(f32[32,256]{1,0:T(8,128)S(1)} %get-tuple-element.28), channel_id=1, source_target_pairs={{3,4},{5,6},{7,8},{9,10},{11,12},{13,14},{15,16},{17,18},{19,20},{... | collective-permute-start | bytes 98312 | tf_op jit(solution)/shard_map/ppermute | solution.py:535
  7.7 4.8 %collective-permute-start.4 = (f32[32,256]{1,0:T(8,128)S(1)}, f32[32,256]{1,0:T(8,128)S(1)}, u32[]{:S(2)}, u32[]{:S(2)}) collective-permute-start(f32[32,256]{1,0:T(8,128)S(1)} %get-tuple-element.41), channel_id=1, source_target_pairs={{3,4},{5,6},{7,8},{9,10},{11,12},{13,14},{15,16},{17,18},{19,20},{... | collective-permute-start | bytes 98312 | tf_op jit(solution)/shard_map/ppermute | solution.py:555
  9.5 1.9 %collective-permute-start.3 = (f32[64,256]{1,0:T(8,128)S(1)}, f32[64,256]{1,0:T(8,128)S(1)}, u32[]{:S(2)}, u32[]{:S(2)}) collective-permute-start(f32[64,256]{1,0:T(8,128)S(1)} %send_near.1), channel_id=1, source_target_pairs={{0,1},{1,0},{2,3},{3,2},{4,5},{5,4},{6,7},{7,6},{8,9},{9,8},{10,11... | collective-permute-start | bytes 196616 | tf_op jit(solution)/shard_map/ppermute | solution.py:479
  10.7 3.4 %collective-permute-start.5 = (f32[32,256]{1,0:T(8,128)S(1)}, f32[32,256]{1,0:T(8,128)S(1)}, u32[]{:S(2)}, u32[]{:S(2)}) collective-permute-start(f32[32,256]{1,0:T(8,128)S(1)} %get-tuple-element.42), channel_id=1, source_target_pairs={{4,5},{5,4},{6,7},{7,6},{8,9},{9,8},{10,11},{11,10},{12,13},{13,12... | collective-permute-start | bytes 98312 | tf_op jit(solution)/shard_map/ppermute | solution.py:567

commit v5 on v4

--- a/solution.py
+++ b/solution.py
@@ -71,18 +71,17 @@
 RISE, FALL, LOW_WEIGHT, HIGH_WEIGHT = build_tables()
 
 
-def crossing_pairs(slabs, groups):
+def crossing_pairs(slabs, groups, cycle):
     count = slabs * groups
     pairs = [(d, d + 1) for d in range(3, count - 3, 2)]
     pairs += [(d + 1, d) for d, _ in pairs]
-    cycle = ((0, 1), (1, 2), (2, 0))
     return pairs + list(cycle) + [(count - 1 - d, count - 1 - e) for d, e in cycle]
 
 
 def end_pairs(slabs, groups):
     count = slabs * groups
     pairs = [(d, d ^ 1) for d in range(4, count - 4)]
-    cycle = ((2, 1), (1, 0), (0, 3), (3, 2))
+    cycle = ((1, 2), (2, 3), (3, 0), (0, 1))
     return pairs + list(cycle) + [(count - 1 - d, count - 1 - e) for d, e in cycle]
 
 
@@ -279,10 +278,10 @@
         out[field] = partial[field]
 
 
-def far_exterior(slabs, groups, far_ref, ends_ref, start):
+def far_exterior(slabs, groups, far_ref, ends_ref, start, missing):
     device = lax.axis_index("slab") * groups + lax.axis_index("patch")
     count = slabs * groups
-    left_out = (device == 1) | (device == count - 2)
+    left_out = (device == missing) | (device == count - 1 - missing)
     outside = (device == 0) | (device == count - 1)
     found = []
     for which in range(2):
@@ -361,7 +360,7 @@
 
 
 def near_kernel(slabs, groups, before, drive, far, out1):
-    exterior = far_exterior(slabs, groups, far, None, 0)
+    exterior = far_exterior(slabs, groups, far, None, 0, 1)
     up = upper_message(before, drive, exterior)
     down = lower_message(before, drive, exterior)
     for which in range(2):
@@ -408,7 +407,7 @@
     out, new_states, middle, after, sums
 ):
     low, high = low_and_high(
-        [near[0:16, :], near[16:32, :]], far_exterior(slabs, groups, far, passed, ROWS)
+        [near[0:16, :], near[16:32, :]], far_exterior(slabs, groups, far, passed, ROWS, 1)
     )
     for f in (0, 1, 3, 4):
         for k in range(4):
@@ -438,7 +437,7 @@
         out[f] = 0.5 * fields[f] + 0.5 * after[f]
 
 
-def fifth_kernel(slabs, groups, before, near, far, ends, first_far, out, held, sems):
+def fifth_kernel(slabs, groups, before, near, ends, far, first_far, out, held, sems):
     copies = []
     for f in (2, 5):
         copies.append(pltpu.make_async_copy(before.at[f], out.at[f], sems.at[f]))
@@ -450,7 +449,7 @@
     for which in range(2):
         here = slice(16 * which, 16 * which + 16)
         beside.append(near[here, :] + share * first_far[here, :])
-    low, high = low_and_high(beside, far_exterior(slabs, groups, far, ends, 0))
+    low, high = low_and_high(beside, far_exterior(slabs, groups, far, ends, 0, 2))
     low = [0.5 * v for v in low]
     high = [0.5 * v for v in high]
     for slot, f in enumerate((0, 1, 3, 4)):
@@ -469,7 +468,8 @@
 
 def on_device(slabs, groups, fields, pole_state, pole_decay, pole_gain, surface_resistance, face_owner):
     f32 = jnp.float32
-    crossing = crossing_pairs(slabs, groups)
+    crossing = crossing_pairs(slabs, groups, ((0, 1), (1, 2), (2, 0)))
+    crossing_back = crossing_pairs(slabs, groups, ((0, 2), (2, 1), (1, 0)))
     ending = end_pairs(slabs, groups)
 
     def within(message, flip):
@@ -552,7 +552,7 @@
         out_specs=[VM] * 3,
         name="send_far",
     )(before, current, summed, names, own, near, *others)
-    later_far = lax.ppermute(second2, AXES, crossing)
+    later_far = lax.ppermute(second2, AXES, crossing_back)
 
     far, drive = in_vmem(far, drive)
     second1 = pl.pallas_call(
@@ -562,7 +562,6 @@
         out_specs=VM,
         name="send_near",
     )(before, drive, far)
-    second1, second3 = lax.optimization_barrier((second1, second3))
     later_near = within(second1, 1)
     ends = lax.ppermute(second3, AXES, ending)
     later_near, later_far, ends = in_vmem(later_near, later_far, ends)
@@ -596,7 +595,7 @@
         out_specs=HB,
         scratch_shapes=[pltpu.VMEM((4, 64, width), f32), pltpu.SemaphoreType.DMA((6,))],
         name="finish",
-    )(*in_vmem(almost), later_near, later_far, ends, far)
+    )(*in_vmem(almost), later_near, ends, later_far, far)
     return advanced, advanced_states
 
 

time: 15.1 us -> 13.9 us (0.921)
  the two profiles are of different devices: /device:TPU:1 before, /device:TPU:9 now
where the time goes in v5:
time: 13.9 us; the launch traced here: 13.7 us
  starting transfers between devices  6.16 us (44%)
  Pallas kernels  4.25 us (31%)
  waiting for transfers between devices  1.85 us (13%)
  between operations  1.4 us (10%)
    ppermute x3, starting transfers between devices, within(): return lax.ppermute(message, AXES, pairs)  3.75 us
    ppermute x3, waiting for transfers between devices, within(): return lax.ppermute(message, AXES, pairs)  1.84 us
    ppermute x1, starting transfers between devices, on_device(): later_far = lax.ppermute(second2, AXES, crossing_back)  1.71 us
    pallas_call x1, Pallas kernels, on_device(): pl.pallas_call(functools.partial(fourth_kernel, slabs, groups), out_shape...  1.07 us
    pallas_call x1, Pallas kernels, on_device(): pl.pallas_call(second_kernel, out_shape=(block, per_face, per_face, pltpu...  0.95 us
    pallas_call x1, Pallas kernels, on_device(): pl.pallas_call(first_kernel, out_shape=(faces_only, pltpu.VMEM((8, 128),...  0.91 us
    pallas_call x1, Pallas kernels, on_device(): pl.pallas_call(functools.partial(fifth_kernel, slabs, groups), out_shape=...  0.79 us
    ppermute x1, starting transfers between devices, on_device(): far = lax.ppermute(first2, AXES, crossing)  0.42 us
  transfers between devices with their start and end apart: 6, of which 2 were waited for; matrix products, arithmetic and copies ran while one was open for 0% of the time, Pallas kernels for 19%

profile of v5, /device:TPU:9, one launch (start us, length us, event | category | flops | bytes accessed | tf_op | source)
XLA Modules:
  0.0 13.7 jit_solution(15465559242562894023)
XLA Ops:
  0.6 0.0 copy-start
  1.3 0.9 %send_first.1 = (f32[32,256]{1,0:T(8,128)S(1)}, f32[8,128]{1,0:T(8,128)S(1)}, f32[40,256]{1,0:T(8,128)S(1)}, s32[1,16]{1,0:T(1,128)S(1)}) custom-call(f32[6,64,256]{2,1,0:T(8,128)} %fields.7, f32[1,12]{1,0:T(1,128)} %decay.1, f32[1,12]{1,0:T(1,128)} %gain.1, f32[1]{0:T(128)S(6)} %copy.8.resist, s32[1,16]{1,0:T(1,128)} %bitcast.1), custom_call_target="tpu_custom_call" | custom-call | tf_op jit(solution)/shard_map/send_first/pallas_call | solution.py:487
  2.3 0.7 %collective-permute-start = (f32[40,256]{1,0:T(8,128)S(1)}, f32[40,256]{1,0:T(8,128)S(1)}, u32[]{:S(2)}, u32[]{:S(2)}) collective-permute-start(f32[40,256]{1,0:T(8,128)S(1)} %get-tuple-element.23), channel_id=1, source_target_pairs={{0,1},{1,0},{2,3},{3,2},{4,5},{5,4},{6,7},{7,6},{8,9},{9,8},{10,11... | collective-permute-start | bytes 122888 | tf_op jit(solution)/shard_map/ppermute | solution.py:479
  3.0 0.0 copy-done
  3.0 1.0 %local_first.1 = (f32[6,64,256]{2,1,0:T(8,128)S(1)}, f32[2,16,128]{2,1,0:T(8,128)S(1)}, f32[2,16,128]{2,1,0:T(8,128)S(1)}, f32[12,2,16,16]{3,2,1,0:T(8,128)S(1)}) custom-call(f32[6,64,256]{2,1,0:T(8,128)S(1)} %copy-done, f32[12,2,16,16]{3,2,1,0:T(8,128)} %states_h.1), custom_call_target="tpu_custom_call" | custom-call | tf_op jit(solution)/shard_map/local_first/pallas_call | solution.py:507
  4.0 0.0 collective-permute-done.near
  4.0 1.4 %collective-permute-start.2 = (f32[8,128]{1,0:T(8,128)S(1)}, f32[8,128]{1,0:T(8,128)S(1)}, u32[]{:S(2)}, u32[]{:S(2)}) collective-permute-start(f32[8,128]{1,0:T(8,128)S(1)} %select_maximum_fusion), channel_id=1, source_target_pairs={{0,3},{1,2},{2,1},{3,0},{4,7},{5,6},{6,5},{7,4},{8,11},{9,10},{10,... | collective-permute-start | bytes 12296 | tf_op jit(solution)/shard_map/ppermute | solution.py:479
  5.4 0.4 %collective-permute-start.1 = (f32[32,256]{1,0:T(8,128)S(1)}, f32[32,256]{1,0:T(8,128)S(1)}, u32[]{:S(2)}, u32[]{:S(2)}) collective-permute-start(f32[32,256]{1,0:T(8,128)S(1)} %get-tuple-element.26), channel_id=1, source_target_pairs={{3,4},{5,6},{7,8},{9,10},{11,12},{13,14},{15,16},{17,18},{19,20},{... | collective-permute-start | bytes 98312 | tf_op jit(solution)/shard_map/ppermute | solution.py:535
  5.8 0.1 local_z.1.before
  5.9 1.2 %collective-permute-done.2.refs_0_ = f32[8,128]{1,0:T(8,128)S(1)} collective-permute-done((f32[8,128]{1,0:T(8,128)S(1)}, f32[8,128]{1,0:T(8,128)S(1)}, u32[]{:S(2)}, u32[]{:S(2)}) %collective-permute-start.2) | collective-permute-done | bytes 4128 | tf_op jit(solution)/shard_map/ppermute | solution.py:479
  7.1 0.2 %send_far.1 = (f32[32,256]{1,0:T(8,128)S(1)}, f32[32,256]{1,0:T(8,128)S(1)}, f32[2,16,128]{2,1,0:T(8,128)S(1)}) custom-call(f32[6,64,256]{2,1,0:T(8,128)S(1)} %local_z.1.before, f32[2,16,128]{2,1,0:T(8,128)S(1)} %get-tuple-element.27.current, f32[2,16,128]{2,1,0:T(8,128)S(1)} %get-tuple-element.28.summed, s32[1,16]{1,0:T(1,128)S(1)} %get-tuple-element.29.owner, ...), custom_call_target="tpu_custom_call" | custom-call | tf_op jit(solution)/shard_map/send_far/pallas_call | solution.py:548
  7.3 0.3 %collective-permute-start.4 = (f32[32,256]{1,0:T(8,128)S(1)}, f32[32,256]{1,0:T(8,128)S(1)}, u32[]{:S(2)}, u32[]{:S(2)}) collective-permute-start(f32[32,256]{1,0:T(8,128)S(1)} %get-tuple-element.37), channel_id=1, source_target_pairs={{4,5},{5,4},{6,7},{7,6},{8,9},{9,8},{10,11},{11,10},{12,13},{13,12... | collective-permute-start | bytes 98312 | tf_op jit(solution)/shard_map/ppermute | solution.py:566
  7.5 1.7 %collective-permute-start.5 = (f32[32,256]{1,0:T(8,128)S(1)}, f32[32,256]{1,0:T(8,128)S(1)}, u32[]{:S(2)}, u32[]{:S(2)}) collective-permute-start(f32[32,256]{1,0:T(8,128)S(1)} %get-tuple-element.38), channel_id=1, source_target_pairs={{3,4},{5,6},{7,8},{9,10},{11,12},{13,14},{15,16},{17,18},{19,20},{... | collective-permute-start | bytes 98312 | tf_op jit(solution)/shard_map/ppermute | solution.py:555
  9.3 0.0 collective-permute-done.1.far.first_far
  9.3 1.6 %collective-permute-start.3 = (f32[64,256]{1,0:T(8,128)S(1)}, f32[64,256]{1,0:T(8,128)S(1)}, u32[]{:S(2)}, u32[]{:S(2)}) collective-permute-start(f32[64,256]{1,0:T(8,128)S(1)} %send_near.1), channel_id=1, source_target_pairs={{0,1},{1,0},{2,3},{3,2},{4,5},{5,4},{6,7},{7,6},{8,9},{9,8},{10,11... | collective-permute-start | bytes 196616 | tf_op jit(solution)/shard_map/ppermute | solution.py:479
  10.9 0.2 %poles.1 = (f32[12,2,16,16]{3,2,1,0:T(8,128)S(1)}, f32[2,16,128]{2,1,0:T(8,128)S(1)}, f32[32,128]{1,0:T(8,128)S(1)}) custom-call(f32[12,2,16,16]{3,2,1,0:T(8,128)S(1)} %get-tuple-element.32.states, f32[2,16,128]{2,1,0:T(8,128)S(1)} %get-tuple-element.27.current, s32[1,16]{1,0:T(1,128)S(1)} %get-tuple-element.29.owner, f32[8,128]{1,0:T(8,128)S(1)} %get-tuple-element.22.own, ...), custom_call_target="tpu_custom_call" | custom-call | flops 2000000000 | tf_op jit(solution)/shard_map/poles/pallas_call | solution.py:569
  11.1 0.7 %collective-permute-done.3.passed.near = f32[64,256]{1,0:T(8,128)S(1)} collective-permute-done((f32[64,256]{1,0:T(8,128)S(1)}, f32[64,256]{1,0:T(8,128)S(1)}, u32[]{:S(2)}, u32[]{:S(2)}) %collective-permute-start.3) | collective-permute-done | bytes 65568 | tf_op jit(solution)/shard_map/ppermute | solution.py:479
  11.8 1.1 %local_second.1 = (f32[6,64,256]{2,1,0:T(8,128)S(1)}, f32[12,2,16,16]{3,2,1,0:T(8,128)}) custom-call(f32[6,64,256]{2,1,0:T(8,128)S(1)} %copy-done, f32[6,64,256]{2,1,0:T(8,128)S(1)} %local_z.1.before, f32[32,256]{1,0:T(8,128)S(1)} %collective-permute-done.1.far.first_far, f32[64,256]{1,0:T(8,128)S(1)} %collective-permute-done.3.passed.near, ...), custom_call_target="tpu_custom_call" | custom-call | flops 2000000000 | tf_op jit(solution)/shard_map/local_second/pallas_call | solution.py:577
  12.9 0.0 collective-permute-done.4.ends
  12.9 0.0 collective-permute-done.5.far
  12.9 0.8 %finish.1 = f32[6,64,256]{2,1,0:T(8,128)} custom-call(f32[6,64,256]{2,1,0:T(8,128)S(1)} %get-tuple-element.36.before, f32[64,256]{1,0:T(8,128)S(1)} %collective-permute-done.3.passed.near, f32[32,256]{1,0:T(8,128)S(1)} %collective-permute-done.4.ends, f32[32,256]{1,0:T(8,128)S(1)} %collective-permute-done.5.far, ...), custom_call_target="tpu_custom_call" | custom-call | tf_op jit(solution)/shard_map/finish/pallas_call | solution.py:591
  (4 shorter events, 0.0 us)
Async XLA Ops:
  0.6 2.4 %copy-start = (f32[6,64,256]{2,1,0:T(8,128)S(1)}, f32[6,64,256]{2,1,0:T(8,128)}, u32[]{:S(2)}) copy-start(f32[6,64,256]{2,1,0:T(8,128)} %fields.7) | copy-start | bytes 1179652
  2.3 1.7 %collective-permute-start = (f32[40,256]{1,0:T(8,128)S(1)}, f32[40,256]{1,0:T(8,128)S(1)}, u32[]{:S(2)}, u32[]{:S(2)}) collective-permute-start(f32[40,256]{1,0:T(8,128)S(1)} %get-tuple-element.23), channel_id=1, source_target_pairs={{0,1},{1,0},{2,3},{3,2},{4,5},{5,4},{6,7},{7,6},{8,9},{9,8},{10,11... | collective-permute-start | bytes 122888 | tf_op jit(solution)/shard_map/ppermute | solution.py:479
  4.0 3.1 %collective-permute-start.2 = (f32[8,128]{1,0:T(8,128)S(1)}, f32[8,128]{1,0:T(8,128)S(1)}, u32[]{:S(2)}, u32[]{:S(2)}) collective-permute-start(f32[8,128]{1,0:T(8,128)S(1)} %select_maximum_fusion), channel_id=1, source_target_pairs={{0,3},{1,2},{2,1},{3,0},{4,7},{5,6},{6,5},{7,4},{8,11},{9,10},{10,... | collective-permute-start | bytes 12296 | tf_op jit(solution)/shard_map/ppermute | solution.py:479
  5.4 3.9 %collective-permute-start.1 = (f32[32,256]{1,0:T(8,128)S(1)}, f32[32,256]{1,0:T(8,128)S(1)}, u32[]{:S(2)}, u32[]{:S(2)}) collective-permute-start(f32[32,256]{1,0:T(8,128)S(1)} %get-tuple-element.26), channel_id=1, source_target_pairs={{3,4},{5,6},{7,8},{9,10},{11,12},{13,14},{15,16},{17,18},{19,20},{... | collective-permute-start | bytes 98312 | tf_op jit(solution)/shard_map/ppermute | solution.py:535
  7.3 5.6 %collective-permute-start.4 = (f32[32,256]{1,0:T(8,128)S(1)}, f32[32,256]{1,0:T(8,128)S(1)}, u32[]{:S(2)}, u32[]{:S(2)}) collective-permute-start(f32[32,256]{1,0:T(8,128)S(1)} %get-tuple-element.37), channel_id=1, source_target_pairs={{4,5},{5,4},{6,7},{7,6},{8,9},{9,8},{10,11},{11,10},{12,13},{13,12... | collective-permute-start | bytes 98312 | tf_op jit(solution)/shard_map/ppermute | solution.py:566
  7.5 5.3 %collective-permute-start.5 = (f32[32,256]{1,0:T(8,128)S(1)}, f32[32,256]{1,0:T(8,128)S(1)}, u32[]{:S(2)}, u32[]{:S(2)}) collective-permute-start(f32[32,256]{1,0:T(8,128)S(1)} %get-tuple-element.38), channel_id=1, source_target_pairs={{3,4},{5,6},{7,8},{9,10},{11,12},{13,14},{15,16},{17,18},{19,20},{... | collective-permute-start | bytes 98312 | tf_op jit(solution)/shard_map/ppermute | solution.py:555
  9.3 2.5 %collective-permute-start.3 = (f32[64,256]{1,0:T(8,128)S(1)}, f32[64,256]{1,0:T(8,128)S(1)}, u32[]{:S(2)}, u32[]{:S(2)}) collective-permute-start(f32[64,256]{1,0:T(8,128)S(1)} %send_near.1), channel_id=1, source_target_pairs={{0,1},{1,0},{2,3},{3,2},{4,5},{5,4},{6,7},{7,6},{8,9},{9,8},{10,11... | collective-permute-start | bytes 196616 | tf_op jit(solution)/shard_map/ppermute | solution.py:479

commit v6 on v4

--- a/solution.py
+++ b/solution.py
@@ -75,14 +75,14 @@
     count = slabs * groups
     pairs = [(d, d + 1) for d in range(3, count - 3, 2)]
     pairs += [(d + 1, d) for d, _ in pairs]
-    cycle = ((0, 1), (1, 2), (2, 0))
+    cycle = ((0, 2), (2, 1), (1, 0))
     return pairs + list(cycle) + [(count - 1 - d, count - 1 - e) for d, e in cycle]
 
 
 def end_pairs(slabs, groups):
     count = slabs * groups
     pairs = [(d, d ^ 1) for d in range(4, count - 4)]
-    cycle = ((2, 1), (1, 0), (0, 3), (3, 2))
+    cycle = ((1, 2), (2, 3), (3, 0), (0, 1))
     return pairs + list(cycle) + [(count - 1 - d, count - 1 - e) for d, e in cycle]
 
 
@@ -279,17 +279,21 @@
         out[field] = partial[field]
 
 
+def inside_kernel(slabs, groups, far, out):
+    device = lax.axis_index("slab") * groups + lax.axis_index("patch")
+    outside = (device == 0) | (device == slabs * groups - 1)
+    out[...] = jnp.where(outside, 0.0, far[...])
+
+
 def far_exterior(slabs, groups, far_ref, ends_ref, start):
     device = lax.axis_index("slab") * groups + lax.axis_index("patch")
     count = slabs * groups
-    left_out = (device == 1) | (device == count - 2)
+    left_out = (device == 2) | (device == count - 3)
     outside = (device == 0) | (device == count - 1)
     found = []
     for which in range(2):
         far = jnp.where(outside, 0.0, far_ref[16 * which : 16 * which + 16, :])
-        ends = 0.0
-        if ends_ref is not None:
-            ends = ends_ref[start + 16 * which : start + 16 * which + 16, :]
+        ends = ends_ref[start + 16 * which : start + 16 * which + 16, :]
         found.append(jnp.where(left_out, ends, far))
     return found
 
@@ -342,7 +346,7 @@
     )
 
 
-def third_kernel(held, before, current, summed, owner, own, near, *refs):
+def third_kernel(held, before, current, summed, owner, own, sent, near, *refs):
     others = refs[:-3]
     out2, out3, drive = refs[-3:]
     resist = face_parameter(owner[...], parameters(held, own, near, others), 2, 0)
@@ -357,17 +361,17 @@
         here = slice(16 * which, 16 * which + 16)
         far = jnp.where(is_even(), down[which], up[which])
         out2[here, :] = far
-        out3[here, :] = far
-
-
-def near_kernel(slabs, groups, before, drive, far, out1):
-    exterior = far_exterior(slabs, groups, far, None, 0)
+        out3[here, :] = sent[here, :]
+        out3[ROWS + 16 * which : ROWS + 16 * which + 16, :] = far
+
+
+def near_kernel(slabs, groups, before, drive, far, ends, out1):
+    exterior = far_exterior(slabs, groups, far, ends, 0)
     up = upper_message(before, drive, exterior)
     down = lower_message(before, drive, exterior)
     for which in range(2):
         here = slice(16 * which, 16 * which + 16)
         out1[here, :] = jnp.where(is_even(), up[which], down[which])
-    out1[ROWS : 2 * ROWS, :] = far[...]
 
 
 def z_update(field, k, low, high):
@@ -404,11 +408,11 @@
 
 
 def fourth_kernel(
-    slabs, groups, fields, before, far, passed, near, drive, renewed, total, table,
+    slabs, groups, fields, before, far, ends, near, drive, renewed, total, table,
     out, new_states, middle, after, sums
 ):
     low, high = low_and_high(
-        [near[0:16, :], near[16:32, :]], far_exterior(slabs, groups, far, passed, ROWS)
+        [near[0:16, :], near[16:32, :]], far_exterior(slabs, groups, far, ends, 0)
     )
     for f in (0, 1, 3, 4):
         for k in range(4):
@@ -438,19 +442,14 @@
         out[f] = 0.5 * fields[f] + 0.5 * after[f]
 
 
-def fifth_kernel(slabs, groups, before, near, far, ends, first_far, out, held, sems):
+def fifth_kernel(slabs, groups, before, near, far, ends, out, held, sems):
     copies = []
     for f in (2, 5):
         copies.append(pltpu.make_async_copy(before.at[f], out.at[f], sems.at[f]))
         copies[-1].start()
-    device = lax.axis_index("slab") * groups + lax.axis_index("patch")
-    outside = (device == 0) | (device == slabs * groups - 1)
-    share = jnp.where(outside, 2.0 * HIGH_WEIGHT[0], 0.0)
-    beside = []
-    for which in range(2):
-        here = slice(16 * which, 16 * which + 16)
-        beside.append(near[here, :] + share * first_far[here, :])
-    low, high = low_and_high(beside, far_exterior(slabs, groups, far, ends, 0))
+    low, high = low_and_high(
+        [near[0:16, :], near[16:32, :]], far_exterior(slabs, groups, far, ends, ROWS)
+    )
     low = [0.5 * v for v in low]
     high = [0.5 * v for v in high]
     for slot, f in enumerate((0, 1, 3, 4)):
@@ -543,29 +542,37 @@
         cost_estimate=COVER,
         name="local_z",
     )(fields_v, partial)
-    own, names, near, *others = in_vmem(own, names, near, *others)
+    own, names, first2, near, *others = in_vmem(own, names, first2, near, *others)
     before, current, summed, states_v = in_vmem(before, current, summed, states_v)
     second2, second3, drive = pl.pallas_call(
         functools.partial(third_kernel, held),
-        out_shape=(faces_only, faces_only, per_face),
-        in_specs=[VM] * (6 + len(others)),
+        out_shape=(faces_only, pltpu.VMEM((2 * ROWS, width), f32), per_face),
+        in_specs=[VM] * (7 + len(others)),
         out_specs=[VM] * 3,
         name="send_far",
-    )(before, current, summed, names, own, near, *others)
+    )(before, current, summed, names, own, first2, near, *others)
     later_far = lax.ppermute(second2, AXES, crossing)
 
-    far, drive = in_vmem(far, drive)
+    ends = lax.ppermute(second3, AXES, ending)
+
+    far = pl.pallas_call(
+        functools.partial(inside_kernel, slabs, groups),
+        out_shape=faces_only,
+        in_specs=[VM],
+        out_specs=VM,
+        cost_estimate=COVER,
+        name="inside",
+    )(*in_vmem(far))
+    far, ends, drive = in_vmem(far, ends, drive)
     second1 = pl.pallas_call(
         functools.partial(near_kernel, slabs, groups),
-        out_shape=pltpu.VMEM((2 * ROWS, width), f32),
-        in_specs=[VM] * 3,
+        out_shape=faces_only,
+        in_specs=[VM] * 4,
         out_specs=VM,
         name="send_near",
-    )(before, drive, far)
-    second1, second3 = lax.optimization_barrier((second1, second3))
+    )(before, drive, far, ends)
     later_near = within(second1, 1)
-    ends = lax.ppermute(second3, AXES, ending)
-    later_near, later_far, ends = in_vmem(later_near, later_far, ends)
+    later_near, later_far = in_vmem(later_near, later_far)
 
     renewed, total, table = pl.pallas_call(
         functools.partial(poles_kernel, held),
@@ -587,16 +594,16 @@
         ],
         cost_estimate=COVER,
         name="local_second",
-    )(fields_v, before, far, later_near, near, drive, *in_vmem(renewed, total, table))
+    )(fields_v, before, far, ends, near, drive, *in_vmem(renewed, total, table))
 
     advanced = pl.pallas_call(
         functools.partial(fifth_kernel, slabs, groups),
         out_shape=jax.ShapeDtypeStruct(fields.shape, f32),
-        in_specs=[VM] * 5,
+        in_specs=[VM] * 4,
         out_specs=HB,
         scratch_shapes=[pltpu.VMEM((4, 64, width), f32), pltpu.SemaphoreType.DMA((6,))],
         name="finish",
-    )(*in_vmem(almost), later_near, later_far, ends, far)
+    )(*in_vmem(almost), later_near, later_far, ends)
     return advanced, advanced_states
 
 

time: 15.1 us -> 14 us (0.927)
  waiting for transfers between devices: 3.57 us -> 2.11 us
  starting transfers between devices: 5.71 us -> 5.92 us
    ppermute x1, starting transfers between devices: 1.79 us -> 0.01 us  [on_device(): later_far = lax.ppermute(second2, AXES, crossing)]
    ppermute x1, starting transfers between devices: 0.06 us -> 1.79 us  [on_device(): ends = lax.ppermute(second3, AXES, ending)]
    ppermute x3, waiting for transfers between devices: 1.92 us -> 1.04 us  [within(): return lax.ppermute(message, AXES, pairs)]
    ppermute x1, waiting for transfers between devices: 1.64 us -> 1.06 us  [on_device(): ends = lax.ppermute(second3, AXES, ending)]
    ppermute x1, starting transfers between devices: 0.06 us -> 0.34 us  [on_device(): far = lax.ppermute(first2, AXES, crossing)]
  transfers between devices with their start and end apart: 6 -> 6, of which waited for: 4 -> 3; matrix products, arithmetic and copies ran while one was open for 0% -> 0% of each run, Pallas kernels for 17% -> 19%
where the time goes in v6:
time: 14 us; the launch traced here: 13.7 us
  starting transfers between devices  5.92 us (42%)
  Pallas kernels  4.26 us (30%)
  waiting for transfers between devices  2.11 us (15%)
  between operations  1.39 us (10%)
    ppermute x3, starting transfers between devices, within(): return lax.ppermute(message, AXES, pairs)  3.8 us
    ppermute x1, starting transfers between devices, on_device(): ends = lax.ppermute(second3, AXES, ending)  1.79 us
    pallas_call x1, Pallas kernels, on_device(): pl.pallas_call(functools.partial(fourth_kernel, slabs, groups), out_shape...  1.07 us
    ppermute x1, waiting for transfers between devices, on_device(): ends = lax.ppermute(second3, AXES, ending)  1.06 us
    ppermute x3, waiting for transfers between devices, within(): return lax.ppermute(message, AXES, pairs)  1.04 us
    pallas_call x1, Pallas kernels, on_device(): pl.pallas_call(second_kernel, out_shape=(block, per_face, per_face, pltpu...  0.95 us
    pallas_call x1, Pallas kernels, on_device(): pl.pallas_call(first_kernel, out_shape=(faces_only, pltpu.VMEM((8, 128),...  0.91 us
    pallas_call x1, Pallas kernels, on_device(): pl.pallas_call(functools.partial(fifth_kernel, slabs, groups), out_shape=...  0.79 us
  transfers between devices with their start and end apart: 6, of which 3 were waited for; matrix products, arithmetic and copies ran while one was open for 0% of the time, Pallas kernels for 19%

profile of v6, /device:TPU:1, one launch (start us, length us, event | category | flops | bytes accessed | tf_op | source)
XLA Modules:
  0.0 13.7 jit_solution(17607716786864243444)
XLA Ops:
  0.6 0.0 copy-start
  1.3 0.9 %send_first.1 = (f32[32,256]{1,0:T(8,128)S(1)}, f32[8,128]{1,0:T(8,128)S(1)}, f32[40,256]{1,0:T(8,128)S(1)}, s32[1,16]{1,0:T(1,128)S(1)}) custom-call(f32[6,64,256]{2,1,0:T(8,128)} %fields.7, f32[1,12]{1,0:T(1,128)} %decay.1, f32[1,12]{1,0:T(1,128)} %gain.1, f32[1]{0:T(128)S(6)} %copy.8.resist, s32[1,16]{1,0:T(1,128)} %bitcast.1), custom_call_target="tpu_custom_call" | custom-call | tf_op jit(solution)/shard_map/send_first/pallas_call | solution.py:486
  2.3 0.1 collective-permute-start
  2.4 0.0 copy-done
  2.4 1.0 %local_first.1 = (f32[6,64,256]{2,1,0:T(8,128)S(1)}, f32[2,16,128]{2,1,0:T(8,128)S(1)}, f32[2,16,128]{2,1,0:T(8,128)S(1)}, f32[12,2,16,16]{3,2,1,0:T(8,128)S(1)}) custom-call(f32[6,64,256]{2,1,0:T(8,128)S(1)} %copy-done, f32[12,2,16,16]{3,2,1,0:T(8,128)} %states_h.1), custom_call_target="tpu_custom_call" | custom-call | tf_op jit(solution)/shard_map/local_first/pallas_call | solution.py:506
  3.3 0.2 %collective-permute-done.near = f32[40,256]{1,0:T(8,128)S(1)} collective-permute-done((f32[40,256]{1,0:T(8,128)S(1)}, f32[40,256]{1,0:T(8,128)S(1)}, u32[]{:S(2)}, u32[]{:S(2)}) %collective-permute-start) | collective-permute-done | bytes 40992 | tf_op jit(solution)/shard_map/ppermute | solution.py:478
  3.6 2.7 %collective-permute-start.2 = (f32[8,128]{1,0:T(8,128)S(1)}, f32[8,128]{1,0:T(8,128)S(1)}, u32[]{:S(2)}, u32[]{:S(2)}) collective-permute-start(f32[8,128]{1,0:T(8,128)S(1)} %select_maximum_fusion), channel_id=1, source_target_pairs={{0,3},{1,2},{2,1},{3,0},{4,7},{5,6},{6,5},{7,4},{8,11},{9,10},{10,... | collective-permute-start | bytes 12296 | tf_op jit(solution)/shard_map/ppermute | solution.py:478
  6.2 0.1 local_z.1.before
  6.3 0.3 %collective-permute-start.1 = (f32[32,256]{1,0:T(8,128)S(1)}, f32[32,256]{1,0:T(8,128)S(1)}, u32[]{:S(2)}, u32[]{:S(2)}) collective-permute-start(f32[32,256]{1,0:T(8,128)S(1)} %get-tuple-element.26.sent), channel_id=1, source_target_pairs={{3,4},{5,6},{7,8},{9,10},{11,12},{13,14},{15,16},{17,18},{19,20},{... | collective-permute-start | bytes 98312 | tf_op jit(solution)/shard_map/ppermute | solution.py:534
  6.7 0.8 %collective-permute-done.2.refs_0_ = f32[8,128]{1,0:T(8,128)S(1)} collective-permute-done((f32[8,128]{1,0:T(8,128)S(1)}, f32[8,128]{1,0:T(8,128)S(1)}, u32[]{:S(2)}, u32[]{:S(2)}) %collective-permute-start.2) | collective-permute-done | bytes 4128 | tf_op jit(solution)/shard_map/ppermute | solution.py:478
  7.5 0.2 %send_far.1 = (f32[32,256]{1,0:T(8,128)S(1)}, f32[64,256]{1,0:T(8,128)S(1)}, f32[2,16,128]{2,1,0:T(8,128)S(1)}) custom-call(f32[6,64,256]{2,1,0:T(8,128)S(1)} %local_z.1.before, f32[2,16,128]{2,1,0:T(8,128)S(1)} %get-tuple-element.27.current, f32[2,16,128]{2,1,0:T(8,128)S(1)} %get-tuple-element.28.summed, s32[1,16]{1,0:T(1,128)S(1)} %get-tuple-element.29.owner, ...), custom_call_target="tpu_custom_call" | custom-call | tf_op jit(solution)/shard_map/send_far/pallas_call | solution.py:547
  7.7 1.8 %collective-permute-start.3 = (f32[64,256]{1,0:T(8,128)S(1)}, f32[64,256]{1,0:T(8,128)S(1)}, u32[]{:S(2)}, u32[]{:S(2)}) collective-permute-start(f32[64,256]{1,0:T(8,128)S(1)} %get-tuple-element.31), channel_id=1, source_target_pairs={{4,5},{5,4},{6,7},{7,6},{8,9},{9,8},{10,11},{11,10},{12,13},{13,12... | collective-permute-start | bytes 196616 | tf_op jit(solution)/shard_map/ppermute | solution.py:556
  9.5 0.0 collective-permute-start.5
  9.5 0.2 %poles.1 = (f32[12,2,16,16]{3,2,1,0:T(8,128)S(1)}, f32[2,16,128]{2,1,0:T(8,128)S(1)}, f32[32,128]{1,0:T(8,128)S(1)}) custom-call(f32[12,2,16,16]{3,2,1,0:T(8,128)S(1)} %get-tuple-element.33.states, f32[2,16,128]{2,1,0:T(8,128)S(1)} %get-tuple-element.27.current, s32[1,16]{1,0:T(1,128)S(1)} %get-tuple-element.29.owner, f32[8,128]{1,0:T(8,128)S(1)} %get-tuple-element.22.own, ...), custom_call_target="tpu_custom_call" | custom-call | flops 2000000000 | tf_op jit(solution)/shard_map/poles/pallas_call | solution.py:577
  9.7 0.0 collective-permute-done.1.far
  9.7 1.1 %collective-permute-done.3.ends = f32[64,256]{1,0:T(8,128)S(1)} collective-permute-done((f32[64,256]{1,0:T(8,128)S(1)}, f32[64,256]{1,0:T(8,128)S(1)}, u32[]{:S(2)}, u32[]{:S(2)}) %collective-permute-start.3) | collective-permute-done | bytes 65568 | tf_op jit(solution)/shard_map/ppermute | solution.py:556
  10.8 1.0 %collective-permute-start.4 = (f32[32,256]{1,0:T(8,128)S(1)}, f32[32,256]{1,0:T(8,128)S(1)}, u32[]{:S(2)}, u32[]{:S(2)}) collective-permute-start(f32[32,256]{1,0:T(8,128)S(1)} %send_near.1), channel_id=1, source_target_pairs={{0,1},{1,0},{2,3},{3,2},{4,5},{5,4},{6,7},{7,6},{8,9},{9,8},{10,11... | collective-permute-start | bytes 98312 | tf_op jit(solution)/shard_map/ppermute | solution.py:478
  11.8 1.1 %local_second.1 = (f32[6,64,256]{2,1,0:T(8,128)S(1)}, f32[12,2,16,16]{3,2,1,0:T(8,128)}) custom-call(f32[6,64,256]{2,1,0:T(8,128)S(1)} %copy-done, f32[6,64,256]{2,1,0:T(8,128)S(1)} %local_z.1.before, f32[32,256]{1,0:T(8,128)S(1)} %inside.1.far, f32[64,256]{1,0:T(8,128)S(1)} %collective-permute-done.3.ends, f32[40,256]{1,0:T(8,128)S(1)} %collective-permute-done.near, ...), custom_call_target="tpu_custom_call" | custom-call | flops 2000000000 | tf_op jit(solution)/shard_map/local_second/pallas_call | solution.py:585
  12.9 0.0 collective-permute-done.5.far
  12.9 0.0 collective-permute-done.4.near
  12.9 0.8 %finish.1 = f32[6,64,256]{2,1,0:T(8,128)} custom-call(f32[6,64,256]{2,1,0:T(8,128)S(1)} %get-tuple-element.37.before, f32[32,256]{1,0:T(8,128)S(1)} %collective-permute-done.4.near, f32[32,256]{1,0:T(8,128)S(1)} %collective-permute-done.5.far, f32[64,256]{1,0:T(8,128)S(1)} %collective-permute-done.3.ends), custom_call_target="tpu_custom_call" | custom-call | tf_op jit(solution)/shard_map/finish/pallas_call | solution.py:599
  (5 shorter events, 0.1 us)
Async XLA Ops:
  0.6 1.7 %copy-start = (f32[6,64,256]{2,1,0:T(8,128)S(1)}, f32[6,64,256]{2,1,0:T(8,128)}, u32[]{:S(2)}) copy-start(f32[6,64,256]{2,1,0:T(8,128)} %fields.7) | copy-start | bytes 1179652
  2.3 1.3 %collective-permute-start = (f32[40,256]{1,0:T(8,128)S(1)}, f32[40,256]{1,0:T(8,128)S(1)}, u32[]{:S(2)}, u32[]{:S(2)}) collective-permute-start(f32[40,256]{1,0:T(8,128)S(1)} %get-tuple-element.23), channel_id=1, source_target_pairs={{0,1},{1,0},{2,3},{3,2},{4,5},{5,4},{6,7},{7,6},{8,9},{9,8},{10,11... | collective-permute-start | bytes 122888 | tf_op jit(solution)/shard_map/ppermute | solution.py:478
  3.6 4.0 %collective-permute-start.2 = (f32[8,128]{1,0:T(8,128)S(1)}, f32[8,128]{1,0:T(8,128)S(1)}, u32[]{:S(2)}, u32[]{:S(2)}) collective-permute-start(f32[8,128]{1,0:T(8,128)S(1)} %select_maximum_fusion), channel_id=1, source_target_pairs={{0,3},{1,2},{2,1},{3,0},{4,7},{5,6},{6,5},{7,4},{8,11},{9,10},{10,... | collective-permute-start | bytes 12296 | tf_op jit(solution)/shard_map/ppermute | solution.py:478
  6.3 3.4 %collective-permute-start.1 = (f32[32,256]{1,0:T(8,128)S(1)}, f32[32,256]{1,0:T(8,128)S(1)}, u32[]{:S(2)}, u32[]{:S(2)}) collective-permute-start(f32[32,256]{1,0:T(8,128)S(1)} %get-tuple-element.26.sent), channel_id=1, source_target_pairs={{3,4},{5,6},{7,8},{9,10},{11,12},{13,14},{15,16},{17,18},{19,20},{... | collective-permute-start | bytes 98312 | tf_op jit(solution)/shard_map/ppermute | solution.py:534
  7.7 3.1 %collective-permute-start.3 = (f32[64,256]{1,0:T(8,128)S(1)}, f32[64,256]{1,0:T(8,128)S(1)}, u32[]{:S(2)}, u32[]{:S(2)}) collective-permute-start(f32[64,256]{1,0:T(8,128)S(1)} %get-tuple-element.31), channel_id=1, source_target_pairs={{4,5},{5,4},{6,7},{7,6},{8,9},{9,8},{10,11},{11,10},{12,13},{13,12... | collective-permute-start | bytes 196616 | tf_op jit(solution)/shard_map/ppermute | solution.py:556
  9.5 3.4 %collective-permute-start.5 = (f32[32,256]{1,0:T(8,128)S(1)}, f32[32,256]{1,0:T(8,128)S(1)}, u32[]{:S(2)}, u32[]{:S(2)}) collective-permute-start(f32[32,256]{1,0:T(8,128)S(1)} %get-tuple-element.38), channel_id=1, source_target_pairs={{3,4},{5,6},{7,8},{9,10},{11,12},{13,14},{15,16},{17,18},{19,20},{... | collective-permute-start | bytes 98312 | tf_op jit(solution)/shard_map/ppermute | solution.py:554
  10.8 2.1 %collective-permute-start.4 = (f32[32,256]{1,0:T(8,128)S(1)}, f32[32,256]{1,0:T(8,128)S(1)}, u32[]{:S(2)}, u32[]{:S(2)}) collective-permute-start(f32[32,256]{1,0:T(8,128)S(1)} %send_near.1), channel_id=1, source_target_pairs={{0,1},{1,0},{2,3},{3,2},{4,5},{5,4},{6,7},{7,6},{8,9},{9,8},{10,11... | collective-permute-start | bytes 98312 | tf_op jit(solution)/shard_map/ppermute | solution.py:478

commit v7 on v5

--- a/solution.py
+++ b/solution.py
@@ -90,7 +90,7 @@
 
 
 def first_kernel(
-    fields, decay, gain, resist, owner, out2, own, out1, names, faces, decays, gains, resists, sems
+    fields, decay, gain, resist, out2, own, out1, faces, decays, gains, sems
 ):
     copies = [
         pltpu.make_async_copy(fields.at[0:2, 48:64], faces.at[0, 0:2], sems.at[0]),
@@ -99,8 +99,6 @@
         pltpu.make_async_copy(fields.at[3:5, 0:16], faces.at[1, 2:4], sems.at[3]),
         pltpu.make_async_copy(decay, decays, sems.at[4]),
         pltpu.make_async_copy(gain, gains, sems.at[5]),
-        pltpu.make_async_copy(resist, resists, sems.at[6]),
-        pltpu.make_async_copy(owner, names, sems.at[7]),
     ]
     for copy in copies:
         copy.start()
@@ -117,7 +115,7 @@
     own[...] = jnp.zeros_like(own)
     own[0:1, 0:POLES] = decays[...]
     own[1:2, 0:POLES] = gains[...]
-    own[2:3, :] = jnp.full((1, 128), resists[0], jnp.float32)
+    own[2:3, :] = jnp.full((1, 128), resist[0], jnp.float32)
     out1[32:40, 0:128] = own[...]
 
 
@@ -257,13 +255,18 @@
     return found
 
 
-def second_kernel(fields, states_h, out, current, summed, states, sem):
-    copy = pltpu.make_async_copy(states_h, states, sem)
+def second_kernel(fields, states_h, owner_h, out, current, summed, states, owner, sems):
+    copy = pltpu.make_async_copy(states_h, states, sems.at[0])
     copy.start()
-    update(fields, fields, out, None, "xy")
+    names = pltpu.make_async_copy(owner_h, owner, sems.at[1])
+    names.start()
+    update(fields, fields, out, None, "x")
+    for field in (0, 3):
+        out[field] = fields[field]
     for part, value in enumerate(currents(fields)):
         current[part] = value
     copy.wait()
+    names.wait()
     for part in range(2):
         total = states[0, part]
         for pole in range(1, POLES):
@@ -273,9 +276,7 @@
 
 
 def upright_kernel(fields, partial, out):
-    update(fields, partial, out, None, "z")
-    for field in (2, 5):
-        out[field] = partial[field]
+    update(fields, partial, out, None, "yz")
 
 
 def far_exterior(slabs, groups, far_ref, ends_ref, start, missing):
@@ -484,39 +485,38 @@
     block = pltpu.VMEM(fields.shape, f32)
     per_face = pltpu.VMEM((2, 16, 128), f32)
     (fields_v,) = in_vmem(fields)
-    first2, own, first1, names = pl.pallas_call(
+    first2, own, first1 = pl.pallas_call(
         first_kernel,
         out_shape=(
             faces_only,
             pltpu.VMEM((8, 128), f32),
             pltpu.VMEM((MESSAGE, width), f32),
-            pltpu.VMEM(owner.shape, owner.dtype),
         ),
-        in_specs=[HB] * 5,
-        out_specs=[VM] * 4,
+        in_specs=[HB] * 3 + [pl.BlockSpec(memory_space=pltpu.SMEM)],
+        out_specs=[VM] * 3,
         scratch_shapes=[
             pltpu.VMEM((2, 4, 16, width), f32),
             pltpu.VMEM((1, POLES), f32),
             pltpu.VMEM((1, POLES), f32),
-            pltpu.SMEM((1,), f32),
-            pltpu.SemaphoreType.DMA((8,)),
+            pltpu.SemaphoreType.DMA((6,)),
         ],
         name="send_first",
-    )(fields, pole_decay, pole_gain, surface_resistance, owner)
+    )(fields, pole_decay, pole_gain, surface_resistance)
     near = within(first1, 1)
-    partial, current, summed, states_v = pl.pallas_call(
+    partial, current, summed, states_v, names = pl.pallas_call(
             second_kernel,
             out_shape=(
                 block,
                 per_face,
                 per_face,
                 pltpu.VMEM(pole_state.shape, f32),
+                pltpu.VMEM(owner.shape, owner.dtype),
             ),
-            in_specs=[VM, HB],
-            out_specs=[VM] * 4,
-            scratch_shapes=[pltpu.SemaphoreType.DMA],
+            in_specs=[VM, HB, HB],
+            out_specs=[VM] * 5,
+            scratch_shapes=[pltpu.SemaphoreType.DMA((2,))],
             name="local_first",
-        )(fields_v, pole_state)
+        )(fields_v, pole_state, owner)
 
     known, held, others = [own[0:3]], [(0, 0, 0)], []
     for r in range(1, groups.bit_length()):

time: 13.9 us -> 13.9 us (level)
  transfers between devices with their start and end apart: 6 -> 6, of which waited for: 2 -> 2; matrix products, arithmetic and copies ran while one was open for 0% -> 0% of each run, Pallas kernels for 19% -> 20%
where the time goes in v7:
time: 13.9 us; the launch traced here: 13.7 us
  starting transfers between devices  6.16 us (44%)
  Pallas kernels  4.37 us (31%)
  waiting for transfers between devices  1.72 us (12%)
  between operations  1.4 us (10%)
    ppermute x3, starting transfers between devices, within(): return lax.ppermute(message, AXES, pairs)  3.74 us
    ppermute x1, starting transfers between devices, on_device(): later_far = lax.ppermute(second2, AXES, crossing_back)  1.72 us
    ppermute x3, waiting for transfers between devices, within(): return lax.ppermute(message, AXES, pairs)  1.71 us
    pallas_call x1, Pallas kernels, on_device(): pl.pallas_call(functools.partial(fourth_kernel, slabs, groups), out_shape...  1.07 us
    pallas_call x1, Pallas kernels, on_device(): pl.pallas_call(second_kernel, out_shape=(block, per_face, per_face, pltpu...  0.96 us
    pallas_call x1, Pallas kernels, on_device(): pl.pallas_call(first_kernel, out_shape=(faces_only, pltpu.VMEM((8, 128),...  0.88 us
    pallas_call x1, Pallas kernels, on_device(): pl.pallas_call(functools.partial(fifth_kernel, slabs, groups), out_shape=...  0.79 us
    ppermute x1, starting transfers between devices, on_device(): far = lax.ppermute(first2, AXES, crossing)  0.43 us
  transfers between devices with their start and end apart: 6, of which 2 were waited for; matrix products, arithmetic and copies ran while one was open for 0% of the time, Pallas kernels for 20%

profile of v7, /device:TPU:9, one launch (start us, length us, event | category | flops | bytes accessed | tf_op | source)
XLA Modules:
  0.0 13.7 jit_solution(17431043123822778534)
XLA Ops:
  0.6 0.0 copy-start
  1.3 0.9 %send_first.1 = (f32[32,256]{1,0:T(8,128)S(1)}, f32[8,128]{1,0:T(8,128)S(1)}, f32[40,256]{1,0:T(8,128)S(1)}) custom-call(f32[6,64,256]{2,1,0:T(8,128)} %fields.7, f32[1,12]{1,0:T(1,128)} %decay.1, f32[1,12]{1,0:T(1,128)} %gain.1, f32[1]{0:T(128)S(6)} %copy.8.resist), custom_call_target="tpu_custom_call" | custom-call | tf_op jit(solution)/shard_map/send_first/pallas_call | solution.py:488
  2.2 0.7 %collective-permute-start = (f32[40,256]{1,0:T(8,128)S(1)}, f32[40,256]{1,0:T(8,128)S(1)}, u32[]{:S(2)}, u32[]{:S(2)}) collective-permute-start(f32[40,256]{1,0:T(8,128)S(1)} %get-tuple-element.23), channel_id=1, source_target_pairs={{0,1},{1,0},{2,3},{3,2},{4,5},{5,4},{6,7},{7,6},{8,9},{9,8},{10,11... | collective-permute-start | bytes 122888 | tf_op jit(solution)/shard_map/ppermute | solution.py:480
  3.0 0.0 copy-done
  3.0 1.0 %local_first.1 = (f32[6,64,256]{2,1,0:T(8,128)S(1)}, f32[2,16,128]{2,1,0:T(8,128)S(1)}, f32[2,16,128]{2,1,0:T(8,128)S(1)}, f32[12,2,16,16]{3,2,1,0:T(8,128)S(1)}, s32[1,16]{1,0:T(1,128)S(1)}) custom-call(f32[6,64,256]{2,1,0:T(8,128)S(1)} %copy-done, f32[12,2,16,16]{3,2,1,0:T(8,128)} %states_h.1, s32[1,16]{1,0:T(1,128)} %bitcast.1), custom_call_target="tpu_custom_call" | custom-call | tf_op jit(solution)/shard_map/local_first/pallas_call | solution.py:506
  3.9 0.0 collective-permute-done.near
  4.0 1.4 %collective-permute-start.2 = (f32[8,128]{1,0:T(8,128)S(1)}, f32[8,128]{1,0:T(8,128)S(1)}, u32[]{:S(2)}, u32[]{:S(2)}) collective-permute-start(f32[8,128]{1,0:T(8,128)S(1)} %select_maximum_fusion), channel_id=1, source_target_pairs={{0,3},{1,2},{2,1},{3,0},{4,7},{5,6},{6,5},{7,4},{8,11},{9,10},{10,... | collective-permute-start | bytes 12296 | tf_op jit(solution)/shard_map/ppermute | solution.py:480
  5.4 0.4 %collective-permute-start.1 = (f32[32,256]{1,0:T(8,128)S(1)}, f32[32,256]{1,0:T(8,128)S(1)}, u32[]{:S(2)}, u32[]{:S(2)}) collective-permute-start(f32[32,256]{1,0:T(8,128)S(1)} %get-tuple-element.26), channel_id=1, source_target_pairs={{3,4},{5,6},{7,8},{9,10},{11,12},{13,14},{15,16},{17,18},{19,20},{... | collective-permute-start | bytes 98312 | tf_op jit(solution)/shard_map/ppermute | solution.py:535
  5.8 0.2 %local_z.1.before = f32[6,64,256]{2,1,0:T(8,128)S(1)} custom-call(f32[6,64,256]{2,1,0:T(8,128)S(1)} %copy-done, f32[6,64,256]{2,1,0:T(8,128)S(1)} %get-tuple-element.21.partial), custom_call_target="tpu_custom_call" | custom-call | flops 2000000000 | tf_op jit(solution)/shard_map/local_z/pallas_call | solution.py:538
  6.0 1.0 %collective-permute-done.2.refs_0_ = f32[8,128]{1,0:T(8,128)S(1)} collective-permute-done((f32[8,128]{1,0:T(8,128)S(1)}, f32[8,128]{1,0:T(8,128)S(1)}, u32[]{:S(2)}, u32[]{:S(2)}) %collective-permute-start.2) | collective-permute-done | bytes 4128 | tf_op jit(solution)/shard_map/ppermute | solution.py:480
  7.1 0.2 %send_far.1 = (f32[32,256]{1,0:T(8,128)S(1)}, f32[32,256]{1,0:T(8,128)S(1)}, f32[2,16,128]{2,1,0:T(8,128)S(1)}) custom-call(f32[6,64,256]{2,1,0:T(8,128)S(1)} %local_z.1.before, f32[2,16,128]{2,1,0:T(8,128)S(1)} %get-tuple-element.27.current, f32[2,16,128]{2,1,0:T(8,128)S(1)} %get-tuple-element.28.summed, s32[1,16]{1,0:T(1,128)S(1)} %get-tuple-element.29.owner, ...), custom_call_target="tpu_custom_call" | custom-call | tf_op jit(solution)/shard_map/send_far/pallas_call | solution.py:548
  7.2 0.3 %collective-permute-start.4 = (f32[32,256]{1,0:T(8,128)S(1)}, f32[32,256]{1,0:T(8,128)S(1)}, u32[]{:S(2)}, u32[]{:S(2)}) collective-permute-start(f32[32,256]{1,0:T(8,128)S(1)} %get-tuple-element.37), channel_id=1, source_target_pairs={{4,5},{5,4},{6,7},{7,6},{8,9},{9,8},{10,11},{11,10},{12,13},{13,12... | collective-permute-start | bytes 98312 | tf_op jit(solution)/shard_map/ppermute | solution.py:566
  7.5 1.7 %collective-permute-start.5 = (f32[32,256]{1,0:T(8,128)S(1)}, f32[32,256]{1,0:T(8,128)S(1)}, u32[]{:S(2)}, u32[]{:S(2)}) collective-permute-start(f32[32,256]{1,0:T(8,128)S(1)} %get-tuple-element.38), channel_id=1, source_target_pairs={{3,4},{5,6},{7,8},{9,10},{11,12},{13,14},{15,16},{17,18},{19,20},{... | collective-permute-start | bytes 98312 | tf_op jit(solution)/shard_map/ppermute | solution.py:555
  9.2 0.0 collective-permute-done.1.far.first_far
  9.3 1.6 %collective-permute-start.3 = (f32[64,256]{1,0:T(8,128)S(1)}, f32[64,256]{1,0:T(8,128)S(1)}, u32[]{:S(2)}, u32[]{:S(2)}) collective-permute-start(f32[64,256]{1,0:T(8,128)S(1)} %send_near.1), channel_id=1, source_target_pairs={{0,1},{1,0},{2,3},{3,2},{4,5},{5,4},{6,7},{7,6},{8,9},{9,8},{10,11... | collective-permute-start | bytes 196616 | tf_op jit(solution)/shard_map/ppermute | solution.py:480
  10.9 0.2 %poles.1 = (f32[12,2,16,16]{3,2,1,0:T(8,128)S(1)}, f32[2,16,128]{2,1,0:T(8,128)S(1)}, f32[32,128]{1,0:T(8,128)S(1)}) custom-call(f32[12,2,16,16]{3,2,1,0:T(8,128)S(1)} %get-tuple-element.32.states, f32[2,16,128]{2,1,0:T(8,128)S(1)} %get-tuple-element.27.current, s32[1,16]{1,0:T(1,128)S(1)} %get-tuple-element.29.owner, f32[8,128]{1,0:T(8,128)S(1)} %get-tuple-element.22.own, ...), custom_call_target="tpu_custom_call" | custom-call | flops 2000000000 | tf_op jit(solution)/shard_map/poles/pallas_call | solution.py:569
  11.1 0.7 %collective-permute-done.3.passed.near = f32[64,256]{1,0:T(8,128)S(1)} collective-permute-done((f32[64,256]{1,0:T(8,128)S(1)}, f32[64,256]{1,0:T(8,128)S(1)}, u32[]{:S(2)}, u32[]{:S(2)}) %collective-permute-start.3) | collective-permute-done | bytes 65568 | tf_op jit(solution)/shard_map/ppermute | solution.py:480
  11.8 1.1 %local_second.1 = (f32[6,64,256]{2,1,0:T(8,128)S(1)}, f32[12,2,16,16]{3,2,1,0:T(8,128)}) custom-call(f32[6,64,256]{2,1,0:T(8,128)S(1)} %copy-done, f32[6,64,256]{2,1,0:T(8,128)S(1)} %local_z.1.before, f32[32,256]{1,0:T(8,128)S(1)} %collective-permute-done.1.far.first_far, f32[64,256]{1,0:T(8,128)S(1)} %collective-permute-done.3.passed.near, ...), custom_call_target="tpu_custom_call" | custom-call | flops 2000000000 | tf_op jit(solution)/shard_map/local_second/pallas_call | solution.py:577
  12.9 0.0 collective-permute-done.4.ends
  12.9 0.0 collective-permute-done.5.far
  12.9 0.8 %finish.1 = f32[6,64,256]{2,1,0:T(8,128)} custom-call(f32[6,64,256]{2,1,0:T(8,128)S(1)} %get-tuple-element.36.before, f32[64,256]{1,0:T(8,128)S(1)} %collective-permute-done.3.passed.near, f32[32,256]{1,0:T(8,128)S(1)} %collective-permute-done.4.ends, f32[32,256]{1,0:T(8,128)S(1)} %collective-permute-done.5.far, ...), custom_call_target="tpu_custom_call" | custom-call | tf_op jit(solution)/shard_map/finish/pallas_call | solution.py:591
  (4 shorter events, 0.0 us)
Async XLA Ops:
  0.6 2.3 %copy-start = (f32[6,64,256]{2,1,0:T(8,128)S(1)}, f32[6,64,256]{2,1,0:T(8,128)}, u32[]{:S(2)}) copy-start(f32[6,64,256]{2,1,0:T(8,128)} %fields.7) | copy-start | bytes 1179652
  2.2 1.7 %collective-permute-start = (f32[40,256]{1,0:T(8,128)S(1)}, f32[40,256]{1,0:T(8,128)S(1)}, u32[]{:S(2)}, u32[]{:S(2)}) collective-permute-start(f32[40,256]{1,0:T(8,128)S(1)} %get-tuple-element.23), channel_id=1, source_target_pairs={{0,1},{1,0},{2,3},{3,2},{4,5},{5,4},{6,7},{7,6},{8,9},{9,8},{10,11... | collective-permute-start | bytes 122888 | tf_op jit(solution)/shard_map/ppermute | solution.py:480
  4.0 3.1 %collective-permute-start.2 = (f32[8,128]{1,0:T(8,128)S(1)}, f32[8,128]{1,0:T(8,128)S(1)}, u32[]{:S(2)}, u32[]{:S(2)}) collective-permute-start(f32[8,128]{1,0:T(8,128)S(1)} %select_maximum_fusion), channel_id=1, source_target_pairs={{0,3},{1,2},{2,1},{3,0},{4,7},{5,6},{6,5},{7,4},{8,11},{9,10},{10,... | collective-permute-start | bytes 12296 | tf_op jit(solution)/shard_map/ppermute | solution.py:480
  5.4 3.9 %collective-permute-start.1 = (f32[32,256]{1,0:T(8,128)S(1)}, f32[32,256]{1,0:T(8,128)S(1)}, u32[]{:S(2)}, u32[]{:S(2)}) collective-permute-start(f32[32,256]{1,0:T(8,128)S(1)} %get-tuple-element.26), channel_id=1, source_target_pairs={{3,4},{5,6},{7,8},{9,10},{11,12},{13,14},{15,16},{17,18},{19,20},{... | collective-permute-start | bytes 98312 | tf_op jit(solution)/shard_map/ppermute | solution.py:535
  7.2 5.6 %collective-permute-start.4 = (f32[32,256]{1,0:T(8,128)S(1)}, f32[32,256]{1,0:T(8,128)S(1)}, u32[]{:S(2)}, u32[]{:S(2)}) collective-permute-start(f32[32,256]{1,0:T(8,128)S(1)} %get-tuple-element.37), channel_id=1, source_target_pairs={{4,5},{5,4},{6,7},{7,6},{8,9},{9,8},{10,11},{11,10},{12,13},{13,12... | collective-permute-start | bytes 98312 | tf_op jit(solution)/shard_map/ppermute | solution.py:566
  7.5 5.4 %collective-permute-start.5 = (f32[32,256]{1,0:T(8,128)S(1)}, f32[32,256]{1,0:T(8,128)S(1)}, u32[]{:S(2)}, u32[]{:S(2)}) collective-permute-start(f32[32,256]{1,0:T(8,128)S(1)} %get-tuple-element.38), channel_id=1, source_target_pairs={{3,4},{5,6},{7,8},{9,10},{11,12},{13,14},{15,16},{17,18},{19,20},{... | collective-permute-start | bytes 98312 | tf_op jit(solution)/shard_map/ppermute | solution.py:555
  9.3 2.5 %collective-permute-start.3 = (f32[64,256]{1,0:T(8,128)S(1)}, f32[64,256]{1,0:T(8,128)S(1)}, u32[]{:S(2)}, u32[]{:S(2)}) collective-permute-start(f32[64,256]{1,0:T(8,128)S(1)} %send_near.1), channel_id=1, source_target_pairs={{0,1},{1,0},{2,3},{3,2},{4,5},{5,4},{6,7},{7,6},{8,9},{9,8},{10,11... | collective-permute-start | bytes 196616 | tf_op jit(solution)/shard_map/ppermute | solution.py:480
